TPU v7x, 32 devices: a whole 2x2x4 slice. The times are simulated.
32 devices in a mesh: dp: 8 (over y, x, core), tensor: 4 (over z).
Axes of the slice: x: 2, y: 2, z: 4, core: 2. Of those that a mesh axis runs over, the one named last changes fastest.
Arguments:
- inputs: bfloat16 [4096, 1024], P(('dp', 'tensor')), may hold values from -6 to 6
- cotangent: bfloat16 [4096, 1024], P(('dp', 'tensor')), may hold values from -6 to 6
- norm_attend: bfloat16 [1024], replicated, may hold values from 0.5 to 1.5
- norm_memory: bfloat16 [1024], replicated, may hold values from 0.5 to 1.5
- project_in: bfloat16 [1024, 3, 1024], P('dp', None, 'tensor'), may hold values from -0.1875 to 0.1875
- project_out: bfloat16 [1024, 1024], P('tensor', 'dp'), may hold values from -2 to 2
- query_weight: bfloat16 [1024, 2048], P('dp', 'tensor'), may hold values from -0.1875 to 0.1875
- gate_weight: bfloat16 [1024, 1024], P('dp', 'tensor'), may hold values from -0.1875 to 0.1875
- memory_out: bfloat16 [1024, 1024], P('tensor', 'dp'), may hold values from -0.5 to 0.5
- half_keys: bfloat16 [4, 2, 256, 256], P('tensor'), may hold values from -6 to 6
- value_table: bfloat16 [65536, 1024], P('dp', 'tensor'), may hold values from -6 to 6
- key_picks: int32 [4, 2, 32, 4096], P(None, None, None, 'dp'), may hold values from 0 to 255
- segment_ids: int32 [4096], P('dp'), may hold values from 0 to 2, as said below
- adapter_ids: int32 [8, 3], P('dp'), may hold values from 0 to 7
- down_input: bfloat16 [1024, 384], P('dp'), may hold values from -0.1875 to 0.1875
- up_input: bfloat16 [128, 3, 1024], P('dp', None, 'tensor'), may hold values from -1.5 to 1.5
- down_attend: bfloat16 [1024, 128], P('tensor', 'dp'), may hold values from -2 to 2
- up_attend: bfloat16 [128, 1024], P('dp'), may hold values from -1.5 to 1.5
- down_memory: bfloat16 [1024, 256], P('dp'), may hold values from -0.1875 to 0.1875
- up_query: bfloat16 [128, 2048], P('dp', 'tensor'), may hold values from -1.5 to 1.5
- up_gate: bfloat16 [128, 1024], P('dp', 'tensor'), may hold values from -1.5 to 1.5
- down_mixed: bfloat16 [1024, 128], P('tensor', 'dp'), may hold values from -0.5 to 0.5
- up_mixed: bfloat16 [128, 1024], P('dp'), may hold values from -1.5 to 1.5
Outputs:
- outputs: bfloat16 [4096, 1024], P(('dp', 'tensor'))
- input_grad: float32 [4096, 1024], P(('dp', 'tensor'))
- grad_down_input: float32 [1024, 384], P('dp', 'tensor')
- grad_up_input: float32 [128, 3, 1024], P('dp', None, 'tensor')
- grad_down_attend: float32 [1024, 128], P('tensor', 'dp')
- grad_up_attend: float32 [128, 1024], P('dp', 'tensor')
- grad_down_memory: float32 [1024, 256], P('dp', 'tensor')
- grad_up_query: float32 [128, 2048], P('dp', 'tensor')
- grad_up_gate: float32 [128, 1024], P('dp', 'tensor')
- grad_down_mixed: float32 [1024, 128], P('tensor', 'dp')
- grad_up_mixed: float32 [128, 1024], P('dp', 'tensor')
Inputs may be any that keep to these rules, and one draw needn't show every extreme that they name: `segment_ids`: in each group the prompt (0) comes first with 256 to 384 tokens, then continuation 1, then continuation 2, each continuation holding a quarter or more of the rest.
All inputs are finite; a program needn't handle non-finite values.
Results may differ from a plain program's by a relative error of at most 0.03.
Values may be sent and summed in bfloat16 or wider, within the bound.
A program may use at most 192 MiB of HBM per device.

v0:
```python
import functools

import jax
import jax.numpy as jnp
from jax import lax
from jax.experimental import pallas as pl
from jax.experimental.pallas import tpu as pltpu
from jax.sharding import PartitionSpec as P

DP, TP = "dp", "tensor"
HD = 64
NKEYS = 256
RANK = 16
NAD = 8
EPS = 1e-06
NEGATIVE = -1e30
F32, BF16, I32 = jnp.float32, jnp.bfloat16, jnp.int32
MESH = pl.DeviceIdType.MESH
ANY = pl.BlockSpec(memory_space=pl.ANY)


def mm(a, b):
    return lax.dot_general(a, b, (((1,), (0,)), ((), ())), preferred_element_type=F32)


def mt(a, b):
    return lax.dot_general(a, b, (((1,), (1,)), ((), ())), preferred_element_type=F32)


def tm(a, b):
    return lax.dot_general(a, b, (((0,), (0,)), ((), ())), preferred_element_type=F32)


def two_parts(x):
    top = x.astype(BF16)
    return top, (x - top.astype(F32)).astype(BF16)


SHARE, PIECE, TREE = 0, 1, 2


def exchange(items, cid):
    arrays = [item[0] for item in items]
    kinds = [item[1] for item in items]
    axes = [item[2] for item in items]
    n = len(items)
    used = [axis for axis in (DP, TP) if axis in axes]
    sizes = {axis: lax.axis_size(axis) for axis in used}
    most = max(sizes.values())
    trees = [a for a in range(n) if kinds[a] == TREE]

    def body(*refs):
        ins, outs = refs[:n], refs[n : 2 * n]
        send, recv, pass_send, pass_recv, local = refs[2 * n :]
        me = {axis: lax.axis_index(axis) for axis in used}
        barrier = pltpu.get_barrier_semaphore()
        for axis in used:

            @pl.loop(1, sizes[axis])
            def _(d):
                pl.semaphore_signal(
                    barrier,
                    inc=1,
                    device_id={axis: lax.rem(me[axis] + d, sizes[axis])},
                    device_id_type=MESH,
                )

        def source(a, p):
            return ins[a].at[p] if kinds[a] == PIECE else ins[a]

        own = [
            pltpu.make_async_copy(source(a, me[axes[a]]), outs[a].at[me[axes[a]]], local.at[a])
            for a in range(n)
        ]
        for c in own:
            c.start()
        pl.semaphore_wait(barrier, sum(sizes.values()) - len(used))

        def copy(a, d):
            axis = axes[a]
            peer = lax.rem(me[axis] + d, sizes[axis])
            return pltpu.make_async_remote_copy(
                src_ref=source(a, peer),
                dst_ref=outs[a].at[me[axis]],
                send_sem=send.at[a, d],
                recv_sem=recv.at[a, d],
                device_id={axis: peer},
                device_id_type=MESH,
            )

        def tree_copy(a, d):
            peer = lax.rem(me[DP] + 2 * d, sizes[DP])
            return pltpu.make_async_remote_copy(
                src_ref=ins[a],
                dst_ref=outs[a].at[me[DP]],
                send_sem=send.at[a, d],
                recv_sem=recv.at[a, d],
                device_id={DP: peer},
                device_id_type=MESH,
            )

        def pass_on(a, d):
            holder = lax.rem(me[DP] - 2 * d + sizes[DP], sizes[DP])
            sibling = me[DP] + 1 - 2 * lax.rem(me[DP], 2)
            return pltpu.make_async_remote_copy(
                src_ref=ins[a] if isinstance(d, int) else outs[a].at[holder],
                dst_ref=outs[a].at[holder],
                send_sem=pass_send.at[a, d],
                recv_sem=pass_recv.at[a, d],
                device_id={DP: sibling},
                device_id_type=MESH,
            )

        if trees:

            @pl.loop(1, sizes[DP] // 2)
            def _(d):
                for a in trees:
                    tree_copy(a, d).start()

            for a in trees:
                pass_on(a, 0).start()
        for axis in used:
            mine = [a for a in range(n) if axes[a] == axis and kinds[a] != TREE]
            if mine:

                @pl.loop(1, sizes[axis])
                def _(d):
                    for a in mine:
                        copy(a, d).start()

        if trees:

            @pl.loop(1, sizes[DP] // 2)
            def _(d):
                for a in trees:
                    tree_copy(a, d).wait_recv()
                    pass_on(a, d).start()

            @pl.loop(1, sizes[DP] // 2)
            def _(d):
                for a in trees:
                    tree_copy(a, d).wait_send()
                    pass_on(a, d).wait()

            for a in trees:
                pass_on(a, 0).wait()
        for axis in used:
            mine = [a for a in range(n) if axes[a] == axis and kinds[a] != TREE]
            if mine:

                @pl.loop(1, sizes[axis])
                def _(d):
                    for a in mine:
                        copy(a, d).wait()

        for c in own:
            c.wait()

    shapes = [
        jax.ShapeDtypeStruct(
            (sizes[axes[a]],) + (x.shape[1:] if kinds[a] == PIECE else x.shape), x.dtype
        )
        for a, x in enumerate(arrays)
    ]
    sems = pltpu.SemaphoreType.DMA((n, most))
    return pl.pallas_call(
        body,
        out_shape=shapes,
        in_specs=[ANY] * n,
        out_specs=[ANY] * n,
        scratch_shapes=[sems, sems, sems, sems, pltpu.SemaphoreType.DMA((n,))],
        compiler_params=pltpu.CompilerParams(collective_id=cid, has_side_effects=True),
    )(*arrays)


def rms_forward(values, gain):
    factor = lax.rsqrt(jnp.mean(values * values, axis=-1, keepdims=True) + EPS)
    return values * factor * gain


def rms_backward(values, gain, upstream):
    factor = lax.rsqrt(jnp.mean(values * values, axis=-1, keepdims=True) + EPS)
    scaled = upstream * gain
    return factor * scaled - values * (factor * factor * factor) * jnp.mean(
        values * scaled, axis=-1, keepdims=True
    )


def block_probs(projected, key_segments, query_segments, h, r, block, width, scale):
    top = (r + 1) * block
    at = slice(r * block, top)
    lanes = slice(h * HD, (h + 1) * HD)
    queries = projected[at, lanes]
    keys = projected[:top, width + h * HD : width + (h + 1) * HD]
    values = projected[:top, 2 * width + h * HD : 2 * width + (h + 1) * HD]
    scores = mt(queries, keys) * scale
    place = lax.broadcasted_iota(I32, (block, top), 0) + r * block
    other = lax.broadcasted_iota(I32, (block, top), 1)
    ahead = key_segments[:, :top]
    seen = (other <= place) & ((ahead == 0) | (ahead == query_segments[at, :]))
    scores = jnp.where(seen, scores, NEGATIVE)
    raised = jnp.exp(scores - jnp.max(scores, axis=-1, keepdims=True))
    probs = raised / jnp.sum(raised, axis=-1, keepdims=True)
    return queries, keys, values, probs


def attention_forward(projected, segments, width, block=128):
    count = projected.shape[0]

    def body(projected_ref, across_ref, down_ref, out_ref):
        for h in range(width // HD):
            for r in range(count // block):
                _, _, values, probs = block_probs(
                    projected_ref, across_ref, down_ref, h, r, block, width, HD**-0.5
                )
                out_ref[r * block : (r + 1) * block, h * HD : (h + 1) * HD] = mm(
                    probs.astype(BF16), values
                ).astype(BF16)

    return pl.pallas_call(
        body,
        out_shape=jax.ShapeDtypeStruct((count, width), BF16),
        compiler_params=pltpu.CompilerParams(vmem_limit_bytes=32 << 20),
    )(projected, segments[None, :], segments[:, None])


def attention_backward(projected, segments, upstream, width, block=128):
    count = projected.shape[0]
    scale = HD**-0.5

    def body(projected_ref, across_ref, down_ref, upstream_ref, out_ref, key_sum, value_sum):
        for h in range(width // HD):
            key_sum[...] = jnp.zeros_like(key_sum)
            value_sum[...] = jnp.zeros_like(value_sum)
            lanes = slice(h * HD, (h + 1) * HD)
            for r in range(count // block):
                at, top = slice(r * block, (r + 1) * block), (r + 1) * block
                queries, keys, values, probs = block_probs(
                    projected_ref, across_ref, down_ref, h, r, block, width, scale
                )
                above = upstream_ref[at, lanes]
                grad_probs = mt(above, values)
                inner = jnp.sum(probs * grad_probs, axis=-1, keepdims=True)
                grad_scores = (probs * (grad_probs - inner)).astype(BF16)
                out_ref[at, lanes] = (mm(grad_scores, keys) * scale).astype(BF16)
                key_sum[:top, :] += tm(grad_scores, queries)
                value_sum[:top, :] += tm(probs.astype(BF16), above)
            out_ref[:, width + h * HD : width + (h + 1) * HD] = (key_sum[...] * scale).astype(BF16)
            out_ref[:, 2 * width + h * HD : 2 * width + (h + 1) * HD] = value_sum[...].astype(BF16)

    return pl.pallas_call(
        body,
        out_shape=jax.ShapeDtypeStruct((count, 3 * width), BF16),
        scratch_shapes=[pltpu.VMEM((count, HD), F32), pltpu.VMEM((count, HD), F32)],
        compiler_params=pltpu.CompilerParams(vmem_limit_bytes=32 << 20),
    )(projected, segments[None, :], segments[:, None], upstream)


def pick_weights(query, keys, picks):
    count, half = query.shape[0], keys.shape[2]
    number = picks.shape[1]
    chunk = 128
    scale = (2 * half) ** -0.5

    def body(query_ref, keys_ref, picks_ref, out_ref, every):
        for part in range(2):
            top, rest = two_parts(query_ref[:, part * half : (part + 1) * half])
            every[...] = mt(keys_ref[part], top) + mt(keys_ref[part], rest)
            slot = lax.broadcasted_iota(I32, (NKEYS, chunk), 0)
            for c in range(count // chunk):
                lanes = slice(c * chunk, (c + 1) * chunk)
                scores = every[:, lanes]
                rows = []
                for k in range(number):
                    hit = slot == picks_ref[part, k : k + 1, lanes]
                    rows.append(jnp.sum(jnp.where(hit, scores, 0.0), axis=0, keepdims=True))
                found = jnp.concatenate(rows, axis=0)
                if part == 0:
                    out_ref[:, lanes] = found
                else:
                    total = (out_ref[:, lanes] + found) * scale
                    raised = jnp.exp(total - jnp.max(total, axis=0, keepdims=True))
                    out_ref[:, lanes] = raised / jnp.sum(raised, axis=0, keepdims=True)

    return pl.pallas_call(
        body,
        out_shape=jax.ShapeDtypeStruct((number, count), F32),
        scratch_shapes=[pltpu.VMEM((NKEYS, count), F32)],
        compiler_params=pltpu.CompilerParams(vmem_limit_bytes=32 << 20),
    )(query, keys, picks)


def query_grads(weights, pieces, keys, picks):
    number, count = weights.shape
    half = keys.shape[2]
    chunk = 128
    scale = (2 * half) ** -0.5

    def body(weights_ref, pieces_ref, keys_ref, picks_ref, out_ref, dense):
        slot = lax.broadcasted_iota(I32, (NKEYS, chunk), 0)
        for part in range(2):
            for c in range(count // chunk):
                lanes = slice(c * chunk, (c + 1) * chunk)
                weight = weights_ref[:, lanes]
                grad = sum(pieces_ref[p, :, lanes].astype(F32) for p in range(pieces.shape[0]))
                grad = weight * (grad - jnp.sum(grad * weight, axis=0, keepdims=True)) * scale
                total = jnp.zeros((NKEYS, chunk), F32)
                for k in range(number):
                    hit = slot == picks_ref[part, k : k + 1, lanes]
                    total += jnp.where(hit, grad[k : k + 1, :], 0.0)
                dense[:, lanes] = total
            top, rest = two_parts(dense[...])
            out_ref[:, part * half : (part + 1) * half] = (
                tm(top, keys_ref[part]) + tm(rest, keys_ref[part])
            ).astype(BF16)

    return pl.pallas_call(
        body,
        out_shape=jax.ShapeDtypeStruct((count, 2 * half), BF16),
        scratch_shapes=[pltpu.VMEM((NKEYS, count), F32)],
        compiler_params=pltpu.CompilerParams(vmem_limit_bytes=32 << 20),
    )(weights, pieces, keys, picks)


def spread_picks(first, second, weights, sub=32, conv=32):
    tokens, picks = first.shape
    stride = sub + 1

    def body(first_ref, second_ref, weights_ref, out_ref, low, high):
        slot = lax.broadcasted_iota(I32, (NKEYS, picks), 0)
        for n in range(sub):
            b = jnp.where(slot == second_ref[n : n + 1, :], 1.0, 0.0).astype(BF16)
            a = jnp.where(slot == first_ref[n : n + 1, :], weights_ref[n : n + 1, :], 0.0)
            both = mt(a.astype(BF16), b)
            low[pl.ds(n, NKEYS, stride=stride), :] = both[:, :128]
            high[pl.ds(n, NKEYS, stride=stride), :] = both[:, 128:]

        @pl.loop(0, NKEYS // conv)
        def _(c):
            for q in range(conv):
                i = c * conv + q
                at = pl.multiple_of(i * NKEYS, NKEYS)
                rows = pl.ds(i * stride, sub)
                out_ref[:, pl.ds(at, 128)] = low[rows, :].astype(BF16)
                out_ref[:, pl.ds(at + 128, 128)] = high[rows, :].astype(BF16)

    line = pl.BlockSpec((sub, picks), lambda t: (t, 0))
    rows = NKEYS * NKEYS
    return pl.pallas_call(
        body,
        grid=(tokens // sub,),
        out_shape=jax.ShapeDtypeStruct((tokens, rows), BF16),
        in_specs=[line] * 3,
        out_specs=pl.BlockSpec((sub, rows), lambda t: (t, 0)),
        scratch_shapes=[pltpu.VMEM((NKEYS * stride, 128), F32)] * 2,
        compiler_params=pltpu.CompilerParams(vmem_limit_bytes=40 << 20),
    )(first, second, weights)


def recall(dense, table, block=4096):
    tokens, rows = dense.shape
    width = table.shape[1]

    def body(dense_ref, table_ref, out_ref):
        @pl.when(pl.program_id(0) == 0)
        def _():
            out_ref[...] = jnp.zeros_like(out_ref)

        out_ref[...] += mm(dense_ref[...], table_ref[...])

    return pl.pallas_call(
        body,
        grid=(rows // block,),
        out_shape=jax.ShapeDtypeStruct((tokens, width), F32),
        in_specs=[
            pl.BlockSpec((tokens, block), lambda s: (0, s)),
            pl.BlockSpec((block, width), lambda s: (s, 0)),
        ],
        out_specs=pl.BlockSpec((tokens, width), lambda s: (0, 0)),
        compiler_params=pltpu.CompilerParams(vmem_limit_bytes=40 << 20),
    )(dense, table)


def pick_grads(first, second, grads, scale, table, per_block=16):
    tokens, picks = first.shape
    width = grads.shape[1]
    rows = per_block * NKEYS
    blocks = table.shape[0] // rows

    def body(first_ref, second_ref, grads_ref, scale_ref, table_ref, out_ref, kept):
        step = pl.program_id(0)

        @pl.when(step == 0)
        def _():
            kept[...] = jnp.zeros_like(kept)

        own = first_ref[...]
        low = second_ref[...] & 127
        factor = jnp.broadcast_to(scale_ref[...], (tokens, 128))
        total = kept[...]
        for b in range(per_block):
            every = mt(grads_ref[...], table_ref[b * NKEYS : (b + 1) * NKEYS, :])
            packed = (every[:, 128:] * factor).astype(I32) * 65536 + (
                every[:, :128] * factor
            ).astype(I32)
            found = jnp.take_along_axis(packed, low, axis=1, mode="promise_in_bounds")
            total = jnp.where(own == step * per_block + b, found, total)
        kept[...] = total

        @pl.when(step == blocks - 1)
        def _():
            p = kept[...]
            right = lax.shift_right_arithmetic(lax.shift_left(p, 16), 16)
            left = lax.shift_right_arithmetic(p - right, 16)
            both = jnp.where(second_ref[...] >= 128, left, right).astype(F32) / factor
            out_ref[...] = both.T.astype(BF16)

    whole = lambda shape: pl.BlockSpec(shape, lambda s: (0, 0))
    return pl.pallas_call(
        body,
        grid=(blocks,),
        out_shape=jax.ShapeDtypeStruct((picks, tokens), BF16),
        in_specs=[
            whole((tokens, picks)),
            whole((tokens, picks)),
            whole((tokens, width)),
            whole((tokens, 1)),
            pl.BlockSpec((rows, width), lambda s: (s, 0)),
        ],
        out_specs=whole((picks, tokens)),
        scratch_shapes=[pltpu.VMEM((tokens, picks), I32)],
        compiler_params=pltpu.CompilerParams(vmem_limit_bytes=48 << 20),
    )(first, second, grads, scale, table)


def by_part(down, parts):
    shaped = down.reshape(down.shape[0], NAD, parts, RANK).transpose(0, 2, 1, 3)
    return shaped.reshape(down.shape)


def on_device(
    inputs,
    cotangent,
    norm_attend,
    norm_memory,
    project_in,
    project_out,
    query_weight,
    gate_weight,
    memory_out,
    half_keys,
    value_table,
    key_picks,
    segment_ids,
    adapter_ids,
    down_input,
    up_input,
    down_attend,
    up_attend,
    down_memory,
    up_query,
    up_gate,
    down_mixed,
    up_mixed,
):
    groups = lax.axis_size(DP)
    ranks = lax.axis_size(TP)
    rank = lax.axis_index(TP)
    local = inputs.shape[0]
    count = segment_ids.shape[0]
    width = project_in.shape[2]
    model = inputs.shape[1]
    space = NAD * RANK
    own_adapters = NAD // ranks

    table = lax.all_gather(value_table, DP, axis=0, tiled=True)
    small = jnp.concatenate(
        [
            up_input.reshape(up_input.shape[0], 3 * width),
            up_query,
            up_gate,
            up_attend,
            up_mixed,
            down_attend.T,
            down_mixed.T,
        ],
        axis=1,
    )
    flat_in = project_in.reshape(project_in.shape[0], 3 * width)
    shards = (flat_in, by_part(down_input, 3), small, project_out.T)
    late = (query_weight, gate_weight, by_part(down_memory, 2), memory_out.T)
    got = exchange([(inputs, SHARE, TP)] + [(x, TREE, DP) for x in shards + late], 1)
    input_rows = got[0].reshape(count, model)
    full_in, full_down_input, full_small, out_t, full_query, full_gate, full_down_memory, mixed_t = [
        x.reshape(-1, x.shape[2]) for x in got[1:]
    ]
    at, pieces = 0, []
    for size in (3 * width, up_query.shape[1], width, model, model, width, width):
        pieces.append(full_small[:, at : at + size])
        at += size
    full_up_input, full_up_query, full_up_gate, full_up_attend, full_up_mixed, attend_t, low_mixed_t = (
        pieces
    )

    owner = jnp.zeros((count,), I32)
    for s in range(adapter_ids.shape[1]):
        owner = jnp.where(segment_ids == s, adapter_ids[0, s], owner)
    column = jnp.arange(space)
    mask = (owner[:, None] == (column // RANK)[None, :]).astype(F32)
    mask_own = lax.dynamic_slice_in_dim(mask, rank * local, local, 0)
    mask_two = jnp.concatenate([mask, mask], axis=1)
    mask_three = jnp.concatenate([mask_two, mask], axis=1)

    first_picks = key_picks[:, 0].reshape(-1, count).T
    second_picks = key_picks[:, 1].reshape(-1, count).T
    own_picks = lax.dynamic_index_in_dim(key_picks, rank, 0, keepdims=False)

    gain_one = norm_attend.astype(F32)
    gain_two = norm_memory.astype(F32)
    normed_one = rms_forward(input_rows.astype(F32), gain_one).astype(BF16)
    low_one = (mm(normed_one, full_down_input) * mask_three).astype(BF16)
    projected = mm(normed_one, full_in) + jnp.concatenate(
        [
            mm(
                low_one[:, p * space : (p + 1) * space],
                full_up_input[:, p * width : (p + 1) * width],
            )
            for p in range(3)
        ],
        axis=1,
    )
    projected = projected.astype(BF16)
    attended = attention_forward(projected, segment_ids, width)
    partial_out = mt(attended, out_t).astype(BF16)
    partial_two = (mt(attended, attend_t) * mask).astype(BF16)
    out_pieces, two_pieces = exchange(
        [
            (partial_out.reshape(ranks, local, model), PIECE, TP),
            (partial_two.reshape(ranks, local, space), PIECE, TP),
        ],
        2,
    )
    low_two = two_pieces.astype(F32).sum(axis=0).astype(BF16)
    residual = inputs.astype(F32)
    middle = residual + out_pieces.astype(F32).sum(axis=0) + mm(low_two, full_up_attend)
    normed_two = rms_forward(middle, gain_two).astype(BF16)
    largest = jnp.max(jnp.sum(jnp.square(value_table.astype(F32)), axis=1))
    normed_rows, low_two_rows, cotangent_rows, norms = exchange(
        [
            (normed_two, SHARE, TP),
            (low_two, SHARE, TP),
            (cotangent, SHARE, TP),
            (jnp.broadcast_to(largest, (8, 128)), SHARE, DP),
        ],
        3,
    )
    normed_rows = normed_rows.reshape(count, model)
    low_two_rows = low_two_rows.reshape(count, space)
    cotangent_rows = cotangent_rows.reshape(count, model)

    low_three = (mm(normed_rows, full_down_memory) * mask_two).astype(BF16)
    memory_query = mm(normed_rows, full_query) + mm(low_three[:, :space], full_up_query)
    gate_pre = mm(normed_rows, full_gate) + mm(low_three[:, space:], full_up_gate)
    weights = pick_weights(memory_query, half_keys[0], own_picks)
    (all_weights,) = exchange([(weights.astype(BF16), SHARE, TP)], 4)
    by_token = all_weights.reshape(-1, count).astype(F32).T
    dense = spread_picks(first_picks, second_picks, by_token)

    grad_low_four = (mt(cotangent_rows, full_up_mixed) * mask).astype(BF16)
    grad_mixed = mm(cotangent_rows, mixed_t) + mm(grad_low_four, low_mixed_t)

    recalled = recall(dense, table)
    sigmoid = jax.nn.sigmoid(gate_pre)
    gate_act = gate_pre * sigmoid
    mixed = (gate_act * recalled).astype(BF16)
    grad_recalled = (grad_mixed * gate_act).astype(BF16)
    grad_gate = (grad_mixed * recalled * sigmoid * (1.0 + gate_pre * (1.0 - sigmoid))).astype(BF16)
    bound = jnp.max(norms) * jnp.sum(
        jnp.square(grad_recalled.astype(F32)), axis=1, keepdims=True
    )
    scale = 32000.0 * lax.rsqrt(jnp.maximum(bound, 1e-30))
    picked = pick_grads(first_picks, second_picks, grad_recalled, scale, table)
    (pick_pieces,) = exchange([(picked.reshape(ranks, -1, count), PIECE, TP)], 5)

    partial_mixed = mt(mixed, mixed_t).astype(BF16)
    partial_four = (mt(mixed, low_mixed_t) * mask).astype(BF16)
    grad_down_mixed = tm(grad_low_four, mixed)

    grad_query = query_grads(weights, pick_pieces, half_keys[0], own_picks)
    partial_normed = (mt(grad_query, full_query) + mt(grad_gate, full_gate)).astype(BF16)
    folds = [
        ((column[:, None] % RANK) == (column[None, :] - p * RANK)).astype(BF16) for p in range(3)
    ]
    three_query = (mt(grad_query, full_up_query) * mask).astype(BF16)
    three_gate = (mt(grad_gate, full_up_gate) * mask).astype(BF16)
    partial_three = (mm(three_query, folds[0]) + mm(three_gate, folds[1])).astype(BF16)
    grad_up_query = tm(low_three[:, :space], grad_query)
    grad_up_gate = tm(low_three[:, space:], grad_gate)
    normed_pieces, three_pieces, mixed_pieces, four_pieces = exchange(
        [
            (partial_normed.reshape(ranks, local, model), PIECE, TP),
            (partial_three.reshape(ranks, local, space), PIECE, TP),
            (partial_mixed.reshape(ranks, local, model), PIECE, TP),
            (partial_four.reshape(ranks, local, space), PIECE, TP),
        ],
        6,
    )
    low_four = four_pieces.astype(F32).sum(axis=0).astype(BF16)
    outputs = (
        middle + mixed_pieces.astype(F32).sum(axis=0) + mm(low_four, full_up_mixed)
    ).astype(BF16)
    grad_three = three_pieces.astype(F32).sum(axis=0).astype(BF16)
    grad_three_full = jnp.concatenate(
        [mt(grad_three, folds[p]) * mask_own for p in range(2)], axis=1
    ).astype(BF16)
    grad_normed_two = normed_pieces.astype(F32).sum(axis=0) + mt(grad_three_full, full_down_memory)
    grad_middle = cotangent.astype(F32) + rms_backward(middle, gain_two, grad_normed_two)
    grad_branch = grad_middle.astype(BF16)
    branch_rows, grad_three_rows, low_four_rows = exchange(
        [(grad_branch, SHARE, TP), (grad_three, SHARE, TP), (low_four, SHARE, TP)], 7
    )
    branch_rows = branch_rows.reshape(count, model)
    grad_three_rows = grad_three_rows.reshape(count, space)
    low_four_rows = low_four_rows.reshape(count, space)

    grad_low_two = (mt(branch_rows, full_up_attend) * mask).astype(BF16)
    grad_attended = (mm(branch_rows, out_t) + mm(grad_low_two, attend_t)).astype(BF16)
    grad_projected = attention_backward(projected, segment_ids, grad_attended, width)
    partial_input = mt(grad_projected, full_in).astype(BF16)
    partial_one = sum(
        mm(
            (
                mt(
                    grad_projected[:, p * width : (p + 1) * width],
                    full_up_input[:, p * width : (p + 1) * width],
                )
                * mask
            ).astype(BF16),
            folds[p],
        )
        for p in range(3)
    ).astype(BF16)
    input_pieces, one_partials = exchange(
        [(partial_input.reshape(ranks, local, model), PIECE, TP), (partial_one, SHARE, TP)], 8
    )
    grad_one_rows = one_partials.astype(F32).sum(axis=0).astype(BF16)
    grad_one = lax.dynamic_slice_in_dim(grad_one_rows, rank * local, local, 0)
    grad_one_full = jnp.concatenate(
        [mt(grad_one, folds[p]) * mask_own for p in range(3)], axis=1
    ).astype(BF16)
    grad_normed_one = input_pieces.astype(F32).sum(axis=0) + mt(grad_one_full, full_down_input)
    input_grad = grad_middle + rms_backward(residual, gain_one, grad_normed_one)

    def own_columns(compact, parts):
        columns = jnp.arange(own_adapters * parts * RANK)
        pattern = (column[:, None] == (columns % (parts * RANK))[None, :]).astype(BF16)
        mine = owner[:, None] == (rank * own_adapters + columns // (parts * RANK))[None, :]
        return jnp.where(mine, mm(compact, pattern), 0.0).astype(BF16)

    grad_down_input = tm(normed_one, own_columns(grad_one_rows, 3))
    grad_down_memory = tm(normed_rows, own_columns(grad_three_rows, 2))
    grad_up_input = jnp.concatenate(
        [
            tm(
                low_one[:, p * space : (p + 1) * space],
                grad_projected[:, p * width : (p + 1) * width],
            )
            for p in range(3)
        ],
        axis=1,
    )
    grad_down_attend = tm(grad_low_two, attended)
    own_branch = lax.dynamic_slice_in_dim(branch_rows, rank * width, width, 1)
    own_cotangent = lax.dynamic_slice_in_dim(cotangent_rows, rank * width, width, 1)
    grad_up_attend = tm(low_two_rows, own_branch)
    grad_up_mixed = tm(low_four_rows, own_cotangent)
    ups = jnp.concatenate(
        [
            grad_up_input,
            grad_up_query,
            grad_up_gate,
            grad_up_attend,
            grad_up_mixed,
            grad_down_attend,
            grad_down_mixed,
        ],
        axis=1,
    ).astype(BF16)
    downs = jnp.concatenate([grad_down_input, grad_down_memory], axis=1).astype(BF16)
    up_parts, down_parts = exchange(
        [
            (ups.reshape(groups, -1, ups.shape[1]), PIECE, DP),
            (downs.reshape(groups, -1, downs.shape[1]), PIECE, DP),
        ],
        9,
    )
    up_sums = up_parts.astype(F32).sum(axis=0)
    down_sums = down_parts.astype(F32).sum(axis=0)
    at, parts = 0, []
    for size in (3 * width, up_query.shape[1], width, width, width, width, width):
        parts.append(up_sums[:, at : at + size])
        at += size
    cut = own_adapters * 3 * RANK
    return (
        outputs,
        input_grad,
        down_sums[:, :cut],
        parts[0].reshape(up_input.shape),
        parts[5].T,
        parts[3],
        down_sums[:, cut:],
        parts[1],
        parts[2],
        parts[6].T,
        parts[4],
    )


def solution(mesh):
    rows = P((DP, TP), None)
    both = P(DP, TP)
    wide = P(DP, None)
    turned = P(TP, DP)
    split = P(DP, None, TP)
    return jax.shard_map(
        on_device,
        mesh=mesh,
        in_specs=(
            rows,
            rows,
            P(),
            P(),
            split,
            turned,
            both,
            both,
            turned,
            P(TP, None, None, None),
            both,
            P(None, None, None, DP),
            P(DP),
            wide,
            wide,
            split,
            turned,
            wide,
            wide,
            both,
            both,
            turned,
            wide,
        ),
        out_specs=(rows, rows, both, split, turned, both, both, both, both, turned, both),
        check_vma=False,
    )
```

profile of v0, /device:TPU:9, one launch (start us, length us, event | category | flops | bytes accessed | tf_op | source)
XLA Modules:
  0.0 582.5 jit_solution(3492585265321409069)
XLA Ops:
  13.4 73.3 %shard_map.302 = (bf16[4,128,1024]{2,1,0:T(8,128)(2,1)}, bf16[8,128,768]{2,1,0:T(8,128)(2,1)}, bf16[8,128,384]{2,1,0:T(8,128)(2,1)}, bf16[8,16,4096]{2,1,0:T(8,1...) custom-call(bf16[128,1024]{1,0:T(8,128)(2,1)} %refs_0_.1, ...), custom_call_target="tpu_custom_call" | custom-call | tf_op jit(solution)/shard_map/pallas_call | solution.py:167
  87.8 1.5 multiply_reduce_fusion.1
  89.3 1.9 select_select_fusion
  91.4 1.6 multiply_convert_fusion
  95.9 5.0 shard_map.303
  101.8 1.5 convolution_convert_fusion.2
  103.3 29.9 %shard_map.304 = (bf16[4,128,1024]{2,1,0:T(8,128)(2,1)}, bf16[4,128,128]{2,1,0:T(8,128)(2,1)}) custom-call(bf16[4,128,1024]{2,1,0:T(8,128)(2,1)} %bitcast.170, bf16[4,128,128]{2,1,0:T(8,128)(2,1)} %bitcast.241), custom_call_target="tpu_custom_call" | custom-call | tf_op jit(solution)/shard_map/pallas_call | solution.py:167
  134.1 3.4 multiply_reduce_fusion
  138.1 1.5 convert_reduce_fusion.3
  141.3 1.2 broadcast_in_dim.27.refs_3_
  142.6 51.7 %shard_map.305 = (bf16[4,128,1024]{2,1,0:T(8,128)(2,1)}, bf16[4,128,128]{2,1,0:T(8,128)(2,1)}, bf16[4,128,1024]{2,1,0:T(8,128)(2,1)}, f32[8,8,128]{2,1,0:T(8,128)}) custom-call(bf16[128,1024]{1,0:T(8,128)(2,1)} %multiply_convert_fusion.4.refs_0_, bf16[128,128]{1,0:T(8,128)(2,1)} %copy-done.43, bf16[128,1024]{1,0:T(8,128)(2,1)} %refs_2_.1, ...), custom_call_target="tpu_custom_call" | custom-call | tf_op jit(solution)/shard_map/pallas_call | solution.py:167
  195.3 1.8 fusion.6
  198.2 5.5 shard_map.306.weights_ref
  204.3 7.7 %shard_map.310 = bf16[4,32,512]{2,1,0:T(8,128)(2,1)} custom-call(bf16[32,512]{1,0:T(8,128)(2,1)} %convert_element_type.184.refs_0_), custom_call_target="tpu_custom_call" | custom-call | tf_op jit(solution)/shard_map/pallas_call | solution.py:167
  215.0 2.5 fusion.1
  217.6 2.3 copy.162
  219.9 2.3 copy.163
  223.0 34.5 %shard_map.311.dense_ref = bf16[512,65536]{1,0:T(8,128)(2,1)} custom-call(s32[512,128]{1,0:T(8,128)S(1)} %bitcast.159, s32[512,128]{1,0:T(8,128)S(1)} %bitcast.161, f32[512,128]{1,0:T(8,128)S(1)} %bitcast.163), custom_call_target="tpu_custom_call" | custom-call | tf_op jit(solution)/shard_map/pallas_call | solution.py:350
  259.5 1.8 fusion.83
  261.4 1.4 fusion.18
  263.8 1.2 convolution_add_fusion.3
  265.1 36.4 %shard_map.312 = f32[512,256]{1,0:T(8,128)S(1)} custom-call(bf16[512,65536]{1,0:T(8,128)(2,1)} %shard_map.311.dense_ref, bf16[65536,256]{1,0:T(8,128)(2,1)} %all-gather.2.cloned.1.call-done.table_ref), custom_call_target="tpu_custom_call" | custom-call | tf_op jit(solution)/shard_map/pallas_call | solution.py:372
  301.5 1.4 multiply_convert_fusion.1
  302.9 1.8 fusion.13
  304.7 1.4 convolution_convert_fusion.1
  306.9 52.7 %shard_map.307 = bf16[128,512]{1,0:T(8,128)(2,1)S(1)} custom-call(s32[512,128]{1,0:T(8,128)S(1)} %bitcast.160, s32[512,128]{1,0:T(8,128)S(1)} %bitcast.162, bf16[512,256]{1,0:T(8,128)(2,1)S(1)} %get-tuple-element.105.grads_ref, f32[512,1]{1,0:T(8,128)S(1)} %copy.152.scale_ref, bf16[65536,256]{1,0:T(8,128)(2,1)} %all-gather.2.cloned.1.call-done.table_ref), custom_call_target="tpu_custom_call" | custom-call | tf_op jit(solution)/shard_map/pallas_call | solution.py:420
  360.3 4.8 shard_map.308.pieces_ref
  366.0 4.8 shard_map.309
  370.9 3.4 fusion.178
  374.2 1.4 fusion.22
  375.6 3.2 add_convert_fusion
  378.8 1.9 fusion.12
  380.8 55.6 %shard_map.313 = (bf16[4,128,1024]{2,1,0:T(8,128)(2,1)}, bf16[4,128,128]{2,1,0:T(8,128)(2,1)}, bf16[4,128,1024]{2,1,0:T(8,128)(2,1)}, bf16[4,128,128]{2,1,0:T(8,128)(2,1)}) custom-call(bf16[4,128,1024]{2,1,0:T(8,128)(2,1)} %bitcast.175, bf16[4,128,128]{2,1,0:T(8,128)(2,1)} %bitcast.222, bf16[4,128,1024]{2,1,0:T(8,128)(2,1)} %bitcast.171, ...), custom_call_target="tpu_custom_call" | custom-call | tf_op jit(solution)/shard_map/pallas_call | solution.py:167
  437.8 1.5 convert_reduce_fusion.1
  439.3 2.2 multiply_reduce_fusion.2
  442.1 2.1 fusion.173
  444.2 31.0 %shard_map.314 = (bf16[4,128,1024]{2,1,0:T(8,128)(2,1)}, bf16[4,128,128]{2,1,0:T(8,128)(2,1)}, bf16[4,128,128]{2,1,0:T(8,128)(2,1)}) custom-call(bf16[128,1024]{1,0:T(8,128)(2,1)} %get-tuple-element.98.refs_0_, bf16[128,128]{1,0:T(8,128)(2,1)} %copy-done.40, bf16[128,128]{1,0:T(8,128)(2,1)} %reduce_sum.176.refs_2_), custom_call_target="tpu_custom_call" | custom-call | tf_op jit(solution)/shard_map/pallas_call | solution.py:167
  475.3 1.8 fusion.19
  478.6 9.0 %shard_map.315 = bf16[512,768]{1,0:T(8,128)(2,1)S(1)} custom-call(bf16[512,768]{1,0:T(8,128)(2,1)S(1)} %fusion.2.projected_ref, s32[1,512]{1,0:T(1,128)S(1)} %bitcast.169, s32[512,1]{1,0:T(8,128)S(1)} %copy.143.down_ref, bf16[512,256]{1,0:T(8,128)(2,1)S(1)} %fusion.7.upstream_ref), custom_call_target="tpu_custom_call" | custom-call | tf_op jit(solution)/shard_map/pallas_call | solution.py:252
  487.6 1.9 fusion.21
  489.6 3.5 convolution_convert_fusion
  498.5 1.2 convolution_add_fusion.9
  499.7 2.0 fusion.17.refs_1_
  501.7 36.0 %shard_map.316 = (bf16[4,128,1024]{2,1,0:T(8,128)(2,1)}, bf16[4,512,128]{2,1,0:T(8,128)(2,1)}) custom-call(bf16[4,128,1024]{2,1,0:T(8,128)(2,1)} %bitcast.208, bf16[512,128]{1,0:T(8,128)(2,1)} %fusion.17.refs_1_), custom_call_target="tpu_custom_call" | custom-call | tf_op jit(solution)/shard_map/pallas_call | solution.py:167
  545.7 18.3 %shard_map.317 = (bf16[8,16,2560]{2,1,0:T(8,128)(2,1)}, bf16[8,128,160]{2,1,0:T(8,128)(2,1)}) custom-call(bf16[8,16,2560]{2,1,0:T(8,128)(2,1)} %copy-done.35, bf16[8,128,160]{2,1,0:T(8,128)(2,1)} %pad_maximum_fusion.refs_1_), custom_call_target="tpu_custom_call" | custom-call | tf_op jit(solution)/shard_map/pallas_call | solution.py:167
  564.0 1.2 convert_reduce_fusion.4
  570.7 1.7 fusion.38
  572.7 1.9 fusion.8
  (278 shorter events, 49.4 us)
Async XLA Ops:
  7.2 5.2 copy-start.78
  7.3 257.8 %all-gather.2.cloned.1.call-start = ((), (), s32[]{:S(2)}) async-start(), calls=%async_computation | async-start | bytes 37748736 | tf_op jit(solution)/shard_map/all_gather | solution.py:477
  8.0 4.6 copy-start.70
  8.0 4.6 copy-start.61
  8.0 4.6 copy-start.62
  8.0 4.6 copy-start.71
  8.1 4.7 copy-start.72
  8.1 79.1 %copy-start.77 = (s32[1,3]{1,0:T(1,128)S(1)}, s32[1,3]{1,0:T(1,128)}, u32[]{:S(2)}) copy-start(s32[1,3]{1,0:T(1,128)} %param.36) | copy-start | bytes 40
  86.7 6.4 %copy-start.36 = (bf16[8,128,384]{2,1,0:T(8,128)(2,1)S(1)}, bf16[8,128,384]{2,1,0:T(8,128)(2,1)}, u32[]{:S(2)}) copy-start(bf16[8,128,384]{2,1,0:T(8,128)(2,1)} %get-tuple-element.39) | copy-start | bytes 2359300
  87.2 13.7 %copy-start.73 = (s32[128]{0:T(128)}, s32[128]{0:T(128)S(1)}, u32[]{:S(2)}) copy-start(s32[128]{0:T(128)S(1)} %get-tuple-element.132) | copy-start | bytes 1540
  91.4 103.9 %copy-start.20 = (f32[512,128]{1,0:T(8,128)}, f32[512,128]{1,0:T(8,128)S(1)}, u32[]{:S(2)}) copy-start(f32[512,128]{1,0:T(8,128)S(1)} %compare_convert_fusion) | copy-start | bytes 786436
  95.9 5.9 %copy-start.13 = (bf16[8,128,256]{2,1,0:T(8,128)(2,1)S(1)}, bf16[8,128,256]{2,1,0:T(8,128)(2,1)}, u32[]{:S(2)}) copy-start(bf16[8,128,256]{2,1,0:T(8,128)(2,1)} %get-tuple-element.41) | copy-start | bytes 1572868
  134.1 5.5 copy-start.43
  134.1 5.5 copy-start.8
  139.9 302.2 %copy-start.4 = (f32[128,1024]{1,0:T(8,128)}, f32[128,1024]{1,0:T(8,128)S(1)}, u32[]{:S(2)}) copy-start(f32[128,1024]{1,0:T(8,128)S(1)} %get-tuple-element.123) | copy-start | bytes 1572868
  140.5 57.4 %copy-start.80 = (f32[128]{0:T(128)}, f32[128]{0:T(128)S(1)}, u32[]{:S(2)}) copy-start(f32[128]{0:T(128)S(1)} %get-tuple-element.118) | copy-start | bytes 1540
  198.2 16.2 %copy-start.63 = (f32[8,8,128]{2,1,0:T(8,128)S(1)}, f32[8,8,128]{2,1,0:T(8,128)}, u32[]{:S(2)}) copy-start(f32[8,8,128]{2,1,0:T(8,128)} %get-tuple-element.50) | copy-start | bytes 98308
  217.6 4.6 copy-start.56
  223.0 36.6 %copy-start.33 = (bf16[512,256]{1,0:T(8,128)(2,1)S(1)}, bf16[512,256]{1,0:T(8,128)(2,1)}, u32[]{:S(2)}) copy-start(bf16[512,256]{1,0:T(8,128)(2,1)} %copy-done.32) | copy-start | bytes 786436
  223.0 38.4 %copy-start.16 = (bf16[4,128,1024]{2,1,0:T(8,128)(2,1)S(1)}, bf16[4,128,1024]{2,1,0:T(8,128)(2,1)}, u32[]{:S(2)}) copy-start(bf16[4,128,1024]{2,1,0:T(8,128)(2,1)} %get-tuple-element.47) | copy-start | bytes 3145732
  223.0 38.4 %copy-start.74 = (s32[128]{0:T(128)S(1)}, s32[128]{0:T(128)}, u32[]{:S(2)}) copy-start(s32[128]{0:T(128)} %copy-done.73) | copy-start | bytes 1540
  257.4 6.4 %copy-start.11 = (bf16[8,128,256]{2,1,0:T(8,128)(2,1)S(1)}, bf16[8,128,256]{2,1,0:T(8,128)(2,1)}, u32[]{:S(2)}) copy-start(bf16[8,128,256]{2,1,0:T(8,128)(2,1)} %get-tuple-element.48) | copy-start | bytes 1572868
  265.1 36.4 %copy-start.31 = (bf16[4,128,1024]{2,1,0:T(8,128)(2,1)S(1)}, bf16[4,128,1024]{2,1,0:T(8,128)(2,1)}, u32[]{:S(2)}) copy-start(bf16[4,128,1024]{2,1,0:T(8,128)(2,1)} %get-tuple-element.44) | copy-start | bytes 3145732
  265.1 36.4 %copy-start.37 = (bf16[8,128,256]{2,1,0:T(8,128)(2,1)S(1)}, bf16[8,128,256]{2,1,0:T(8,128)(2,1)}, u32[]{:S(2)}) copy-start(bf16[8,128,256]{2,1,0:T(8,128)(2,1)} %get-tuple-element.49) | copy-start | bytes 1572868
  265.1 36.4 %copy-start.38 = (f32[512,256]{1,0:T(8,128)S(1)}, f32[512,256]{1,0:T(8,128)}, u32[]{:S(2)}) copy-start(f32[512,256]{1,0:T(8,128)} %convolution_add_fusion.3) | copy-start | bytes 1572868
  265.1 36.4 %copy-start.39 = (f32[512,256]{1,0:T(8,128)S(1)}, f32[512,256]{1,0:T(8,128)}, u32[]{:S(2)}) copy-start(f32[512,256]{1,0:T(8,128)} %fusion.83) | copy-start | bytes 1572868
  370.9 4.7 copy-start.10
  378.8 58.5 %copy-start.21 = (f32[512,128]{1,0:T(8,128)S(1)}, f32[512,128]{1,0:T(8,128)}, u32[]{:S(2)}) copy-start(f32[512,128]{1,0:T(8,128)} %copy-done.20) | copy-start | bytes 786436
  436.4 5.1 copy-start.54
  437.3 6.9 %copy-start.40 = (bf16[128,128]{1,0:T(8,128)(2,1)}, bf16[128,128]{1,0:T(8,128)(2,1)S(1)}, u32[]{:S(2)}) copy-start(bf16[128,128]{1,0:T(8,128)(2,1)S(1)} %reduce_sum.178.refs_1_) | copy-start | bytes 98308
  437.4 4.8 copy-start.27
  437.4 4.8 copy-start.81
  437.4 4.7 copy-start.83
  444.2 33.9 %copy-start.14 = (bf16[8,128,256]{2,1,0:T(8,128)(2,1)S(1)}, bf16[8,128,256]{2,1,0:T(8,128)(2,1)}, u32[]{:S(2)}) copy-start(bf16[8,128,256]{2,1,0:T(8,128)(2,1)} %get-tuple-element.41) | copy-start | bytes 1572868
  489.6 5.2 copy-start.34
  489.6 5.5 copy-start.19
  493.1 5.4 copy-start.65
  493.1 5.4 copy-start.69
  493.1 5.4 copy-start.76
  496.8 42.2 %copy-start.7 = (bf16[1024,512]{1,0:T(8,128)(2,1)S(1)}, bf16[1024,512]{1,0:T(8,128)(2,1)}, u32[]{:S(2)}) copy-start(bf16[1024,512]{1,0:T(8,128)(2,1)} %copy.162) | copy-start | bytes 3145732
  499.7 40.7 %copy-start.6 = (bf16[1024,512]{1,0:T(8,128)(2,1)S(1)}, bf16[1024,512]{1,0:T(8,128)(2,1)}, u32[]{:S(2)}) copy-start(bf16[1024,512]{1,0:T(8,128)(2,1)} %copy.163) | copy-start | bytes 3145732
  501.7 38.7 %copy-start.53 = (bf16[4,128,128]{2,1,0:T(8,128)(2,1)S(1)}, bf16[4,128,128]{2,1,0:T(8,128)(2,1)}, u32[]{:S(2)}) copy-start(bf16[4,128,128]{2,1,0:T(8,128)(2,1)} %get-tuple-element.60) | copy-start | bytes 393220
  501.7 38.7 %copy-start.84 = (s32[64]{0:T(128)S(1)}, s32[64]{0:T(128)}, u32[]{:S(2)}) copy-start(s32[64]{0:T(128)} %get-tuple-element.127) | copy-start | bytes 772
  501.7 38.7 %copy-start.85 = (s32[64]{0:T(128)S(1)}, s32[64]{0:T(128)}, u32[]{:S(2)}) copy-start(s32[64]{0:T(128)} %get-tuple-element.128) | copy-start | bytes 772
  543.6 24.1 %copy-start.22 = (f32[512,128]{1,0:T(8,128)S(1)}, f32[512,128]{1,0:T(8,128)}, u32[]{:S(2)}) copy-start(f32[512,128]{1,0:T(8,128)} %copy-done.20) | copy-start | bytes 786436
  543.6 24.3 %copy-start.82 = (s32[128]{0:T(128)S(1)}, s32[128]{0:T(128)}, u32[]{:S(2)}) copy-start(s32[128]{0:T(128)} %iota_add_fusion) | copy-start | bytes 1540
  544.9 25.6 %copy-start.29 = (bf16[4,128,1024]{2,1,0:T(8,128)(2,1)S(1)}, bf16[4,128,1024]{2,1,0:T(8,128)(2,1)}, u32[]{:S(2)}) copy-start(bf16[4,128,1024]{2,1,0:T(8,128)(2,1)} %get-tuple-element.56) | copy-start | bytes 3145732
  564.0 6.7 %copy-start.9 = (bf16[128,1024]{1,0:T(8,128)(2,1)S(1)}, bf16[128,1024]{1,0:T(8,128)(2,1)}, u32[]{:S(2)}) copy-start(bf16[128,1024]{1,0:T(8,128)(2,1)} %refs_0_.1) | copy-start | bytes 786436
  (40 other events, 105.8 us)
Sparse Core Ops, SparseCore 0:
  10.0 189.8 all-gather.1
where the time goes:
time: 591 us; the launch traced here: 583 us
  Pallas kernels  456 us (77%)
  matrix products  55.9 us (9%)
  other arithmetic  32.1 us (5%)
  local copies, waits for them, and re-layouts  22.1 us (4%)
  between operations  15.7 us (3%)
    pallas_call x9, Pallas kernels, exchange(): pl.pallas_call(body, out_shape=shapes, in_specs=[ANY] * n, out_specs=[ANY...  308 us
    pallas_call x1, Pallas kernels, pick_grads(): pl.pallas_call(body, grid=(blocks,), out_shape=jax.ShapeDtypeStruct((pick...  52.7 us
    pallas_call x1, Pallas kernels, recall(): pl.pallas_call(body, grid=(rows // block,), out_shape=jax.ShapeDtypeStruc...  36.4 us
    pallas_call x1, Pallas kernels, spread_picks(): pl.pallas_call(body, grid=(tokens // sub,), out_shape=jax.ShapeDtypeStruc...  34.5 us
    dot_general x16, matrix products, mt(): lax.dot_general(a, b, (((1,), (1,)), ((), ())), preferred_element_type=F32)  23.7 us
    dot_general x21, matrix products, mm(): lax.dot_general(a, b, (((1,), (0,)), ((), ())), preferred_element_type=F32)  22.7 us
  transfers between devices with their start and end apart: 1, of which 0 were waited for; matrix products, arithmetic and copies ran while one was open for 8% of the time, Pallas kernels for 36%

commit v1 on v0

v1 whole, which is shorter than its diff:
```python
import functools

import jax
import jax.numpy as jnp
from jax import lax
from jax.experimental import pallas as pl
from jax.experimental.pallas import tpu as pltpu
from jax.sharding import PartitionSpec as P

DP, TP = "dp", "tensor"
HD = 64
PARTS = 1
NKEYS = 256
RANK = 16
NAD = 8
EPS = 1e-06
NEGATIVE = -1e30
F32, BF16, I32 = jnp.float32, jnp.bfloat16, jnp.int32
MESH = pl.DeviceIdType.MESH
ANY = pl.BlockSpec(memory_space=pl.ANY)


def mm(a, b):
    return lax.dot_general(a, b, (((1,), (0,)), ((), ())), preferred_element_type=F32)


def mt(a, b):
    return lax.dot_general(a, b, (((1,), (1,)), ((), ())), preferred_element_type=F32)


def tm(a, b):
    return lax.dot_general(a, b, (((0,), (0,)), ((), ())), preferred_element_type=F32)


def two_parts(x):
    top = x.astype(BF16)
    return top, (x - top.astype(F32)).astype(BF16)


SHARE, PIECE, SPLIT, SIDE, TREE, NEST = range(6)


def exchange(items, cid):
    arrays = [item[0] for item in items]
    kinds = [item[1] for item in items]
    axes = [item[2] for item in items]
    n = len(items)
    trees = [a for a in range(n) if kinds[a] in (TREE, NEST)]
    nests = [a for a in range(n) if kinds[a] == NEST]
    used = [axis for axis in (DP, TP) if axis in axes or (axis == TP and nests)]
    sizes = {axis: lax.axis_size(axis) for axis in used}
    half = sizes[DP] // 2 if trees else 0
    relayed = half == 4
    route, load = {}, [0, 0]
    for a in sorted(trees, key=lambda a: -arrays[a].size * (4 if a in nests else 1)):
        route[a] = 1 + (load[0] > load[1])
        load[route[a] - 1] += arrays[a].size * (4 if a in nests else 1)
    most = max(half if a in trees else sizes[axes[a]] for a in range(n))

    def columns(ref, a, p, kind):
        wide = arrays[a].shape[-1] // (sizes[axes[a]] if kind == SPLIT else 1)
        return ref.at[:, pl.ds(pl.multiple_of(p * wide, wide), wide)]

    def body(*refs):
        ins, outs = refs[:n], refs[n : 2 * n]
        stages = dict(zip(nests, refs[2 * n : 2 * n + len(nests)]))
        send, recv, pass_send, pass_recv, nest_send, nest_recv, local = refs[2 * n + len(nests) :]
        me = {axis: lax.axis_index(axis) for axis in used}
        barrier = pltpu.get_barrier_semaphore()
        for axis in used:

            @pl.loop(1, sizes[axis])
            def _(d):
                pl.semaphore_signal(
                    barrier,
                    inc=1,
                    device_id={axis: lax.rem(me[axis] + d, sizes[axis])},
                    device_id_type=MESH,
                )

        def source(a, p):
            if kinds[a] in (PIECE, SIDE):
                return ins[a].at[p]
            return columns(ins[a], a, p, SPLIT) if kinds[a] == SPLIT else ins[a]

        def place(a, p):
            return columns(outs[a], a, p, SIDE) if kinds[a] == SIDE else outs[a].at[p]

        own = []
        for a in range(n):
            if kinds[a] == NEST:
                home = columns(stages[a], a, me[TP], SIDE)
                own.append(pltpu.make_async_copy(ins[a], home, local.at[a]))
            else:
                here = me[axes[a]]
                own.append(pltpu.make_async_copy(source(a, here), place(a, here), local.at[a]))
        for c in own:
            c.start()
        pl.semaphore_wait(barrier, sum(sizes.values()) - len(used))

        def copy(a, d):
            axis = axes[a]
            peer = lax.rem(me[axis] + d, sizes[axis])
            return pltpu.make_async_remote_copy(
                src_ref=source(a, peer),
                dst_ref=place(a, me[axis]),
                send_sem=send.at[a, d],
                recv_sem=recv.at[a, d],
                device_id={axis: peer},
                device_id_type=MESH,
            )

        def nest_copy(a, d):
            return pltpu.make_async_remote_copy(
                src_ref=ins[a],
                dst_ref=columns(stages[a], a, me[TP], SIDE),
                send_sem=nest_send.at[nests.index(a), d],
                recv_sem=nest_recv.at[nests.index(a), d],
                device_id={TP: lax.rem(me[TP] + d, sizes[TP])},
                device_id_type=MESH,
            )

        def first(a):
            return stages[a] if a in stages else ins[a]

        def partner(d):
            if not relayed:
                return lax.rem(me[DP] + 2 * d, sizes[DP])
            across = 2 - 4 * lax.rem(lax.div(me[DP], 2), 2) if d & 1 else 0
            along = 4 - 8 * lax.div(me[DP], 4) if d & 2 else 0
            return me[DP] + across + along

        def holder(d):
            if relayed or (isinstance(d, int) and d == 0):
                return partner(d) if d else me[DP]
            return lax.rem(me[DP] - 2 * d + sizes[DP], sizes[DP])

        def tree_copy(a, d):
            relay = relayed and d == 3
            shard = outs[a].at[holder(route[a])] if relay else first(a)
            return pltpu.make_async_remote_copy(
                src_ref=shard,
                dst_ref=shard if relay else outs[a].at[me[DP]],
                send_sem=send.at[a, d],
                recv_sem=recv.at[a, d],
                device_id={DP: partner(3 - route[a] if relay else d)},
                device_id_type=MESH,
            )

        def pass_on(a, d):
            own = isinstance(d, int) and d == 0
            return pltpu.make_async_remote_copy(
                src_ref=first(a) if own else outs[a].at[holder(d)],
                dst_ref=outs[a].at[holder(d)],
                send_sem=pass_send.at[trees.index(a), d],
                recv_sem=pass_recv.at[trees.index(a), d],
                device_id={DP: me[DP] + 1 - 2 * lax.rem(me[DP], 2)},
                device_id_type=MESH,
            )

        def over(start, stop, chosen, step):
            if chosen:

                @pl.loop(start, stop)
                def _(d):
                    for a in chosen:
                        step(a, d)

        plain = [a for a in trees if a not in nests]
        over(1, sizes.get(TP, 1), nests, lambda a, d: nest_copy(a, d).start())

        def begin(chosen):
            if relayed:
                for a in chosen:
                    tree_copy(a, 1).start()
                    tree_copy(a, 2).start()
            else:
                over(1, half, chosen, lambda a, d: tree_copy(a, d).start())
            for a in chosen:
                pass_on(a, 0).start()

        begin(plain)
        flat = {axis: [a for a in range(n) if axes[a] == axis and a not in trees] for axis in used}
        for axis in used:
            over(1, sizes[axis], flat[axis], lambda a, d: copy(a, d).start())
        over(1, sizes.get(TP, 1), nests, lambda a, d: nest_copy(a, d).wait())
        homes = []
        for a in nests:
            own[a].wait()
            homes.append(pltpu.make_async_copy(stages[a], outs[a].at[me[DP]], local.at[a]))
            homes[-1].start()
        begin(nests)

        def forward(a, d):
            tree_copy(a, d).wait_recv()
            pass_on(a, d).start()

        def settle(a, d):
            tree_copy(a, d).wait_send()
            pass_on(a, d).wait()

        for chosen in (plain, nests):
            if relayed:
                for a in chosen:
                    forward(a, route[a])
                    tree_copy(a, 3).start()
                for a in chosen:
                    forward(a, 3 - route[a])
            else:
                over(1, half, chosen, forward)
        if relayed:
            for a in trees:
                forward(a, 3)
            for d in range(1, 4):
                for a in trees:
                    settle(a, d)
        else:
            over(1, half, trees, settle)
        for a in trees:
            pass_on(a, 0).wait()
        for axis in used:
            over(1, sizes[axis], flat[axis], lambda a, d: copy(a, d).wait())
        for c in homes + [own[a] for a in range(n) if a not in nests]:
            c.wait()

    shapes = []
    for a, x in enumerate(arrays):
        peers = sizes[axes[a]]
        shape = {
            PIECE: (peers,) + x.shape[1:],
            SPLIT: (peers, x.shape[0], x.shape[-1] // peers),
            SIDE: x.shape[1:-1] + (peers * x.shape[-1],),
            NEST: (peers, x.shape[0], sizes.get(TP, 1) * x.shape[-1]),
        }.get(kinds[a], (peers,) + x.shape)
        shapes.append(jax.ShapeDtypeStruct(shape, x.dtype))
    for a in nests:
        shapes.append(jax.ShapeDtypeStruct(shapes[a].shape[1:], arrays[a].dtype))
    flat_sems = pltpu.SemaphoreType.DMA((n, most))
    pass_sems = pltpu.SemaphoreType.DMA((max(len(trees), 1), max(half, 1)))
    nest_sems = pltpu.SemaphoreType.DMA((max(len(nests), 1), sizes.get(TP, 1)))
    return pl.pallas_call(
        body,
        out_shape=shapes,
        in_specs=[ANY] * n,
        out_specs=[ANY] * len(shapes),
        scratch_shapes=[flat_sems] * 2
        + [pass_sems] * 2
        + [nest_sems] * 2
        + [pltpu.SemaphoreType.DMA((n,))],
        compiler_params=pltpu.CompilerParams(collective_id=cid, has_side_effects=True),
    )(*arrays)[:n]


def whole(shape):
    return pl.BlockSpec(shape, lambda *_: (0,) * len(shape))


def stage(body, outs, ins, scratch=(), limit=56):
    return pl.pallas_call(
        body,
        grid=(1,),
        out_shape=[jax.ShapeDtypeStruct(shape, dtype) for shape, dtype in outs],
        in_specs=[whole(x.shape) for x in ins],
        out_specs=[whole(shape) for shape, _ in outs],
        scratch_shapes=list(scratch),
        compiler_params=pltpu.CompilerParams(vmem_limit_bytes=limit << 20),
    )(*ins)


def rms_forward(values, gain):
    factor = lax.rsqrt(jnp.mean(values * values, axis=-1, keepdims=True) + EPS)
    return values * factor * gain


def rms_backward(values, gain, upstream):
    factor = lax.rsqrt(jnp.mean(values * values, axis=-1, keepdims=True) + EPS)
    scaled = upstream * gain
    return factor * scaled - values * (factor * factor * factor) * jnp.mean(
        values * scaled, axis=-1, keepdims=True
    )


def masked(values, owner):
    columns = lax.broadcasted_iota(I32, values.shape, 1)
    adapter = lax.rem(lax.div(columns, RANK), NAD)
    return jnp.where(adapter == owner, values, 0.0).astype(BF16)


def folding(parts):
    shape = (parts * RANK, parts * NAD * RANK)
    short = lax.broadcasted_iota(I32, shape, 0)
    column = lax.broadcasted_iota(I32, shape, 1)
    same = (lax.div(short, RANK) == lax.div(column, NAD * RANK)) & (
        lax.rem(short, RANK) == lax.rem(column, RANK)
    )
    return jnp.where(same, 1.0, 0.0).astype(BF16)


def shorten(values):
    return mt(folding(values.shape[1] // (NAD * RANK)), values).astype(BF16)


def lengthen(short, owner):
    return masked(tm(short, folding(short.shape[0] // RANK)), owner)


def side_by_side(blocks):
    return jnp.concatenate([blocks[p] for p in range(blocks.shape[0])], axis=1)


def block_probs(queries, keys, across_ref, down_ref, r, block):
    top = (r + 1) * block
    at = slice(r * block, top)
    scores = mt(queries[at], keys[:top]) * HD**-0.5
    place = lax.broadcasted_iota(I32, (block, top), 0) + r * block
    other = lax.broadcasted_iota(I32, (block, top), 1)
    ahead = across_ref[:, :top]
    seen = (other <= place) & ((ahead == 0) | (ahead == down_ref[at, :]))
    scores = jnp.where(seen, scores, NEGATIVE)
    raised = jnp.exp(scores - jnp.max(scores, axis=-1, keepdims=True))
    return raised / jnp.sum(raised, axis=-1, keepdims=True)


def wide_lanes(pair, base=0):
    return pl.ds(pl.multiple_of(base + pair * 2 * HD, 2 * HD), 2 * HD)


def project_and_attend(rows, gain, down, ups, weight, across, below, owner, block=128):
    count, model = rows.shape
    width = weight.shape[1] // 3
    space = NAD * RANK

    def body(
        rows_ref, gain_ref, down_ref, ups_ref, weight_ref, across_ref, below_ref, owner_ref,
        normed_ref, low_ref, projected_ref, out_ref,
    ):
        @pl.loop(0, count // block)
        def _(c):
            at = pl.ds(pl.multiple_of(c * block, block), block)
            normed = rms_forward(rows_ref[at, :].astype(F32), gain_ref[...]).astype(BF16)
            normed_ref[at, :] = normed
            low = masked(mm(normed, down_ref[...]), owner_ref[at, :])
            low_ref[at, :] = low
            for p in range(3):
                lanes = slice(p * width, (p + 1) * width)
                projected_ref[at, lanes] = (
                    mm(normed, weight_ref[:, lanes])
                    + mm(low[:, p * space : (p + 1) * space], ups_ref[:, lanes])
                ).astype(BF16)

        @pl.loop(0, width // (2 * HD))
        def _(pair):
            queries, keys, values = [projected_ref[:, wide_lanes(pair, p * width)] for p in range(3)]
            for r in range(count // block):
                top = (r + 1) * block
                parts = []
                for lanes in (slice(0, HD), slice(HD, 2 * HD)):
                    probs = block_probs(
                        queries[:, lanes], keys[:, lanes], across_ref, below_ref, r, block
                    )
                    parts.append(mm(probs.astype(BF16), values[:top, lanes]))
                out_ref[r * block : top, wide_lanes(pair)] = jnp.concatenate(
                    parts, axis=1
                ).astype(BF16)

    return stage(
        body,
        [
            ((count, model), BF16),
            ((count, 3 * space), BF16),
            ((count, 3 * width), BF16),
            ((count, width), BF16),
        ],
        (rows, gain, down, ups, weight, across, below, owner),
    )


def after_attention(attended, attend_t, out_t, ups, spot, rows, gain, owner):
    local, model = rows.shape

    def body(
        attended_ref, attend_ref, out_ref, ups_ref, rows_ref, gain_ref, owner_ref,
        middle_ref, normed_ref, short_ref,
    ):
        low = masked(mt(attended_ref[...], attend_ref[...]), owner_ref[...])
        middle = (
            rows_ref[...].astype(F32)
            + mt(attended_ref[...], out_ref[...])
            + mm(low, ups_ref[:, spot])
        )
        middle_ref[...] = middle
        normed_ref[...] = rms_forward(middle, gain_ref[...]).astype(BF16)
        short_ref[...] = shorten(low)

    return stage(
        body,
        [((local, model), F32), ((local, model), BF16), ((RANK, local), BF16)],
        (attended, attend_t, out_t, ups, rows, gain, owner),
    )


def ask_memory(normed, down, query, gate, ups, query_spot, gate_spot, owner, keys, picks, block=128):
    count = normed.shape[0]
    half = keys.shape[2]
    number = picks.shape[2]
    width = gate.shape[1]
    space = NAD * RANK
    scale = (2 * half) ** -0.5

    def body(
        normed_ref, down_ref, query_ref, gate_ref, ups_ref, owner_ref, keys_ref, picks_ref,
        low_ref, gate_pre_ref, weights_ref, narrow_ref, asked, every,
    ):
        rank = lax.axis_index(TP)

        @pl.loop(0, count // block)
        def _(c):
            at = pl.ds(pl.multiple_of(c * block, block), block)
            rows = normed_ref[at, :]
            low = masked(mm(rows, down_ref[...]), owner_ref[at, :])
            low_ref[at, :] = low
            asked[at, :] = mm(rows, query_ref[...]) + mm(low[:, :space], ups_ref[:, query_spot])
            gate_pre_ref[at, :] = mm(rows, gate_ref[...]) + mm(
                low[:, space:], ups_ref[:, gate_spot]
            )

        slot = lax.broadcasted_iota(I32, (NKEYS, block), 0)
        for part in range(2):
            top, rest = two_parts(asked[:, part * half : (part + 1) * half])
            every[...] = mt(keys_ref[part], top) + mt(keys_ref[part], rest)

            @pl.loop(0, count // block)
            def _(c):
                lanes = pl.ds(pl.multiple_of(c * block, block), block)
                scores = every[:, lanes]
                rows = []
                for k in range(number):
                    hit = slot == picks_ref[rank, part, k : k + 1, lanes]
                    rows.append(jnp.sum(jnp.where(hit, scores, 0.0), axis=0, keepdims=True))
                found = jnp.concatenate(rows, axis=0)
                if part == 0:
                    weights_ref[:, lanes] = found
                else:
                    total = (weights_ref[:, lanes] + found) * scale
                    raised = jnp.exp(total - jnp.max(total, axis=0, keepdims=True))
                    weights = raised / jnp.sum(raised, axis=0, keepdims=True)
                    weights_ref[:, lanes] = weights
                    narrow_ref[:, lanes] = weights.astype(BF16)

    return stage(
        body,
        [
            ((count, 2 * space), BF16),
            ((count, width), F32),
            ((number, count), F32),
            ((number, count), BF16),
        ],
        (normed, down, query, gate, ups, owner, keys, picks),
        [pltpu.VMEM((count, 2 * half), F32), pltpu.VMEM((NKEYS, count), F32)],
    )


def mixed_upstream(rows, mixed_t, ups, up_spot, low_spot, owner, block=128):
    count = rows.shape[0]
    width = mixed_t.shape[1]

    def body(rows_ref, mixed_ref, ups_ref, owner_ref, low_ref, out_ref):
        @pl.loop(0, count // block)
        def _(c):
            at = pl.ds(pl.multiple_of(c * block, block), block)
            low = masked(mt(rows_ref[at, :], ups_ref[:, up_spot]), owner_ref[at, :])
            low_ref[at, :] = low
            out_ref[at, :] = mm(rows_ref[at, :], mixed_ref[...]) + mm(low, ups_ref[:, low_spot])

    return stage(
        body,
        [((count, NAD * RANK), BF16), ((count, width), F32)],
        (rows, mixed_t, ups, owner),
    )


def memory_back(
    weights, pieces, keys, picks, query, gate, grad_gate, mixed, ups, spots, owner, block=128
):
    query_spot, gate_spot, low_spot = spots
    number, count = weights.shape
    half = keys.shape[2]
    scale = (2 * half) ** -0.5
    model = query.shape[0]

    def body(
        weights_ref, pieces_ref, keys_ref, picks_ref, query_ref, gate_ref, grad_gate_ref,
        mixed_ref, ups_ref, owner_ref, grad_query_ref, partial_ref, three_ref, four_ref, dense,
    ):
        rank = lax.axis_index(TP)
        slot = lax.broadcasted_iota(I32, (NKEYS, block), 0)
        for part in range(2):

            @pl.loop(0, count // block)
            def _(c):
                lanes = pl.ds(pl.multiple_of(c * block, block), block)
                weight = weights_ref[:, lanes]
                grad = sum(pieces_ref[p, :, lanes].astype(F32) for p in range(pieces.shape[0]))
                grad = weight * (grad - jnp.sum(grad * weight, axis=0, keepdims=True)) * scale
                total = jnp.zeros((NKEYS, block), F32)
                for k in range(number):
                    hit = slot == picks_ref[rank, part, k : k + 1, lanes]
                    total += jnp.where(hit, grad[k : k + 1, :], 0.0)
                dense[:, lanes] = total

            top, rest = two_parts(dense[...])
            grad_query_ref[:, part * half : (part + 1) * half] = (
                tm(top, keys_ref[part]) + tm(rest, keys_ref[part])
            ).astype(BF16)

        @pl.loop(0, count // block)
        def _(c):
            at = pl.ds(pl.multiple_of(c * block, block), block)
            asked, gates, own = grad_query_ref[at, :], grad_gate_ref[at, :], owner_ref[at, :]
            partial_ref[at, :] = (mt(asked, query_ref[...]) + mt(gates, gate_ref[...])).astype(BF16)
            three = jnp.concatenate(
                [mt(asked, ups_ref[:, query_spot]), mt(gates, ups_ref[:, gate_spot])], axis=1
            )
            three_ref[:, at] = shorten(masked(three, own))
            four_ref[:, at] = shorten(masked(mt(mixed_ref[at, :], ups_ref[:, low_spot]), own))

    return stage(
        body,
        [
            ((count, 2 * half), BF16),
            ((count, model), BF16),
            ((2 * RANK, count), BF16),
            ((RANK, count), BF16),
        ],
        (weights, pieces, keys, picks, query, gate, grad_gate, mixed, ups, owner),
        [pltpu.VMEM((NKEYS, count), F32)],
    )


def residual_back(
    pieces, three, four, middle, cotangent, gain, down_memory, ups, spots, out_t, attend_t, owner,
    mixed_parts,
):
    attend_spot, mixed_spot = spots
    local, model = middle.shape
    count = three.shape[2]

    def body(
        pieces_ref, three_ref, four_ref, middle_ref, cotangent_ref, gain_ref, down_ref, ups_ref,
        out_ref, attend_ref, owner_ref, *refs
    ):
        mixed_refs = refs[: len(mixed_parts)]
        middle_grad_ref, branch_ref, attended_ref, short_ref, three_sum_ref, four_sum_ref, added_ref = (
            refs[len(mixed_parts) :]
        )
        own = pl.ds(pl.multiple_of(lax.axis_index(TP) * local, local), local)
        owner = owner_ref[...]

        def total(ref):
            return sum(ref[p].astype(F32) for p in range(ref.shape[0]))

        three_sum_ref[...] = total(three_ref).astype(BF16)
        four_sum_ref[...] = total(four_ref).astype(BF16)
        low_four = lengthen(four_sum_ref[:, own], owner)
        added_ref[...] = (
            middle_ref[...]
            + sum(ref[...].astype(F32) for ref in mixed_refs)
            + mm(low_four, ups_ref[:, mixed_spot])
        ).astype(BF16)
        grad_three = lengthen(three_sum_ref[:, own], owner)
        upstream = total(pieces_ref) + mt(grad_three, down_ref[...])
        grad = cotangent_ref[...].astype(F32) + rms_backward(
            middle_ref[...], gain_ref[...], upstream
        )
        middle_grad_ref[...] = grad
        branch = grad.astype(BF16)
        branch_ref[...] = branch
        low = masked(mt(branch, ups_ref[:, attend_spot]), owner)
        attended_ref[...] = (mm(branch, out_ref[...]) + mm(low, attend_ref[...])).astype(BF16)
        short_ref[...] = shorten(low)

    return stage(
        body,
        [
            ((local, model), F32),
            ((local, model), BF16),
            ((local, model), BF16),
            ((RANK, local), BF16),
            ((2 * RANK, count), BF16),
            ((RANK, count), BF16),
            ((local, model), BF16),
        ],
        (
            pieces, three, four, middle, cotangent, gain, down_memory, ups, out_t, attend_t, owner,
            *mixed_parts,
        ),
    )


def attend_back(projected, upstream, across, below, weight, ups, owner, block=128):
    count = projected.shape[0]
    width = weight.shape[1] // 3
    model = weight.shape[0]

    def body(
        projected_ref, upstream_ref, across_ref, below_ref, weight_ref, ups_ref, owner_ref,
        grads_ref, partial_ref, short_ref, key_sum, value_sum,
    ):
        @pl.loop(0, width // (2 * HD))
        def _(pair):
            queries, keys, values = [projected_ref[:, wide_lanes(pair, p * width)] for p in range(3)]
            above = upstream_ref[:, wide_lanes(pair)]
            key_sum[...] = jnp.zeros_like(key_sum)
            value_sum[...] = jnp.zeros_like(value_sum)
            for r in range(count // block):
                at, top = slice(r * block, (r + 1) * block), (r + 1) * block
                parts = []
                for h in range(2):
                    lanes = slice(h * HD, (h + 1) * HD)
                    probs = block_probs(
                        queries[:, lanes], keys[:, lanes], across_ref, below_ref, r, block
                    )
                    grad_probs = mt(above[at, lanes], values[:top, lanes])
                    inner = jnp.sum(probs * grad_probs, axis=-1, keepdims=True)
                    grad_scores = (probs * (grad_probs - inner)).astype(BF16)
                    parts.append(mm(grad_scores, keys[:top, lanes]))
                    key_sum[h, :top, :] += tm(grad_scores, queries[at, lanes])
                    value_sum[h, :top, :] += tm(probs.astype(BF16), above[at, lanes])
                grads_ref[at, wide_lanes(pair)] = (
                    jnp.concatenate(parts, axis=1) * HD**-0.5
                ).astype(BF16)
            grads_ref[:, wide_lanes(pair, width)] = (
                jnp.concatenate([key_sum[0], key_sum[1]], axis=1) * HD**-0.5
            ).astype(BF16)
            grads_ref[:, wide_lanes(pair, 2 * width)] = jnp.concatenate(
                [value_sum[0], value_sum[1]], axis=1
            ).astype(BF16)

        @pl.loop(0, count // block)
        def _(c):
            at = pl.ds(pl.multiple_of(c * block, block), block)
            partial_ref[at, :] = mt(grads_ref[at, :], weight_ref[...]).astype(BF16)
            one = jnp.concatenate(
                [
                    mt(
                        grads_ref[at, p * width : (p + 1) * width],
                        ups_ref[:, p * width : (p + 1) * width],
                    )
                    for p in range(3)
                ],
                axis=1,
            )
            short_ref[:, at] = shorten(masked(one, owner_ref[at, :]))

    return stage(
        body,
        [((count, 3 * width), BF16), ((count, model), BF16), ((3 * RANK, count), BF16)],
        (projected, upstream, across, below, weight, ups, owner),
        [pltpu.VMEM((2, count, HD), F32)] * 2,
    )


def input_back(pieces, one, grad_middle, rows, gain, down, owner):
    local, model = rows.shape
    count = one.shape[2]

    def body(
        pieces_ref, one_ref, middle_ref, rows_ref, gain_ref, down_ref, owner_ref, out_ref, sum_ref
    ):
        own = pl.ds(pl.multiple_of(lax.axis_index(TP) * local, local), local)

        def total(ref):
            return sum(ref[p].astype(F32) for p in range(ref.shape[0]))

        sum_ref[...] = total(one_ref).astype(BF16)
        low = lengthen(sum_ref[:, own], owner_ref[...])
        upstream = total(pieces_ref) + mt(low, down_ref[...])
        out_ref[...] = middle_ref[...] + rms_backward(
            rows_ref[...].astype(F32), gain_ref[...], upstream
        )

    return stage(
        body,
        [((local, model), F32), ((3 * RANK, count), BF16)],
        (pieces, one, grad_middle, rows, gain, down, owner),
    )


def own_columns(short, owner, first):
    high, count = short.shape
    adapters = NAD // lax.axis_size(TP)
    pattern = lax.broadcasted_iota(I32, (high, adapters * high), 0) == lax.rem(
        lax.broadcasted_iota(I32, (high, adapters * high), 1), high
    )
    spread = tm(short, jnp.where(pattern, 1.0, 0.0).astype(BF16))
    adapter = lax.div(lax.broadcasted_iota(I32, (count, adapters * high), 1), high) + first
    return jnp.where(adapter == owner, spread, 0.0).astype(BF16)


def adapter_grads(
    low_one, grad_projected, low_three, grad_query, grad_gate, two_short, branch, four_short,
    cotangent, two_back, attended, grad_low_four, mixed, normed_one, one_short, normed_two,
    three_short, owner,
):
    count, width = attended.shape
    model = normed_one.shape[1]
    space = NAD * RANK
    cut = NAD // lax.axis_size(TP) * RANK
    asked = grad_query.shape[1]

    def body(
        low_one_ref, projected_ref, low_three_ref, query_ref, gate_ref, two_ref, branch_ref,
        four_ref, cotangent_ref, back_ref, attended_ref, low_four_ref, mixed_ref, one_rows_ref,
        one_ref, two_rows_ref, three_ref, owner_ref, ups_ref, downs_ref,
    ):
        owner = owner_ref[...]
        rank = lax.axis_index(TP)
        at = 0

        def put(low, rows):
            nonlocal at
            ups_ref[:, at : at + rows.shape[1]] = tm(low, rows).astype(BF16)
            at += rows.shape[1]

        for p in range(3):
            put(
                low_one_ref[:, p * space : (p + 1) * space],
                projected_ref[:, p * width : (p + 1) * width],
            )
        put(low_three_ref[:, :space], query_ref[...])
        put(low_three_ref[:, space:], gate_ref[...])
        put(lengthen(side_by_side(two_ref), owner), branch_ref[...])
        own = pl.ds(pl.multiple_of(rank * width, width), width)
        put(lengthen(four_ref[...], owner), cotangent_ref[:, own])
        put(lengthen(side_by_side(back_ref), owner), attended_ref[...])
        put(low_four_ref[...], mixed_ref[...])
        first = rank * (NAD // lax.axis_size(TP))
        one = own_columns(one_ref[...], owner, first)
        three = own_columns(three_ref[...], owner, first)

        @pl.loop(0, model // width)
        def _(c):
            lanes = pl.ds(pl.multiple_of(c * width, width), width)
            downs_ref[lanes, : 3 * cut] = tm(one_rows_ref[:, lanes], one).astype(BF16)
            downs_ref[lanes, 3 * cut :] = tm(two_rows_ref[:, lanes], three).astype(BF16)

    return stage(
        body,
        [((space, 7 * width + 2 * width + asked - width), BF16), ((model, 5 * cut), BF16)],
        (
            low_one, grad_projected, low_three, grad_query, grad_gate, two_short, branch,
            four_short, cotangent, two_back, attended, grad_low_four, mixed, normed_one,
            one_short, normed_two, three_short, owner,
        ),
    )


def spread_picks(first, second, weights, sub=32, conv=32):
    tokens, picks = first.shape
    stride = sub + 1

    def body(first_ref, second_ref, weights_ref, out_ref, low, high):
        slot = lax.broadcasted_iota(I32, (NKEYS, picks), 0)
        for n in range(sub):
            b = jnp.where(slot == second_ref[n : n + 1, :], 1.0, 0.0).astype(BF16)
            a = jnp.where(slot == first_ref[n : n + 1, :], weights_ref[n : n + 1, :], 0.0)
            both = mt(a.astype(BF16), b)
            low[pl.ds(n, NKEYS, stride=stride), :] = both[:, :128]
            high[pl.ds(n, NKEYS, stride=stride), :] = both[:, 128:]

        @pl.loop(0, NKEYS // conv)
        def _(c):
            for q in range(conv):
                i = c * conv + q
                at = pl.multiple_of(i * NKEYS, NKEYS)
                rows = pl.ds(i * stride, sub)
                out_ref[:, pl.ds(at, 128)] = low[rows, :].astype(BF16)
                out_ref[:, pl.ds(at + 128, 128)] = high[rows, :].astype(BF16)

    line = pl.BlockSpec((sub, picks), lambda t: (t, 0))
    rows = NKEYS * NKEYS
    return pl.pallas_call(
        body,
        grid=(tokens // sub,),
        out_shape=jax.ShapeDtypeStruct((tokens, rows), BF16),
        in_specs=[line] * 3,
        out_specs=pl.BlockSpec((sub, rows), lambda t: (t, 0)),
        scratch_shapes=[pltpu.VMEM((NKEYS * stride, 128), F32)] * 2,
        compiler_params=pltpu.CompilerParams(vmem_limit_bytes=40 << 20),
    )(first, second, weights)


def recall(dense, table, part, parts, before, after):
    tokens, rows = dense.shape
    width = table.shape[2]
    groups, block = table.shape[0], table.shape[1]
    last = part == parts - 1

    def body(*refs):
        dense_ref, table_ref = refs[:2]
        step = pl.program_id(0)
        total = refs[-1]

        @pl.when(step == 0)
        def _():
            total[...] = refs[2][...] if part else jnp.zeros_like(total)

        total[...] += mm(dense_ref[...], table_ref[...])
        if not last:
            return

        @pl.when(step == groups - 1)
        def _():
            gate_ref, upstream_ref, norms_ref = refs[-8:-5]
            mixed_ref, grad_ref, grad_gate_ref, scale_ref = refs[-5:-1]
            gate, recalled, upstream = gate_ref[...], total[...], upstream_ref[...]
            sigmoid = 1.0 / (1.0 + jnp.exp(-gate))
            act = gate * sigmoid
            mixed_ref[...] = (act * recalled).astype(BF16)
            grad = (upstream * act).astype(BF16)
            grad_ref[...] = grad
            grad_gate_ref[...] = (
                upstream * recalled * sigmoid * (1.0 + gate * (1.0 - sigmoid))
            ).astype(BF16)
            wide = grad.astype(F32)
            bound = jnp.max(norms_ref[...]) * jnp.sum(wide * wide, axis=1, keepdims=True)
            scale_ref[...] = 32000.0 * lax.rsqrt(jnp.maximum(bound, 1e-30))

    one = (tokens, width)
    outs = [(one, BF16)] * 3 + [((tokens, 1), F32)] if last else [(one, F32)]
    more = ([before] if part else []) + (list(after) if last else [])
    return pl.pallas_call(
        body,
        grid=(groups,),
        out_shape=[jax.ShapeDtypeStruct(shape, dtype) for shape, dtype in outs],
        in_specs=[
            pl.BlockSpec((tokens, block), lambda s: (0, s * parts + part)),
            pl.BlockSpec((None, block, width), lambda s: (s, 0, 0)),
        ]
        + [whole(x.shape) for x in more],
        out_specs=[whole(shape) for shape, _ in outs],
        scratch_shapes=[pltpu.VMEM(one, F32)] if last else [],
        compiler_params=pltpu.CompilerParams(vmem_limit_bytes=40 << 20),
    )(dense, table, *more)


def pick_grads(first, second, grads, scale, table, part, parts, before):
    tokens, picks = first.shape
    width = grads.shape[1]
    groups, rows = table.shape[0], table.shape[1]
    per_block = rows // NKEYS
    last = part == parts - 1

    def body(first_ref, second_ref, grads_ref, scale_ref, table_ref, *refs):
        step = pl.program_id(0)
        out_ref, kept = refs[-2], refs[-1]

        @pl.when(step == 0)
        def _():
            kept[...] = refs[0][...] if part else jnp.zeros_like(kept)

        own = first_ref[...]
        low = second_ref[...] & 127
        factor = jnp.broadcast_to(scale_ref[...], (tokens, 128))
        total = kept[...]
        for b in range(per_block):
            every = mt(grads_ref[...], table_ref[b * NKEYS : (b + 1) * NKEYS, :])
            packed = (every[:, 128:] * factor).astype(I32) * 65536 + (
                every[:, :128] * factor
            ).astype(I32)
            found = jnp.take_along_axis(packed, low, axis=1, mode="promise_in_bounds")
            total = jnp.where(own == (step * parts + part) * per_block + b, found, total)
        kept[...] = total

        @pl.when(step == groups - 1)
        def _():
            p = kept[...]
            if not last:
                out_ref[...] = p
                return
            right = lax.shift_right_arithmetic(lax.shift_left(p, 16), 16)
            left = lax.shift_right_arithmetic(p - right, 16)
            both = jnp.where(second_ref[...] >= 128, left, right).astype(F32) / factor
            out_ref[...] = both.T.astype(BF16)

    shape, dtype = ((picks, tokens), BF16) if last else ((tokens, picks), I32)
    more = [before] if part else []
    return pl.pallas_call(
        body,
        grid=(groups,),
        out_shape=jax.ShapeDtypeStruct(shape, dtype),
        in_specs=[whole(x.shape) for x in (first, second, grads, scale)]
        + [pl.BlockSpec((None, rows, width), lambda s: (s, 0, 0))]
        + [whole(x.shape) for x in more],
        out_specs=whole(shape),
        scratch_shapes=[pltpu.VMEM((tokens, picks), I32)],
        compiler_params=pltpu.CompilerParams(vmem_limit_bytes=48 << 20),
    )(first, second, grads, scale, table, *more)


def add_up(up_parts, down_parts, sizes, cut):
    high, tall, wide = up_parts.shape[1], down_parts.shape[1], down_parts.shape[2]

    def body(ups_ref, downs_ref, *out_refs):
        def total(ref, lanes):
            return sum(ref[p, :, lanes].astype(F32) for p in range(ref.shape[0]))

        at = 0
        for size, ref in zip(sizes, out_refs):
            ref[...] = total(ups_ref, slice(at, at + size))
            at += size
        out_refs[-2][...] = total(downs_ref, slice(0, cut))
        out_refs[-1][...] = total(downs_ref, slice(cut, wide))

    return stage(
        body,
        [((high, size), F32) for size in sizes] + [((tall, cut), F32), ((tall, wide - cut), F32)],
        (up_parts, down_parts),
    )


def make_ready(down_input, down_memory, turned, joined):
    def body(input_ref, memory_ref, *refs):
        ins, outs = refs[: len(turned) + len(joined)], refs[len(turned) + len(joined) :]

        def ordered(ref, parts):
            size = NAD * parts * RANK
            row = lax.broadcasted_iota(I32, (size, size), 0)
            column = lax.broadcasted_iota(I32, (size, size), 1)
            part, rest = lax.div(column, NAD * RANK), lax.rem(column, NAD * RANK)
            adapter, rank = lax.div(rest, RANK), lax.rem(rest, RANK)
            came = adapter * (parts * RANK) + part * RANK + rank
            return mm(ref[...], jnp.where(row == came, 1.0, 0.0).astype(BF16)).astype(BF16)

        outs[0][...] = ordered(input_ref, 3)
        outs[1][...] = ordered(memory_ref, 2)
        at = 0
        for ref in ins[len(turned) :]:
            outs[2][:, at : at + ref.shape[1]] = ref[...]
            at += ref.shape[1]
        for ref, out in zip(ins[: len(turned) - 1], outs[3:]):
            out[...] = ref[...].astype(F32).T.astype(BF16)
        outs[2][:, at:] = ins[len(turned) - 1][...].astype(F32).T.astype(BF16)

    small = sum(x.shape[1] for x in joined) + turned[-1].shape[0]
    return stage(
        body,
        [
            (down_input.shape, BF16),
            (down_memory.shape, BF16),
            ((joined[0].shape[0], small), BF16),
        ]
        + [(x.shape[::-1], BF16) for x in turned[:-1]],
        (down_input, down_memory, *turned, *joined),
    )


def by_part(down, parts):
    shaped = down.reshape(down.shape[0], NAD, parts, RANK).transpose(0, 2, 1, 3)
    return shaped.reshape(down.shape)


def on_device(
    inputs,
    cotangent,
    norm_attend,
    norm_memory,
    project_in,
    project_out,
    query_weight,
    gate_weight,
    memory_out,
    half_keys,
    value_table,
    key_picks,
    segment_ids,
    adapter_ids,
    down_input,
    up_input,
    down_attend,
    up_attend,
    down_memory,
    up_query,
    up_gate,
    down_mixed,
    up_mixed,
):
    groups = lax.axis_size(DP)
    ranks = lax.axis_size(TP)
    rank = lax.axis_index(TP)
    local = inputs.shape[0]
    count = segment_ids.shape[0]
    width = project_in.shape[2]
    model = inputs.shape[1]
    own_adapters = NAD // ranks

    flat_in = project_in.reshape(project_in.shape[0], 3 * width)
    joined = (up_input.reshape(up_input.shape[0], 3 * width), up_query, up_gate, up_attend, up_mixed)
    turned = (project_out, memory_out, down_attend, down_mixed)
    if project_out.shape[1] % 128 == 0:
        parted_input, parted_memory, small, out_turned, mixed_turned, attend_turned = make_ready(
            down_input, down_memory, turned, joined
        )
    else:
        parted_input, parted_memory = by_part(down_input, 3), by_part(down_memory, 2)
        out_turned, mixed_turned, attend_turned, low_turned = [x.T for x in turned]
        small = jnp.concatenate(joined + (low_turned,), axis=1)
    share = value_table.shape[0] // PARTS
    tables = [
        lax.all_gather(value_table[p * share : (p + 1) * share], DP, axis=0) for p in range(PARTS)
    ]
    got = exchange(
        [(inputs, SHARE, TP), (cotangent, SHARE, TP)]
        + [(x, TREE, DP) for x in (flat_in, parted_input, small)]
        + [(out_turned, NEST, DP), (attend_turned, NEST, DP)],
        1,
    )
    input_rows = got[0].reshape(count, model)
    cotangent_rows = got[1].reshape(count, model)
    full_in, full_down_input, ups, out_t, attend_t = [x.reshape(-1, x.shape[2]) for x in got[2:]]
    spots, at = [], 0
    for size in (3 * width, up_query.shape[1], width, model, model, width):
        spots.append(slice(at, at + size))
        at += size
    _, query_spot, gate_spot, attend_spot, mixed_spot, low_spot = spots

    owner = jnp.zeros((count,), I32)
    for s in range(adapter_ids.shape[1]):
        owner = jnp.where(segment_ids == s, adapter_ids[0, s], owner)
    owner = owner[:, None]
    owner_own = lax.dynamic_slice_in_dim(owner, rank * local, local, 0)
    across, below = segment_ids[None, :], segment_ids[:, None]
    gain_one = norm_attend.astype(F32)[None, :]
    gain_two = norm_memory.astype(F32)[None, :]
    first_picks = key_picks[:, 0].reshape(-1, count).T
    second_picks = key_picks[:, 1].reshape(-1, count).T
    keys = half_keys[0]

    normed_one, low_one, projected, attended = project_and_attend(
        input_rows, gain_one, full_down_input, ups, full_in, across, below, owner
    )
    (attended_own,) = exchange([(attended.reshape(ranks, local, width), SIDE, TP)], 2)
    middle, normed_two, two_short = after_attention(
        attended_own, attend_t, out_t, ups, attend_spot, inputs, gain_two, owner_own
    )
    largest = jnp.max(jnp.sum(jnp.square(value_table.astype(F32)), axis=1))
    got = exchange(
        [
            (normed_two, SHARE, TP),
            (two_short, SHARE, TP),
            (jnp.broadcast_to(largest, (8, 128)), SHARE, DP),
        ]
        + [(x, TREE, DP) for x in (query_weight, gate_weight, parted_memory, mixed_turned)],
        3,
    )
    normed_rows, two_short, norms = got[0].reshape(count, model), got[1], got[2]
    full_query, full_gate, full_down_memory, mixed_t = [x.reshape(-1, x.shape[2]) for x in got[3:]]
    low_three, gate_pre, weights, narrow = ask_memory(
        normed_rows,
        full_down_memory,
        full_query,
        full_gate,
        ups,
        query_spot,
        gate_spot,
        owner,
        keys,
        key_picks,
    )
    (all_weights,) = exchange([(narrow, SHARE, TP)], 4)
    by_token = all_weights.reshape(-1, count).astype(F32).T
    dense = spread_picks(first_picks, second_picks, by_token)
    grad_low_four, grad_mixed = mixed_upstream(
        cotangent_rows, mixed_t, ups, mixed_spot, low_spot, owner
    )
    recalled = None
    for part in range(PARTS):
        recalled = recall(
            dense, tables[part], part, PARTS, recalled, (gate_pre, grad_mixed, norms)
        )
        if part < PARTS - 1:
            (recalled,) = recalled
    mixed, grad_recalled, grad_gate, scale = recalled
    partial_mixed = mt(mixed, mixed_t).astype(BF16).reshape(ranks, local, model)

    def block_of(blocks, d):
        return lax.dynamic_index_in_dim(blocks, lax.rem(rank + d, ranks), 0, keepdims=False)

    def turn(d):
        return [(p, (p + d) % ranks) for p in range(ranks)]

    mixed_parts = [block_of(partial_mixed, 0)] + [
        lax.ppermute(block_of(partial_mixed, d), TP, turn(d)) for d in range(1, ranks)
    ]
    picked = None
    for part in range(PARTS):
        picked = pick_grads(
            first_picks, second_picks, grad_recalled, scale, tables[part], part, PARTS, picked
        )
    picked, mixed_parts = lax.optimization_barrier((picked, mixed_parts))
    (pick_pieces,) = exchange([(picked.reshape(ranks, -1, count), PIECE, TP)], 5)
    grad_query, partial_normed, three_short, four_short = memory_back(
        weights,
        pick_pieces,
        keys,
        key_picks,
        full_query,
        full_gate,
        grad_gate,
        mixed,
        ups,
        (query_spot, gate_spot, low_spot),
        owner,
    )
    normed_pieces, three_short, four_short = exchange(
        [
            (partial_normed.reshape(ranks, local, model), PIECE, TP),
            (three_short, SHARE, TP),
            (four_short, SHARE, TP),
        ],
        6,
    )
    grad_middle, grad_branch, grad_attended, two_back, three_short, four_short, outputs = (
        residual_back(
            normed_pieces,
            three_short,
            four_short,
            middle,
            cotangent,
            gain_two,
            full_down_memory,
            ups,
            (attend_spot, mixed_spot),
            out_t,
            attend_t,
            owner_own,
            mixed_parts,
        )
    )
    grad_attended, two_back = exchange([(grad_attended, SPLIT, TP), (two_back, SHARE, TP)], 7)
    grad_projected, partial_input, one_short = attend_back(
        projected, grad_attended.reshape(count, width), across, below, full_in, ups, owner
    )
    input_pieces, one_short, own_branch = exchange(
        [
            (partial_input.reshape(ranks, local, model), PIECE, TP),
            (one_short, SHARE, TP),
            (grad_branch, SPLIT, TP),
        ],
        8,
    )
    input_grad, one_short = input_back(
        input_pieces, one_short, grad_middle, inputs, gain_one, full_down_input, owner_own
    )
    up_sent, down_sent = adapter_grads(
        low_one,
        grad_projected,
        low_three,
        grad_query,
        grad_gate,
        two_short,
        own_branch.reshape(count, width),
        four_short,
        cotangent_rows,
        two_back,
        attended,
        grad_low_four,
        mixed,
        normed_one,
        one_short,
        normed_rows,
        three_short,
        owner,
    )
    up_parts, down_parts = exchange(
        [
            (up_sent.reshape(groups, -1, up_sent.shape[1]), PIECE, DP),
            (down_sent.reshape(groups, -1, down_sent.shape[1]), PIECE, DP),
        ],
        9,
    )
    parts = add_up(
        up_parts,
        down_parts,
        (3 * width, up_query.shape[1], width, width, width, width, width),
        own_adapters * 3 * RANK,
    )
    return (
        outputs,
        input_grad,
        parts[7],
        parts[0].reshape(up_input.shape),
        parts[5].T,
        parts[3],
        parts[8],
        parts[1],
        parts[2],
        parts[6].T,
        parts[4],
    )


def solution(mesh):
    rows = P((DP, TP), None)
    both = P(DP, TP)
    wide = P(DP, None)
    turned = P(TP, DP)
    split = P(DP, None, TP)
    return jax.shard_map(
        on_device,
        mesh=mesh,
        in_specs=(
            rows,
            rows,
            P(),
            P(),
            split,
            turned,
            both,
            both,
            turned,
            P(TP, None, None, None),
            both,
            P(None, None, None, DP),
            P(DP),
            wide,
            wide,
            split,
            turned,
            wide,
            wide,
            both,
            both,
            turned,
            wide,
        ),
        out_specs=(rows, rows, both, split, turned, both, both, both, both, turned, both),
        check_vma=False,
    )
```

time: 591 us -> 449 us (0.76); the launches traced: 583 us -> 448 us
  matrix products: 55.9 us -> 0.47 us
  Pallas kernels: 456 us -> 406 us
  other arithmetic: 32.1 us -> 8 us
  local copies, waits for them, and re-layouts: 22.1 us -> 14.6 us
    pallas_call x9, Pallas kernels: 308 us -> 208 us  [exchange(): pl.pallas_call(body, out_shape=shapes, in_specs=[ANY] * n, out_specs=[ANY...]
    pallas_call x6 -> x13, Pallas kernels: 113 us -> 164 us  [the longest x11 80.1 us: stage(): pl.pallas_call(body, grid=(1,), out_shape=[jax.ShapeDtypeStruct(shape, dt...]
    dot_general x32 -> x0, matrix products: 32.2 us -> none  [the longest x21 22.7 us: mm(): lax.dot_general(a, b, (((1,), (0,)), ((), ())), preferred_element_type=F32)]
    dot_general x16 -> x1, matrix products: 23.7 us -> 0.47 us  [mt(): lax.dot_general(a, b, (((1,), (1,)), ((), ())), preferred_element_type=F32)]
    reduce_sum x11 -> x0, other arithmetic: 10.9 us -> none  [the longest x1 1.5 us: rms_forward(): factor = lax.rsqrt(jnp.mean(values * values, axis=-1, keepdims=True) + EPS)]
    convert_element_type x8 -> x0, other arithmetic: 7.84 us -> none  [the longest x2 4.15 us: on_device(): normed_one = rms_forward(input_rows.astype(F32), gain_one).astype(BF16)]
  transfers between devices with their start and end apart: 1 -> 4, of which waited for: 0 -> 0; matrix products, arithmetic and copies ran while one was open for 8% -> 4% of each run, Pallas kernels for 36% -> 52%
where the time goes in v1:
time: 449 us; the launch traced here: 448 us
  Pallas kernels  406 us (90%)
  local copies, waits for them, and re-layouts  14.6 us (3%)
  between operations  14.4 us (3%)
  other arithmetic  8 us (2%)
    pallas_call x9, Pallas kernels, exchange(): pl.pallas_call(body, out_shape=shapes, in_specs=[ANY] * n, out_specs=[ANY...  208 us
    pallas_call x11, Pallas kernels, stage(): pl.pallas_call(body, grid=(1,), out_shape=[jax.ShapeDtypeStruct(shape, dt...  80.1 us
    pallas_call x1, Pallas kernels, pick_grads(): pl.pallas_call(body, grid=(groups,), out_shape=jax.ShapeDtypeStruct(shape...  50.9 us
    pallas_call x1, Pallas kernels, spread_picks(): pl.pallas_call(body, grid=(tokens // sub,), out_shape=jax.ShapeDtypeStruc...  34.3 us
    pallas_call x1, Pallas kernels, recall(): pl.pallas_call(body, grid=(groups,), out_shape=[jax.ShapeDtypeStruct(shap...  33.3 us
  transfers between devices with their start and end apart: 4, of which 0 were waited for; matrix products, arithmetic and copies ran while one was open for 4% of the time, Pallas kernels for 52%

profile of v1, /device:TPU:9, one launch (start us, length us, event | category | flops | bytes accessed | tf_op | source)
XLA Modules:
  0.0 448.4 jit_solution(14410062711371078050)
XLA Ops:
  7.3 0.7 all-gather.3.cloned.1.call-update
  8.0 0.7 copy.49.refs_2_
  8.7 0.7 copy.50.refs_3_
  9.5 0.6 copy.74
  10.3 0.8 copy.51.refs_2_
  11.1 0.6 fusion.1
  11.7 1.9 select_select_fusion
  13.6 0.9 copy.53.owner_ref
  14.5 0.9 copy.52.below_ref
  15.4 0.6 broadcast_in_dim.43
  16.0 2.1 shard_map.302
  18.1 67.7 %shard_map.303 = (bf16[4,128,1024]{2,1,0:T(8,128)(2,1)}, bf16[4,128,1024]{2,1,0:T(8,128)(2,1)}, bf16[8,128,768]{2,1,0:T(8,128)(2,1)}, bf16[8,128,384]{2,1,0:T(8,...) custom-call(bf16[128,1024]{1,0:T(8,128)(2,1)} %rows_ref.3, ...), custom_call_target="tpu_custom_call" | custom-call | tf_op jit(solution)/shard_map/pallas_call | solution.py:241
  85.8 12.6 %shard_map.304 = (bf16[512,1024]{1,0:T(8,128)(2,1)}, bf16[512,384]{1,0:T(8,128)(2,1)}, bf16[512,768]{1,0:T(8,128)(2,1)}, bf16[512,256]{1,0:T(8,128)(2,1)}) custom-call(bf16[512,1024]{1,0:T(8,128)(2,1)} %bitcast.107, f32[1,1024]{1,0:T(1,128)} %bitcast.118, bf16[1024,384]{1,0:T(8,128)(2,1)} %bitcast.90, bf16[128,3840]{1,0:T(8,128)(2,1)} %bitcast.72, ...), custom_call_target="tpu_custom_call" | custom-call | tf_op jit(solution)/shard_map/pallas_call | solution.py:259
  98.5 8.3 %shard_map.305.attended_ref = bf16[128,1024]{1,0:T(8,128)(2,1)} custom-call(bf16[4,128,256]{2,1,0:T(8,128)(2,1)} %bitcast.102), custom_call_target="tpu_custom_call" | custom-call | tf_op jit(solution)/shard_map/pallas_call | solution.py:241
  106.8 0.7 copy.54.owner_ref
  107.5 0.6 broadcast_in_dim.44
  108.1 3.3 multiply_reduce_fusion
  111.5 0.6 reduce_max.9
  112.1 3.9 shard_map.306
  116.0 1.3 broadcast_in_dim.42.refs_2_
  117.3 31.1 %shard_map.307 = (bf16[4,128,1024]{2,1,0:T(8,128)(2,1)}, bf16[4,16,128]{2,1,0:T(8,128)(2,1)}, f32[8,8,128]{2,1,0:T(8,128)}, bf16[8,128,512]{2,1,0:T(8,128)(2,1)}...) custom-call(bf16[128,1024]{1,0:T(8,128)(2,1)} %get-tuple-element.101.refs_0_, ...), custom_call_target="tpu_custom_call" | custom-call | tf_op jit(solution)/shard_map/pallas_call | solution.py:241
  148.4 11.9 %shard_map.308 = (bf16[512,256]{1,0:T(8,128)(2,1)}, f32[512,256]{1,0:T(8,128)}, f32[32,512]{1,0:T(8,128)}, bf16[32,512]{1,0:T(8,128)(2,1)}) custom-call(bf16[512,1024]{1,0:T(8,128)(2,1)} %bitcast.83, bf16[1024,256]{1,0:T(8,128)(2,1)} %bitcast.92, bf16[1024,512]{1,0:T(8,128)(2,1)} %bitcast.88, bf16[1024,256]{1,0:T(8,128)(2,1)} %bitcast.94, ...), custom_call_target="tpu_custom_call" | custom-call | tf_op jit(solution)/shard_map/pallas_call | solution.py:259
  160.4 5.9 %shard_map.309 = bf16[4,32,512]{2,1,0:T(8,128)(2,1)} custom-call(bf16[32,512]{1,0:T(8,128)(2,1)} %get-tuple-element.110.refs_0_), custom_call_target="tpu_custom_call" | custom-call | tf_op jit(solution)/shard_map/pallas_call | solution.py:241
  166.2 0.9 bitcast_convert_fusion
  167.6 4.6 %shard_map.311 = (bf16[512,128]{1,0:T(8,128)(2,1)}, f32[512,256]{1,0:T(8,128)}) custom-call(bf16[512,1024]{1,0:T(8,128)(2,1)} %bitcast.86, bf16[1024,256]{1,0:T(8,128)(2,1)} %bitcast.96, bf16[128,3840]{1,0:T(8,128)(2,1)} %bitcast.75, s32[512,1]{1,0:T(8,128)} %copy.53.owner_ref), custom_call_target="tpu_custom_call" | custom-call | tf_op jit(solution)/shard_map/pallas_call | solution.py:259
  172.3 34.3 %shard_map.310.refs_0_ = bf16[512,65536]{1,0:T(8,128)(2,1)} custom-call(s32[512,128]{1,0:T(8,128)S(1)} %bitcast.64, s32[512,128]{1,0:T(8,128)S(1)} %bitcast.66, f32[512,128]{1,0:T(8,128)S(1)} %bitcast.68), custom_call_target="tpu_custom_call" | custom-call | tf_op jit(solution)/shard_map/pallas_call | solution.py:782
  206.6 33.3 %shard_map.312 = (bf16[512,256]{1,0:T(8,128)(2,1)S(1)}, bf16[512,256]{1,0:T(8,128)(2,1)S(1)}, bf16[512,256]{1,0:T(8,128)(2,1)S(1)}, f32[512,1]{1,0:T(8,128)S(1)}) custom-call(bf16[512,65536]{1,0:T(8,128)(2,1)} %shard_map.310.refs_0_, bf16[8,8192,256]{2,1,0:T(8,128)(2,1)} %bitcast.70, f32[512,256]{1,0:T(8,128)S(1)} %copy-done.2, f32[512,256]{1,0:T(8,128)S(1)} %copy-done.3, ...), custom_call_target="tpu_custom_call" | custom-call | tf_op jit(solution)/shard_map/pallas_call | solution.py:832
  240.0 0.7 copy-done.1
  241.2 0.8 dynamic-slice_bitcast_fusion
  242.0 0.8 collective-permute-start
  242.7 1.9 collective-permute-start.1
  244.7 1.2 collective-permute-start.2
  245.8 50.9 %shard_map.313 = bf16[128,512]{1,0:T(8,128)(2,1)S(1)} custom-call(s32[512,128]{1,0:T(8,128)S(1)} %bitcast.65, s32[512,128]{1,0:T(8,128)S(1)} %bitcast.67, bf16[512,256]{1,0:T(8,128)(2,1)S(1)} %get-tuple-element.116.grads_ref, f32[512,1]{1,0:T(8,128)S(1)} %get-tuple-element.117.scale_ref, bf16[8,8192,256]{2,1,0:T(8,128)(2,1)} %bitcast.71), custom_call_target="tpu_custom_call" | custom-call | tf_op jit(solution)/shard_map/pallas_call | solution.py:888
  296.8 0.6 copy-done.4
  297.5 4.8 %shard_map.314.pieces_ref = bf16[4,32,512]{2,1,0:T(8,128)(2,1)} custom-call(bf16[4,32,512]{2,1,0:T(8,128)(2,1)} %bitcast.69), custom_call_target="tpu_custom_call" | custom-call | tf_op jit(solution)/shard_map/pallas_call | solution.py:241
  302.2 11.9 %shard_map.315 = (bf16[512,512]{1,0:T(8,128)(2,1)}, bf16[512,1024]{1,0:T(8,128)(2,1)}, bf16[32,512]{1,0:T(8,128)(2,1)}, bf16[16,512]{1,0:T(8,128)(2,1)}) custom-call(f32[32,512]{1,0:T(8,128)} %get-tuple-element.109.weights_ref, bf16[4,32,512]{2,1,0:T(8,128)(2,1)} %shard_map.314.pieces_ref, bf16[2,256,256]{2,1,0:T(8,128)(2,1)} %bitcast.99, ...), custom_call_target="tpu_custom_call" | custom-call | tf_op jit(solution)/shard_map/pallas_call | solution.py:259
  314.2 29.6 %shard_map.316 = (bf16[4,128,1024]{2,1,0:T(8,128)(2,1)}, bf16[4,32,512]{2,1,0:T(8,128)(2,1)}, bf16[4,16,512]{2,1,0:T(8,128)(2,1)}) custom-call(bf16[4,128,1024]{2,1,0:T(8,128)(2,1)} %bitcast.104, bf16[32,512]{1,0:T(8,128)(2,1)} %get-tuple-element.122.refs_1_, bf16[16,512]{1,0:T(8,128)(2,1)} %get-tuple-element.123.refs_2_), custom_call_target="tpu_custom_call" | custom-call | tf_op jit(solution)/shard_map/pallas_call | solution.py:241
  343.8 5.5 %shard_map.317 = (f32[128,1024]{1,0:T(8,128)}, bf16[128,1024]{1,0:T(8,128)(2,1)}, bf16[128,1024]{1,0:T(8,128)(2,1)}, bf16[16,128]{1,0:T(8,128)(2,1)}, bf16[32,51...) custom-call(bf16[4,128,1024]{2,1,0:T(8,128)(2,1)} %get-tuple-element.124.pieces_ref, ...), custom_call_target="tpu_custom_call" | custom-call | tf_op jit(solution)/shard_map/pallas_call | solution.py:259
  349.4 8.0 %shard_map.318 = (bf16[4,128,256]{2,1,0:T(8,128)(2,1)}, bf16[4,16,128]{2,1,0:T(8,128)(2,1)}) custom-call(bf16[128,1024]{1,0:T(8,128)(2,1)} %get-tuple-element.134.refs_0_, bf16[16,128]{1,0:T(8,128)(2,1)} %get-tuple-element.135.refs_1_), custom_call_target="tpu_custom_call" | custom-call | tf_op jit(solution)/shard_map/pallas_call | solution.py:241
  357.4 15.5 %shard_map.319 = (bf16[512,768]{1,0:T(8,128)(2,1)}, bf16[512,1024]{1,0:T(8,128)(2,1)}, bf16[48,512]{1,0:T(8,128)(2,1)}) custom-call(bf16[512,768]{1,0:T(8,128)(2,1)} %get-tuple-element.133.projected_ref, bf16[512,256]{1,0:T(8,128)(2,1)} %bitcast.112, s32[1,512]{1,0:T(1,128)} %bitcast.121, s32[512,1]{1,0:T(8,128)} %copy.52.below_ref, ...), custom_call_target="tpu_custom_call" | custom-call | tf_op jit(solution)/shard_map/pallas_call | solution.py:259
  372.9 34.6 %shard_map.320 = (bf16[4,128,1024]{2,1,0:T(8,128)(2,1)}, bf16[4,48,512]{2,1,0:T(8,128)(2,1)}, bf16[4,128,256]{2,1,0:T(8,128)(2,1)}) custom-call(bf16[4,128,1024]{2,1,0:T(8,128)(2,1)} %bitcast.103, bf16[48,512]{1,0:T(8,128)(2,1)} %get-tuple-element.138.refs_1_, bf16[128,1024]{1,0:T(8,128)(2,1)} %get-tuple-element.139.refs_2_), custom_call_target="tpu_custom_call" | custom-call | tf_op jit(solution)/shard_map/pallas_call | solution.py:241
  407.5 3.3 shard_map.321
  410.8 6.5 %shard_map.322 = (bf16[128,2560]{1,0:T(8,128)(2,1)}, bf16[1024,160]{1,0:T(8,128)(2,1)}) custom-call(bf16[512,384]{1,0:T(8,128)(2,1)} %get-tuple-element.144.low_one_ref, bf16[512,768]{1,0:T(8,128)(2,1)} %get-tuple-element.145.projected_ref, bf16[512,256]{1,0:T(8,128)(2,1)} %get-tuple-element.146.low_three_ref, ...), custom_call_target="tpu_custom_call" | custom-call | tf_op jit(solution)/shard_map/pallas_call | solution.py:259
  417.4 17.6 %shard_map.323 = (bf16[8,16,2560]{2,1,0:T(8,128)(2,1)}, bf16[8,128,160]{2,1,0:T(8,128)(2,1)}) custom-call(bf16[8,16,2560]{2,1,0:T(8,128)(2,1)} %bitcast.109, bf16[8,128,160]{2,1,0:T(8,128)(2,1)} %bitcast.110), custom_call_target="tpu_custom_call" | custom-call | tf_op jit(solution)/shard_map/pallas_call | solution.py:241
  435.0 2.1 shard_map.324
  437.0 1.4 copy.76
  438.5 1.5 copy.68
  440.0 1.5 copy.70
  (48 shorter events, 1.2 us)
Async XLA Ops:
  7.2 0.8 copy-start.14
  7.2 1.6 copy-start.15
  7.2 2.3 copy-start.13
  7.2 2.9 copy-start.11
  7.2 3.9 copy-start.16
  7.2 4.5 copy-start.12
  7.2 8.2 %copy-start.17 = (bf16[1024]{0:T(1024)(128)(2,1)S(1)}, bf16[1024]{0:T(1024)(128)(2,1)}, u32[]{:S(2)}) copy-start(bf16[1024]{0:T(1024)(128)(2,1)} %param.25) | copy-start | bytes 6148
  7.3 199.4 %all-gather.3.cloned.1.call-start = ((), (), s32[]{:S(2)}) async-start(), calls=%async_computation | async-start | bytes 37748736 | tf_op jit(solution)/shard_map/all_gather | solution.py:1010
  10.1 97.4 %copy-start.18 = (bf16[1024]{0:T(1024)(128)(2,1)S(1)}, bf16[1024]{0:T(1024)(128)(2,1)}, u32[]{:S(2)}) copy-start(bf16[1024]{0:T(1024)(128)(2,1)} %param.26) | copy-start | bytes 6148
  116.0 51.3 %copy-start.6 = (s32[4,2,32,512]{3,2,1,0:T(8,128)S(1)}, s32[4,2,32,512]{3,2,1,0:T(8,128)}, u32[]{:S(2)}) copy-start(s32[4,2,32,512]{3,2,1,0:T(8,128)} %picks_ref.3) | copy-start | bytes 1572868
  172.3 34.4 %copy-start.2 = (f32[512,256]{1,0:T(8,128)S(1)}, f32[512,256]{1,0:T(8,128)}, u32[]{:S(2)}) copy-start(f32[512,256]{1,0:T(8,128)} %get-tuple-element.111.refs_2_) | copy-start | bytes 1572868
  172.3 34.4 %copy-start.3 = (f32[512,256]{1,0:T(8,128)S(1)}, f32[512,256]{1,0:T(8,128)}, u32[]{:S(2)}) copy-start(f32[512,256]{1,0:T(8,128)} %get-tuple-element.114.refs_3_) | copy-start | bytes 1572868
  172.3 34.4 %copy-start.5 = (f32[8,8,128]{2,1,0:T(8,128)S(1)}, f32[8,8,128]{2,1,0:T(8,128)}, u32[]{:S(2)}) copy-start(f32[8,8,128]{2,1,0:T(8,128)} %get-tuple-element.115.refs_4_) | copy-start | bytes 98308
  206.6 34.1 %copy-start.7 = (bf16[8,128,256]{2,1,0:T(8,128)(2,1)S(1)}, bf16[8,128,256]{2,1,0:T(8,128)(2,1)}, u32[]{:S(2)}) copy-start(bf16[8,128,256]{2,1,0:T(8,128)(2,1)} %get-tuple-element.113) | copy-start | bytes 1572868
  240.0 0.7 copy-start.1
  240.7 56.0 %copy-start = (bf16[512,256]{1,0:T(8,128)(2,1)}, bf16[512,256]{1,0:T(8,128)(2,1)S(1)}, u32[]{:S(2)}) copy-start(bf16[512,256]{1,0:T(8,128)(2,1)S(1)} %get-tuple-element.118.mixed_ref) | copy-start | bytes 786436
  242.0 55.4 %collective-permute-start = (bf16[128,1024]{1,0:T(8,128)(2,1)S(1)}, bf16[128,1024]{1,0:T(8,128)(2,1)S(1)}, u32[]{:S(2)}, u32[]{:S(2)}) collective-permute-start(bf16[128,1024]{1,0:T(8,128)(2,1)S(1)} %get-tuple-element.193), channel_id=1, source_target_pairs={{0,1},{1,2},{2,3},{3,0},{4,5},{5,6},{6,7},{7,4},{8,9},{9,10},{10,1... | collective-permute-start | bytes 786440 | tf_op jit(solution)/shard_map/ppermute | solution.py:1093
  242.7 54.7 %collective-permute-start.1 = (bf16[128,1024]{1,0:T(8,128)(2,1)S(1)}, bf16[128,1024]{1,0:T(8,128)(2,1)S(1)}, u32[]{:S(2)}, u32[]{:S(2)}) collective-permute-start(bf16[128,1024]{1,0:T(8,128)(2,1)S(1)} %get-tuple-element.192), channel_id=1, source_target_pairs={{0,2},{1,3},{2,0},{3,1},{4,6},{5,7},{6,4},{7,5},{8,10},{9,11},{10,... | collective-permute-start | bytes 786440 | tf_op jit(solution)/shard_map/ppermute | solution.py:1093
  244.7 52.8 %collective-permute-start.2 = (bf16[128,1024]{1,0:T(8,128)(2,1)S(1)}, bf16[128,1024]{1,0:T(8,128)(2,1)S(1)}, u32[]{:S(2)}, u32[]{:S(2)}) collective-permute-start(bf16[128,1024]{1,0:T(8,128)(2,1)S(1)} %get-tuple-element.191), channel_id=1, source_target_pairs={{0,3},{1,0},{2,1},{3,2},{4,7},{5,4},{6,5},{7,6},{8,11},{9,8},{10,9... | collective-permute-start | bytes 786440 | tf_op jit(solution)/shard_map/ppermute | solution.py:1093
  296.8 0.7 copy-start.4
  297.4 46.4 %copy-start.8 = (bf16[128,1024]{1,0:T(8,128)(2,1)}, bf16[128,1024]{1,0:T(8,128)(2,1)S(1)}, u32[]{:S(2)}) copy-start(bf16[128,1024]{1,0:T(8,128)(2,1)S(1)} %collective-permute-done.refs_1_) | copy-start | bytes 786436
  297.4 46.4 %copy-start.9 = (bf16[128,1024]{1,0:T(8,128)(2,1)}, bf16[128,1024]{1,0:T(8,128)(2,1)S(1)}, u32[]{:S(2)}) copy-start(bf16[128,1024]{1,0:T(8,128)(2,1)S(1)} %collective-permute-done.1.refs_2_) | copy-start | bytes 786436
  297.4 46.4 %copy-start.10 = (bf16[128,1024]{1,0:T(8,128)(2,1)}, bf16[128,1024]{1,0:T(8,128)(2,1)S(1)}, u32[]{:S(2)}) copy-start(bf16[128,1024]{1,0:T(8,128)(2,1)S(1)} %collective-permute-done.2.refs_3_) | copy-start | bytes 786436
Sparse Core Ops, SparseCore 0:
  10.0 193.8 all-gather.2

commit v2 on v0

v2 whole, which is shorter than its diff:
```python
import types

import jax
import jax.numpy as jnp
from jax import lax
from jax.experimental import pallas as pl
from jax.experimental.pallas import tpu as pltpu
from jax.sharding import PartitionSpec as P

DP, TP = "dp", "tensor"
HD = 64
NKEYS = 256
RANK = 16
NAD = 8
EPS = 1e-06
NEGATIVE = -1e30
F32, BF16, I32 = jnp.float32, jnp.bfloat16, jnp.int32
MESH = pl.DeviceIdType.MESH
ANY = pl.BlockSpec(memory_space=pl.ANY)


def mm(a, b):
    return lax.dot_general(a, b, (((1,), (0,)), ((), ())), preferred_element_type=F32)


def mt(a, b):
    return lax.dot_general(a, b, (((1,), (1,)), ((), ())), preferred_element_type=F32)


def tm(a, b):
    return lax.dot_general(a, b, (((0,), (0,)), ((), ())), preferred_element_type=F32)


def two_parts(x):
    top = x.astype(BF16)
    return top, (x - top.astype(F32)).astype(BF16)


def whole(shape):
    return pl.BlockSpec(shape, lambda *_: (0,) * len(shape))


def stage(body, outs, ins, scratch=(), limit=56):
    return pl.pallas_call(
        body,
        grid=(1,),
        out_shape=[jax.ShapeDtypeStruct(shape, dtype) for shape, dtype in outs],
        in_specs=[whole(x.shape) for x in ins],
        out_specs=[whole(shape) for shape, _ in outs],
        scratch_shapes=list(scratch),
        compiler_params=pltpu.CompilerParams(vmem_limit_bytes=limit << 20),
    )(*ins)


def rms_forward(values, gain):
    factor = lax.rsqrt(jnp.mean(values * values, axis=-1, keepdims=True) + EPS)
    return values * factor * gain


def rms_backward(values, gain, upstream):
    factor = lax.rsqrt(jnp.mean(values * values, axis=-1, keepdims=True) + EPS)
    scaled = upstream * gain
    return factor * scaled - values * (factor * factor * factor) * jnp.mean(
        values * scaled, axis=-1, keepdims=True
    )


def masked(values, owner):
    columns = lax.broadcasted_iota(I32, values.shape, 1)
    adapter = lax.rem(lax.div(columns, RANK), NAD)
    return jnp.where(adapter == owner, values, 0.0).astype(BF16)


def folding(parts):
    shape = (parts * RANK, parts * NAD * RANK)
    short = lax.broadcasted_iota(I32, shape, 0)
    column = lax.broadcasted_iota(I32, shape, 1)
    same = (lax.div(short, RANK) == lax.div(column, NAD * RANK)) & (
        lax.rem(short, RANK) == lax.rem(column, RANK)
    )
    return jnp.where(same, 1.0, 0.0).astype(BF16)


def shorten(values):
    return mt(folding(values.shape[1] // (NAD * RANK)), values).astype(BF16)


def lengthen(short, owner):
    return masked(tm(short, folding(short.shape[0] // RANK)), owner)


def side_by_side(blocks):
    return jnp.concatenate([blocks[p] for p in range(blocks.shape[0])], axis=1)


def block_probs(queries, keys, across_ref, down_ref, r, block):
    top = (r + 1) * block
    at = slice(r * block, top)
    scores = mt(queries[at], keys[:top]) * HD**-0.5
    place = lax.broadcasted_iota(I32, (block, top), 0) + r * block
    other = lax.broadcasted_iota(I32, (block, top), 1)
    ahead = across_ref[:, :top]
    seen = (other <= place) & ((ahead == 0) | (ahead == down_ref[at, :]))
    scores = jnp.where(seen, scores, NEGATIVE)
    raised = jnp.exp(scores - jnp.max(scores, axis=-1, keepdims=True))
    return raised / jnp.sum(raised, axis=-1, keepdims=True)


def wide_lanes(pair, base=0):
    return pl.ds(pl.multiple_of(base + pair * 2 * HD, 2 * HD), 2 * HD)


def own_columns(short, owner, first):
    high, count = short.shape
    adapters = NAD // lax.axis_size(TP)
    pattern = lax.broadcasted_iota(I32, (high, adapters * high), 0) == lax.rem(
        lax.broadcasted_iota(I32, (high, adapters * high), 1), high
    )
    spread = tm(short, jnp.where(pattern, 1.0, 0.0).astype(BF16))
    adapter = lax.div(lax.broadcasted_iota(I32, (count, adapters * high), 1), high) + first
    return jnp.where(adapter == owner, spread, 0.0).astype(BF16)


class Waited:
    def __init__(self, names, refs, loads):
        self._pending = dict(zip(names, zip(refs, loads)))

    def __getattr__(self, name):
        ref, load = self._pending[name]
        load.wait()
        setattr(self, name, ref)
        return ref


def backward(given, mixed_parts, ups_spots, cid, block=128):
    _, query_spot, gate_spot, attend_spot, mixed_spot, low_spot = ups_spots
    shown = types.SimpleNamespace(**given)
    picked = given.pop(next(iter(given)))
    names = list(given)
    arrays = [picked, *given.values(), *mixed_parts]
    ranks, groups = lax.axis_size(TP), lax.axis_size(DP)
    count, width = shown.attended.shape
    local, model = shown.inputs.shape
    number = shown.weights.shape[0]
    half = shown.keys.shape[2]
    space = NAD * RANK
    adapters = NAD // ranks
    lines, share = space // groups, model // groups
    wides = [width] * 3 + [2 * half] + [width] * 5
    tall = [adapters * 2 * RANK, adapters * 3 * RANK]
    vmem = dict(
        pick_in=((ranks, number, count), BF16),
        dense=((NKEYS, count), F32),
        grad_query=((count, 2 * half), BF16),
        normed_out=((ranks, local, model), BF16),
        normed_in=((ranks, local, model), BF16),
        three_in=((ranks, 2 * RANK, count), BF16),
        four_in=((ranks, RANK, count), BF16),
        three_sum=((2 * RANK, count), BF16),
        four_sum=((RANK, count), BF16),
        attended_out=((local, model), BF16),
        attended_in=((ranks, local, width), BF16),
        branch_out=((local, model), BF16),
        branch_in=((ranks, local, width), BF16),
        back_in=((ranks, RANK, local), BF16),
        grad_middle=((local, model), F32),
        grads=((count, 3 * width), BF16),
        key_sum=((2, count, HD), F32),
        value_sum=((2, count, HD), F32),
        input_out=((ranks, local, model), BF16),
        input_in=((ranks, local, model), BF16),
        one_in=((ranks, 3 * RANK, count), BF16),
        one_sum=((3 * RANK, count), BF16),
        ups_out=((groups, lines, sum(wides)), BF16),
        memory_out=((groups, tall[0], share), BF16),
        down_out=((groups, tall[1], share), BF16),
        outputs=((local, model), BF16),
        input_grad=((local, model), F32),
    )
    inputs = arrays[1:]
    results = [
        ((local, model), BF16),
        ((local, model), F32),
        ((groups, lines, sum(wides)), BF16),
        ((groups, tall[0], share), BF16),
        ((groups, tall[1], share), BF16),
    ]

    def body(*refs):
        outs = refs[len(arrays) : len(arrays) + len(results)]
        rest = refs[len(arrays) + len(results) :]
        v = types.SimpleNamespace(**dict(zip(vmem, rest[len(inputs) :])))
        loaded, saved, send, recv, far_send, far_recv = rest[len(inputs) + len(vmem) :]
        rank, group = lax.axis_index(TP), lax.axis_index(DP)
        barrier = pltpu.get_barrier_semaphore()
        for d in range(1, ranks):
            pl.semaphore_signal(
                barrier,
                inc=1,
                device_id={TP: lax.rem(rank + d, ranks)},
                device_id_type=MESH,
            )

        @pl.loop(1, groups)
        def _(d):
            pl.semaphore_signal(
                barrier,
                inc=1,
                device_id={DP: lax.rem(group + d, groups)},
                device_id_type=MESH,
            )

        loads = [
            pltpu.make_async_copy(refs[i + 1], rest[i], loaded.at[i]) for i in range(len(inputs))
        ]
        for load in loads:
            load.start()
        need = Waited(names, rest, loads)

        def near(i, d, src, dst):
            return pltpu.make_async_remote_copy(
                src_ref=src,
                dst_ref=dst,
                send_sem=send.at[i, d],
                recv_sem=recv.at[i, d],
                device_id={TP: lax.rem(rank + d, ranks)},
                device_id_type=MESH,
            )

        def far(i, d, src, dst):
            return pltpu.make_async_remote_copy(
                src_ref=src,
                dst_ref=dst,
                send_sem=far_send.at[i, d],
                recv_sem=far_recv.at[i, d],
                device_id={DP: lax.rem(group + d, groups)},
                device_id_type=MESH,
            )

        def far_piece(i, d, ref):
            return far(i, d, ref.at[lax.rem(group + d, groups)], outs[2 + i].at[group])

        def send_far(i, ref):
            @pl.loop(1, groups)
            def _(d):
                far_piece(i, d, ref).start()

            keep = pltpu.make_async_copy(ref.at[group], outs[2 + i].at[group], saved.at[2 + i])
            keep.start()
            return keep

        def shared(i, ref):
            return [near(i, d, ref.at[rank], ref.at[rank]) for d in range(1, ranks)]

        def columns(ref, p):
            return ref.at[:, pl.ds(pl.multiple_of(p * width, width), width)]

        def split(i, src, dst):
            return [
                near(i, d, columns(src, lax.rem(rank + d, ranks)), dst.at[rank])
                for d in range(1, ranks)
            ]

        def total(ref):
            return sum(ref[p].astype(F32) for p in range(ranks))

        own_tokens = pl.ds(pl.multiple_of(rank * local, local), local)
        own_columns_at = pl.ds(pl.multiple_of(rank * width, width), width)

        pick_in = v.pick_in
        own_pick = pltpu.make_async_copy(refs[0].at[rank], pick_in.at[rank], saved.at[0])
        own_pick.start()
        pl.semaphore_wait(barrier, ranks + groups - 2)
        picks_sent = [
            near(0, d, refs[0].at[lax.rem(rank + d, ranks)], pick_in.at[rank])
            for d in range(1, ranks)
        ]
        for c in picks_sent:
            c.start()
        weights_ref, keys_ref, picks_ref = need.weights, need.keys, need.picks
        own_pick.wait()
        for c in picks_sent:
            c.wait()

        slot = lax.broadcasted_iota(I32, (NKEYS, block), 0)
        for part in range(2):

            @pl.loop(0, count // block)
            def _(c):
                lanes = pl.ds(pl.multiple_of(c * block, block), block)
                weight = weights_ref[:, lanes]
                grad = sum(pick_in[p, :, lanes].astype(F32) for p in range(ranks))
                grad = weight * (grad - jnp.sum(grad * weight, axis=0, keepdims=True))
                grad = grad * (2 * half) ** -0.5
                dense = jnp.zeros((NKEYS, block), F32)
                for k in range(number):
                    hit = slot == picks_ref[part, k : k + 1, lanes]
                    dense += jnp.where(hit, grad[k : k + 1, :], 0.0)
                v.dense[:, lanes] = dense

            top, low = two_parts(v.dense[...])
            v.grad_query[:, part * half : (part + 1) * half] = (
                tm(top, keys_ref[part]) + tm(low, keys_ref[part])
            ).astype(BF16)

        query_ref, gate_ref, ups_ref = need.query, need.gate, need.ups
        grad_gate_ref, mixed_ref, owner_ref = need.grad_gate, need.mixed, need.owner
        normed_sent = []
        for d in list(range(1, ranks)) + [0]:
            at = pl.ds(pl.multiple_of(lax.rem(rank + d, ranks) * local, local), local)
            asked, gates, own = v.grad_query[at, :], grad_gate_ref[at, :], owner_ref[at, :]
            part = (mt(asked, query_ref[...]) + mt(gates, gate_ref[...])).astype(BF16)
            if d:
                v.normed_out[d] = part
                normed_sent.append(near(1, d, v.normed_out.at[d], v.normed_in.at[rank]))
                normed_sent[-1].start()
            else:
                v.normed_in[rank] = part
            three = jnp.concatenate(
                [mt(asked, ups_ref[:, query_spot]), mt(gates, ups_ref[:, gate_spot])], axis=1
            )
            v.three_in[rank, :, at] = shorten(masked(three, own))
            v.four_in[rank, :, at] = shorten(
                masked(mt(mixed_ref[at, :], ups_ref[:, low_spot]), own)
            )
        short_sent = shared(2, v.three_in) + shared(3, v.four_in)
        for c in short_sent:
            c.start()
        owner_own = need.owner_own[...]
        middle_ref, cotangent_ref, gain_two = need.middle, need.cotangent, need.gain_two
        down_ref, out_ref, attend_ref = need.down_memory, need.out_t, need.attend_t
        mixed_refs = []
        for i in range(len(names), len(inputs)):
            loads[i].wait()
            mixed_refs.append(rest[i])
        for c in normed_sent + short_sent:
            c.wait()

        v.three_sum[...] = total(v.three_in).astype(BF16)
        v.four_sum[...] = total(v.four_in).astype(BF16)
        grad_three = lengthen(v.three_sum[:, own_tokens], owner_own)
        upstream = total(v.normed_in) + mt(grad_three, down_ref[...])
        grad = cotangent_ref[...].astype(F32) + rms_backward(
            middle_ref[...], gain_two[...].astype(F32), upstream
        )
        v.grad_middle[...] = grad
        branch = grad.astype(BF16)
        v.branch_out[...] = branch
        low = masked(mt(branch, ups_ref[:, attend_spot]), owner_own)
        v.attended_out[...] = (mm(branch, out_ref[...]) + mm(low, attend_ref[...])).astype(BF16)
        v.back_in[rank] = shorten(low)
        v.attended_in[rank] = v.attended_out[:, own_columns_at]
        v.branch_in[rank] = v.branch_out[:, own_columns_at]
        attended_sent = split(4, v.attended_out, v.attended_in)
        later_sent = shared(5, v.back_in) + split(6, v.branch_out, v.branch_in)
        for c in attended_sent + later_sent:
            c.start()

        low_four = lengthen(v.four_sum[:, own_tokens], owner_own)
        v.outputs[...] = (
            middle_ref[...]
            + sum(ref[...].astype(F32) for ref in mixed_refs)
            + mm(low_four, ups_ref[:, mixed_spot])
        ).astype(BF16)
        stores = [pltpu.make_async_copy(v.outputs, outs[0], saved.at[0])]
        stores[0].start()
        owner = owner_ref[...]
        starts = [sum(wides[:i]) for i in range(len(wides))]

        def put(i, left, rows):
            found = tm(left, rows).astype(F32)
            for g in range(groups):
                v.ups_out[g, :, starts[i] : starts[i] + wides[i]] = found[
                    g * lines : (g + 1) * lines
                ].astype(BF16)

        def put_down(out_ref, short, normed_ref):
            spread = own_columns(short, owner, rank * adapters)
            step = max(share, 128)
            for c in range(model // step):
                found = tm(spread, normed_ref[:, c * step : (c + 1) * step]).astype(BF16)
                for p in range(step // share):
                    out_ref[c * (step // share) + p] = found[:, p * share : (p + 1) * share]

        low_three = need.low_three
        put(3, low_three[:, :space], v.grad_query[...])
        put(4, low_three[:, space:], grad_gate_ref[...])
        put(5, lengthen(v.four_sum[...], owner), need.own_cotangent[...])
        put(7, need.low_four_back[...], mixed_ref[...])
        put_down(v.memory_out, v.three_sum[...], need.normed_rows)
        memory_kept = send_far(1, v.memory_out)
        projected_ref, across_ref, below_ref = need.projected, need.across, need.below
        weight_ref = need.full_in
        for c in attended_sent:
            c.wait()

        @pl.loop(0, width // (2 * HD))
        def _(pair):
            queries, keys, values = [projected_ref[:, wide_lanes(pair, p * width)] for p in range(3)]
            above = jnp.concatenate(
                [v.attended_in[p, :, wide_lanes(pair)] for p in range(ranks)], axis=0
            )
            v.key_sum[...] = jnp.zeros_like(v.key_sum)
            v.value_sum[...] = jnp.zeros_like(v.value_sum)
            for r in range(count // block):
                at, top = slice(r * block, (r + 1) * block), (r + 1) * block
                parts = []
                for h in range(2):
                    lanes = slice(h * HD, (h + 1) * HD)
                    probs = block_probs(
                        queries[:, lanes], keys[:, lanes], across_ref, below_ref, r, block
                    )
                    grad_probs = mt(above[at, lanes], values[:top, lanes])
                    inner = jnp.sum(probs * grad_probs, axis=-1, keepdims=True)
                    grad_scores = (probs * (grad_probs - inner)).astype(BF16)
                    parts.append(mm(grad_scores, keys[:top, lanes]))
                    v.key_sum[h, :top, :] += tm(grad_scores, queries[at, lanes])
                    v.value_sum[h, :top, :] += tm(probs.astype(BF16), above[at, lanes])
                v.grads[at, wide_lanes(pair)] = (
                    jnp.concatenate(parts, axis=1) * HD**-0.5
                ).astype(BF16)
            v.grads[:, wide_lanes(pair, width)] = (
                jnp.concatenate([v.key_sum[0], v.key_sum[1]], axis=1) * HD**-0.5
            ).astype(BF16)
            v.grads[:, wide_lanes(pair, 2 * width)] = jnp.concatenate(
                [v.value_sum[0], v.value_sum[1]], axis=1
            ).astype(BF16)

        input_sent = []
        for d in list(range(1, ranks)) + [0]:
            at = pl.ds(pl.multiple_of(lax.rem(rank + d, ranks) * local, local), local)
            part = mt(v.grads[at, :], weight_ref[...]).astype(BF16)
            if d:
                v.input_out[d] = part
                input_sent.append(near(7, d, v.input_out.at[d], v.input_in.at[rank]))
                input_sent[-1].start()
            else:
                v.input_in[rank] = part
            one = jnp.concatenate(
                [
                    mt(
                        v.grads[at, p * width : (p + 1) * width],
                        ups_ref[:, p * width : (p + 1) * width],
                    )
                    for p in range(3)
                ],
                axis=1,
            )
            v.one_in[rank, :, at] = shorten(masked(one, owner_ref[at, :]))
        one_sent = shared(8, v.one_in)
        for c in one_sent:
            c.start()
        for c in later_sent:
            c.wait()
        low_one = need.low_one
        for p in range(3):
            put(
                p,
                low_one[:, p * space : (p + 1) * space],
                v.grads[:, p * width : (p + 1) * width],
            )
        put(6, lengthen(side_by_side(v.back_in), owner), need.attended[...])
        put(
            8,
            lengthen(side_by_side(need.two_short), owner),
            jnp.concatenate([v.branch_in[p] for p in range(ranks)], axis=0),
        )
        ups_kept = send_far(0, v.ups_out)
        down_input_ref, rows_ref, gain_one = need.down_input, need.inputs, need.gain_one
        normed_one_ref = need.normed_one
        for c in one_sent:
            c.wait()
        v.one_sum[...] = total(v.one_in).astype(BF16)
        put_down(v.down_out, v.one_sum[...], normed_one_ref)
        down_kept = send_far(2, v.down_out)
        for c in input_sent:
            c.wait()
        low = lengthen(v.one_sum[:, own_tokens], owner_own)
        upstream = total(v.input_in) + mt(low, down_input_ref[...])
        v.input_grad[...] = v.grad_middle[...] + rms_backward(
            rows_ref[...].astype(F32), gain_one[...].astype(F32), upstream
        )
        stores.append(pltpu.make_async_copy(v.input_grad, outs[1], saved.at[1]))
        stores[1].start()

        @pl.loop(1, groups)
        def _(d):
            for i, ref in enumerate((v.ups_out, v.memory_out, v.down_out)):
                far_piece(i, d, ref).wait()

        for c in stores + [ups_kept, memory_kept, down_kept]:
            c.wait()

    near_sems = pltpu.SemaphoreType.DMA((9, ranks))
    far_sems = pltpu.SemaphoreType.DMA((3, groups))
    return wides, pl.pallas_call(
        body,
        out_shape=[jax.ShapeDtypeStruct(shape, dtype) for shape, dtype in results],
        in_specs=[ANY] * len(arrays),
        out_specs=[ANY] * len(results),
        scratch_shapes=[pltpu.VMEM(x.shape, x.dtype) for x in inputs]
        + [pltpu.VMEM(shape, dtype) for shape, dtype in vmem.values()]
        + [
            pltpu.SemaphoreType.DMA((len(inputs),)),
            pltpu.SemaphoreType.DMA((5,)),
            near_sems,
            near_sems,
            far_sems,
            far_sems,
        ],
        compiler_params=pltpu.CompilerParams(
            collective_id=cid, has_side_effects=True, vmem_limit_bytes=58 << 20
        ),
    )(*arrays)


def forward(given, table, key_picks, spots, cid, block=128, sub=32, conv=32):
    _, query_spot, gate_spot, attend_spot, mixed_spot, low_spot = spots
    shown = types.SimpleNamespace(**given)
    names = list(given)
    local_arrays = list(given.values())
    ranks, groups = lax.axis_size(TP), lax.axis_size(DP)
    local, model = shown.inputs.shape
    count = shown.owner.shape[0]
    width = shown.gate.shape[1]
    half = shown.keys.shape[2]
    number = key_picks.shape[2]
    picks = key_picks.shape[0] * number
    space = NAD * RANK
    rows = table.shape[0]
    piece = rows // 2
    blocks = 2 * groups
    stride = sub + 1
    chips = groups // 2
    relayed = chips == 4
    hops = max(chips, 4)
    tree = [
        (shown.flat_in, 1),
        (shown.down_input, 2),
        (shown.ups, 2),
        (shown.out_t, 1),
        (shown.attend_t, 2),
        (shown.query, 2),
        (shown.gate, 1),
        (shown.down_memory, 1),
        (shown.mixed_t, 1),
    ]
    early, nested, late = (0, 1, 2), (3, 4), (5, 6, 7, 8)
    cuts = 8
    chunks = tuple(range(len(tree), len(tree) + cuts))
    route = [way for _, way in tree] + [1] * (cuts // 2) + [2] * (cuts // 2)
    tree_shapes = [
        (x.shape[0], x.shape[1] * (ranks if a in nested else 1)) for a, (x, _) in enumerate(tree)
    ]
    full = [((groups, *shape), BF16) for shape in tree_shapes]
    results = dict(
        normed_one=((count, model), BF16),
        low_one=((count, 3 * space), BF16),
        projected=((count, 3 * width), BF16),
        attended=((count, width), BF16),
        middle=((local, model), F32),
        two_short=((ranks, RANK, local), BF16),
        normed_rows=((count, model), BF16),
        low_three=((count, 2 * space), BF16),
        weights=((number, count), F32),
        mixed=((count, width), BF16),
        grad_recalled=((count, width), BF16),
        grad_gate=((count, width), BF16),
        scale=((count, 1), F32),
        low_four_back=((count, space), BF16),
        own_cotangent=((count, width), BF16),
        first=((count, picks), I32),
        second=((count, picks), I32),
    )
    vmem = dict(
        rows_in=((ranks, local, model), BF16),
        cotangent_in=((ranks, local, model), BF16),
        out_stage=(tree_shapes[3], BF16),
        attend_stage=(tree_shapes[4], BF16),
        attended_in=((local, model), BF16),
        normed_two=((local, model), BF16),
        asked=((count, 2 * half), F32),
        every=((NKEYS, count), F32),
        gate_pre=((count, width), F32),
        narrow=((ranks, number, count), BF16),
        grad_mixed=((count, width), F32),
        picks=(key_picks.shape, I32),
        by_token=((count, picks), F32),
        low=((NKEYS * stride, 128), F32),
        high=((NKEYS * stride, 128), F32),
        spread=((2, sub, NKEYS * NKEYS), BF16),
        dense_in=((2, count, piece), BF16),
        table_in=((2, piece, width), BF16),
        total=((count, width), F32),
        largest=((8, 1), F32),
    )
    outs = [
        *full,
        *results.values(),
        ((groups, rows, width), BF16),
        ((count, NKEYS * NKEYS), BF16),
    ]

    def body(*refs):
        inputs = refs[: len(names) + 2]
        out_refs = refs[len(inputs) : len(inputs) + len(outs)]
        rest = list(refs[len(inputs) + len(outs) :])

        def take(n):
            taken = rest[:n]
            del rest[:n]
            return taken

        held = take(len(names))
        gathered = take(len(tree))
        r = types.SimpleNamespace(**dict(zip(results, take(len(results)))))
        v = types.SimpleNamespace(**dict(zip(vmem, take(len(vmem)))))
        loaded, kept, stored, near_send, near_recv, tree_send, tree_recv, pass_send, pass_recv = rest[:9]
        moved = rest[9]
        table_ref, picks_ref = inputs[-2:]
        table_out, dense_out = out_refs[-2:]
        rank, group = lax.axis_index(TP), lax.axis_index(DP)
        barrier = pltpu.get_barrier_semaphore()
        for d in range(1, ranks):
            pl.semaphore_signal(
                barrier,
                inc=1,
                device_id={TP: lax.rem(rank + d, ranks)},
                device_id_type=MESH,
            )

        @pl.loop(1, groups)
        def _(d):
            pl.semaphore_signal(
                barrier,
                inc=1,
                device_id={DP: lax.rem(group + d, groups)},
                device_id_type=MESH,
            )

        loads = [
            pltpu.make_async_copy(inputs[i], held[i], loaded.at[i]) for i in range(len(names))
        ]
        loads.append(pltpu.make_async_copy(picks_ref, v.picks, loaded.at[len(names)]))
        for load in loads:
            load.start()
        need = Waited(names, held, loads)
        raw = types.SimpleNamespace(**dict(zip(names, inputs)))

        def near(i, d, src, dst):
            return pltpu.make_async_remote_copy(
                src_ref=src,
                dst_ref=dst,
                send_sem=near_send.at[i, d],
                recv_sem=near_recv.at[i, d],
                device_id={TP: lax.rem(rank + d, ranks)},
                device_id_type=MESH,
            )

        def columns(ref, p, wide):
            return ref.at[:, pl.ds(pl.multiple_of(p * wide, wide), wide)]

        def cut_of(a):
            return pl.ds((a - len(tree)) * (rows // cuts), rows // cuts)

        def source(a):
            if a in chunks:
                return table_ref.at[cut_of(a)]
            if a in nested:
                return (v.out_stage, v.attend_stage)[a - 3]
            return inputs[names.index(given_names[a])]

        given_names = [names[i] for i in tree_names]

        def place(a, p):
            if a in chunks:
                return table_out.at[p, cut_of(a)]
            return gathered[a].at[p]

        def partner(d):
            if not relayed:
                return lax.rem(group + 2 * d, groups)
            across = 2 - 4 * lax.rem(lax.div(group, 2), 2) if d & 1 else 0
            along = 4 - 8 * lax.div(group, 4) if d & 2 else 0
            return group + across + along

        def holder(d):
            if isinstance(d, int) and d == 0:
                return group
            return partner(d) if relayed else lax.rem(group - 2 * d + groups, groups)

        def to_chip(a, d):
            relay = relayed and d == 3
            shard = place(a, holder(route[a])) if relay else source(a)
            return pltpu.make_async_remote_copy(
                src_ref=shard,
                dst_ref=shard if relay else place(a, group),
                send_sem=tree_send.at[a, d],
                recv_sem=tree_recv.at[a, d],
                device_id={DP: partner(3 - route[a] if relay else d)},
                device_id_type=MESH,
            )

        def to_sibling(a, d):
            first = isinstance(d, int) and d == 0
            return pltpu.make_async_remote_copy(
                src_ref=source(a) if first else place(a, holder(d)),
                dst_ref=place(a, holder(d)),
                send_sem=pass_send.at[a, d],
                recv_sem=pass_recv.at[a, d],
                device_id={DP: group + 1 - 2 * lax.rem(group, 2)},
                device_id_type=MESH,
            )

        def own_copy(a):
            return pltpu.make_async_copy(source(a), place(a, group), kept.at[a])

        def begin(chosen):
            for a in chosen:
                own_copy(a).start()
                if relayed:
                    to_chip(a, 1).start()
                    to_chip(a, 2).start()
                else:

                    @pl.loop(1, chips)
                    def _(d):
                        to_chip(a, d).start()

                to_sibling(a, 0).start()

        def begin_table(chosen):
            if not relayed:
                begin(chosen)
                return
            for a in chosen:
                to_chip(a, route[a]).start()

        def rest_of_table(chosen):
            if relayed:
                for a in chosen:
                    to_chip(a, 3 - route[a]).start()
                for a in chosen:
                    own_copy(a).start()
                    to_sibling(a, 0).start()

        def onward(a, d):
            to_chip(a, d).wait_recv()
            to_sibling(a, d).start()

        def relay(chosen):
            if relayed:
                for a in chosen:
                    onward(a, route[a])
                    to_chip(a, 3).start()

        def other(chosen):
            if relayed:
                for a in chosen:
                    onward(a, 3 - route[a])

        def last(chosen):
            for a in chosen:
                if relayed:
                    onward(a, 3)
                else:

                    @pl.loop(1, chips)
                    def _(d):
                        onward(a, d)

        def settle(chosen):
            for a in chosen:
                own_copy(a).wait()
                to_sibling(a, 0).wait()
                if relayed:
                    for d in range(1, 4):
                        to_sibling(a, d).wait()
                        to_chip(a, d).wait_send()
                else:

                    @pl.loop(1, chips)
                    def _(d):
                        to_sibling(a, d).wait()
                        to_chip(a, d).wait_send()

        stores = []

        def store(src, dst):
            stores.append(pltpu.make_async_copy(src, dst, stored.at[len(stores)]))
            stores[-1].start()

        def store_trees(chosen):
            for a in chosen:
                store(gathered[a], out_refs[a])

        result_refs = dict(zip(results, out_refs[len(tree) :]))

        def flat(ref):
            return ref[...].reshape(-1, ref.shape[2])

        def done(ref):
            for name in results:
                if getattr(r, name) is ref:
                    store(ref, result_refs[name])

        pl.semaphore_wait(barrier, ranks + groups - 2)
        homes = []
        for i, (src, dst) in enumerate(((raw.inputs, v.rows_in), (raw.cotangent, v.cotangent_in))):
            homes.append(pltpu.make_async_copy(src, dst.at[rank], moved.at[i]))
        for i, (src, dst) in enumerate(((raw.out_t, v.out_stage), (raw.attend_t, v.attend_stage))):
            homes.append(
                pltpu.make_async_copy(src, columns(dst, rank, src.shape[1]), moved.at[2 + i])
            )
        for c in homes:
            c.start()
        nest_sent = [
            near(i, d, src, columns(dst, rank, src.shape[1]))
            for i, src, dst in ((0, raw.out_t, v.out_stage), (1, raw.attend_t, v.attend_stage))
            for d in range(1, ranks)
        ]
        rows_sent = [near(2, d, raw.inputs, v.rows_in.at[rank]) for d in range(1, ranks)]
        back_sent = [near(3, d, raw.cotangent, v.cotangent_in.at[rank]) for d in range(1, ranks)]
        for c in nest_sent + rows_sent:
            c.start()
        begin(early)
        for c in nest_sent:
            c.wait()
        homes[2].wait()
        homes[3].wait()
        begin(nested)
        begin(late)
        gain_one, owner_ref = need.gain_one, need.owner
        homes[0].wait()
        for c in rows_sent:
            c.wait()
        for c in range(ranks):
            r.normed_one[c * local : (c + 1) * local, :] = rms_forward(
                v.rows_in[c].astype(F32), gain_one[...].astype(F32)
            ).astype(BF16)
        done(r.normed_one)
        for c in back_sent:
            c.start()
        relay(early)
        other(early)
        relay(nested)
        relay(late)
        last(early)
        begin_table(chunks)
        rest_of_table(chunks)
        settle(early)
        store_trees(early)
        weight_ref, down_ref, ups_ref = gathered[:3]

        def up(spot):
            return ups_ref[:, :, spot].reshape(space, -1)

        @pl.loop(0, ranks)
        def _(c):
            at = pl.ds(pl.multiple_of(c * local, local), local)
            normed = r.normed_one[at, :]
            low = masked(mm(normed, flat(down_ref)), owner_ref[at, :])
            r.low_one[at, :] = low
            for p in range(3):
                lanes = slice(p * width, (p + 1) * width)
                r.projected[at, lanes] = (
                    mm(normed, weight_ref[:, :, lanes].reshape(model, width))
                    + mm(low[:, p * space : (p + 1) * space], up(lanes))
                ).astype(BF16)

        across_ref, below_ref = need.across, need.below

        @pl.loop(0, width // (2 * HD))
        def _(pair):
            queries, keys, values = [r.projected[:, wide_lanes(pair, p * width)] for p in range(3)]
            for q in range(count // block):
                top = (q + 1) * block
                parts = []
                for lanes in (slice(0, HD), slice(HD, 2 * HD)):
                    probs = block_probs(
                        queries[:, lanes], keys[:, lanes], across_ref, below_ref, q, block
                    )
                    parts.append(mm(probs.astype(BF16), values[:top, lanes]))
                r.attended[q * block : top, wide_lanes(pair)] = jnp.concatenate(
                    parts, axis=1
                ).astype(BF16)

        def lines_of(p):
            return r.attended.at[pl.ds(pl.multiple_of(p * local, local), local)]

        attended_sent = [
            near(4, d, lines_of(lax.rem(rank + d, ranks)), columns(v.attended_in, rank, width))
            for d in range(1, ranks)
        ]
        for c in attended_sent:
            c.start()
        own_rows = pl.ds(pl.multiple_of(rank * local, local), local)
        v.attended_in[:, pl.ds(pl.multiple_of(rank * width, width), width)] = r.attended[own_rows, :]
        done(r.low_one)
        done(r.projected)
        done(r.attended)
        other(nested)
        last(nested)
        settle(nested)
        store_trees(nested)
        out_ref, attend_ref = gathered[3:5]
        residual_ref, gain_two, owner_own = need.inputs, need.gain_two, need.owner_own[...]
        for c in attended_sent:
            c.wait()
        low = masked(mt(v.attended_in[...], flat(attend_ref)), owner_own)
        middle = (
            residual_ref[...].astype(F32)
            + mt(v.attended_in[...], flat(out_ref))
            + mm(low, up(attend_spot))
        )
        r.middle[...] = middle
        normed = rms_forward(middle, gain_two[...].astype(F32)).astype(BF16)
        v.normed_two[...] = normed
        r.normed_rows[own_rows, :] = normed
        r.two_short[rank] = shorten(low)
        normed_sent = [
            near(5, d, v.normed_two, r.normed_rows.at[own_rows]) for d in range(1, ranks)
        ] + [near(6, d, r.two_short.at[rank], r.two_short.at[rank]) for d in range(1, ranks)]
        for c in normed_sent:
            c.start()
        done(r.middle)
        loads[-1].wait()
        r.first[...] = jnp.concatenate(
            [v.picks[m, 0] for m in range(key_picks.shape[0])], axis=0
        ).T
        r.second[...] = jnp.concatenate(
            [v.picks[m, 1] for m in range(key_picks.shape[0])], axis=0
        ).T
        done(r.first)
        done(r.second)
        other(late)
        last(late)
        settle(late)
        store_trees(late)
        query_ref, gate_ref, memory_ref, mixed_ref = gathered[5:]
        homes[1].wait()
        for c in back_sent:
            c.wait()
        own_lanes = pl.ds(pl.multiple_of(rank * width, width), width)
        for c in range(ranks):
            at = slice(c * local, (c + 1) * local)
            r.own_cotangent[at, :] = v.cotangent_in[c, :, own_lanes]
            low = masked(mt(v.cotangent_in[c], up(mixed_spot)), owner_ref[at, :])
            r.low_four_back[at, :] = low
            v.grad_mixed[at, :] = mm(v.cotangent_in[c], flat(mixed_ref)) + mm(low, up(low_spot))
        done(r.own_cotangent)
        done(r.low_four_back)
        keys_ref = need.keys
        for c in normed_sent:
            c.wait()
        if relayed:
            for a in chunks:
                onward(a, route[a])
        done(r.normed_rows)
        done(r.two_short)

        @pl.loop(0, ranks)
        def _(c):
            at = pl.ds(pl.multiple_of(c * local, local), local)
            normed = r.normed_rows[at, :]
            low = masked(mm(normed, flat(memory_ref)), owner_ref[at, :])
            r.low_three[at, :] = low
            v.asked[at, :] = mm(normed, flat(query_ref)) + mm(low[:, :space], up(query_spot))
            v.gate_pre[at, :] = mm(normed, flat(gate_ref)) + mm(low[:, space:], up(gate_spot))

        done(r.low_three)
        slot = lax.broadcasted_iota(I32, (NKEYS, block), 0)
        for part in range(2):
            top, low = two_parts(v.asked[:, part * half : (part + 1) * half])
            v.every[...] = mt(keys_ref[part], top) + mt(keys_ref[part], low)

            @pl.loop(0, count // block)
            def _(c):
                lanes = pl.ds(pl.multiple_of(c * block, block), block)
                scores = v.every[:, lanes]
                found = []
                for k in range(number):
                    hit = slot == v.picks[rank, part, k : k + 1, lanes]
                    found.append(jnp.sum(jnp.where(hit, scores, 0.0), axis=0, keepdims=True))
                found = jnp.concatenate(found, axis=0)
                if part == 0:
                    r.weights[:, lanes] = found
                else:
                    added = (r.weights[:, lanes] + found) * (2 * half) ** -0.5
                    raised = jnp.exp(added - jnp.max(added, axis=0, keepdims=True))
                    weights = raised / jnp.sum(raised, axis=0, keepdims=True)
                    r.weights[:, lanes] = weights
                    v.narrow[rank, :, lanes] = weights.astype(BF16)

        narrow_sent = [
            near(7, d, v.narrow.at[rank], v.narrow.at[rank]) for d in range(1, ranks)
        ]
        for c in narrow_sent:
            c.start()
        done(r.weights)
        for c in narrow_sent:
            c.wait()
        v.by_token[...] = (
            jnp.concatenate([v.narrow[p] for p in range(ranks)], axis=0).astype(F32).T
        )

        wide_slot = lax.broadcasted_iota(I32, (NKEYS, picks), 0)
        steps = count // sub

        def spread_out(t, s):
            return pltpu.make_async_copy(
                v.spread.at[s],
                dense_out.at[pl.ds(pl.multiple_of(t * sub, sub), sub)],
                moved.at[4 + s],
            )

        @pl.loop(0, steps)
        def _(t):
            s = lax.rem(t, 2)
            at = pl.ds(pl.multiple_of(t * sub, sub), sub)
            firsts, seconds, weights = r.first[at, :], r.second[at, :], v.by_token[at, :]
            for n in range(sub):
                b = jnp.where(wide_slot == seconds[n : n + 1], 1.0, 0.0).astype(BF16)
                a = jnp.where(wide_slot == firsts[n : n + 1], weights[n : n + 1], 0.0).astype(BF16)
                both = mt(a, b)
                v.low[pl.ds(n, NKEYS, stride=stride), :] = both[:, :128]
                v.high[pl.ds(n, NKEYS, stride=stride), :] = both[:, 128:]

            @pl.when(t >= 2)
            def _():
                spread_out(t - 2, s).wait()

            @pl.loop(0, NKEYS // conv)
            def _(c):
                for q in range(conv):
                    i = c * conv + q
                    lanes = pl.multiple_of(i * NKEYS, NKEYS)
                    lines = pl.ds(i * stride, sub)
                    v.spread[s, :, pl.ds(lanes, 128)] = v.low[lines, :].astype(BF16)
                    v.spread[s, :, pl.ds(lanes + 128, 128)] = v.high[lines, :].astype(BF16)

            spread_out(t, s).start()

            @pl.when(t == steps - 9)
            def _():
                other(chunks)
                if relayed:
                    for a in chunks:
                        to_chip(a, 3).start()

        spread_out(steps - 2, steps % 2).wait()
        spread_out(steps - 1, (steps - 1) % 2).wait()

        def block_at(b):
            if not relayed:
                return lax.div(b, 2), lax.rem(b, 2)
            d = lax.div(b, 4)
            across = (2 - 4 * lax.rem(lax.div(group, 2), 2)) * lax.rem(d, 2)
            along = (4 - 8 * lax.div(group, 4)) * lax.div(d, 2)
            near_by = (1 - 2 * lax.rem(group, 2)) * lax.rem(lax.div(b, 2), 2)
            return group + across + along + near_by, lax.rem(b, 2)

        def fetch(b, s):
            p, h = block_at(b)
            return (
                pltpu.make_async_copy(
                    dense_out.at[:, pl.ds(pl.multiple_of((p * 2 + h) * piece, piece), piece)],
                    v.dense_in.at[s],
                    moved.at[6 + s],
                ),
                pltpu.make_async_copy(
                    table_out.at[p, pl.ds(pl.multiple_of(h * piece, piece), piece)],
                    v.table_in.at[s],
                    moved.at[8 + s],
                ),
            )

        def arrived(d):
            for a in chunks:
                if isinstance(d, int) and d == 0:
                    own_copy(a).wait()
                to_sibling(a, d).wait_recv()

        arrived(0)
        if relayed:
            arrived(1)
            arrived(2)
        else:
            last(chunks)

            @pl.loop(1, chips)
            def _(d):
                arrived(d)

        v.total[...] = jnp.zeros_like(v.total)
        v.largest[...] = jnp.zeros_like(v.largest)
        for c in fetch(0, 0):
            c.start()

        @pl.loop(0, blocks)
        def _(b):
            s = lax.rem(b, 2)
            if relayed:

                @pl.when(b == 7)
                def _():
                    last(chunks)

                @pl.when(b == 11)
                def _():
                    arrived(3)

            @pl.when(b + 1 < blocks)
            def _():
                for c in fetch(b + 1, 1 - s):
                    c.start()

            for c in fetch(b, s):
                c.wait()
            v.total[...] += mm(v.dense_in[s], v.table_in[s])
            peak = v.largest[...]
            for c in range(piece // 512):
                values = v.table_in[s, c * 512 : (c + 1) * 512, :].astype(F32)
                squares = values * values
                norms = jnp.sum(squares[:, :128] + squares[:, 128:], axis=1, keepdims=True)
                peak = jnp.maximum(peak, jnp.max(norms.reshape(-1, 8, 1), axis=0))
            v.largest[...] = peak

        gate, recalled, upstream = v.gate_pre[...], v.total[...], v.grad_mixed[...]
        sigmoid = 1.0 / (1.0 + jnp.exp(-gate))
        act = gate * sigmoid
        r.mixed[...] = (act * recalled).astype(BF16)
        grad = (upstream * act).astype(BF16)
        r.grad_recalled[...] = grad
        r.grad_gate[...] = (
            upstream * recalled * sigmoid * (1.0 + gate * (1.0 - sigmoid))
        ).astype(BF16)
        wide = grad.astype(F32)
        bound = jnp.max(v.largest[...]) * jnp.sum(wide * wide, axis=1, keepdims=True)
        r.scale[...] = 32000.0 * lax.rsqrt(jnp.maximum(bound, 1e-30))
        for ref in (r.mixed, r.grad_recalled, r.grad_gate, r.scale):
            done(ref)
        for a in chunks:
            for d in range(4 if relayed else 1):
                to_sibling(a, d).wait_send()
            if relayed:
                for d in range(1, 4):
                    to_chip(a, d).wait_send()
            else:

                @pl.loop(1, chips)
                def _(d):
                    to_sibling(a, d).wait_send()
                    to_chip(a, d).wait_send()

        for name in names:
            getattr(need, name)
        for c in stores:
            c.wait()

    tree_names = [
        next(i for i, y in enumerate(local_arrays) if y is x) for x, _ in tree
    ]
    arrays = [*local_arrays, table, key_picks]
    near_sems = pltpu.SemaphoreType.DMA((8, ranks))
    tree_sems = pltpu.SemaphoreType.DMA((len(route), hops))
    got = pl.pallas_call(
        body,
        out_shape=[jax.ShapeDtypeStruct(shape, dtype) for shape, dtype in outs],
        in_specs=[ANY] * len(arrays),
        out_specs=[ANY] * len(outs),
        scratch_shapes=[pltpu.VMEM(x.shape, x.dtype) for x in local_arrays]
        + [pltpu.VMEM(shape, dtype) for shape, dtype in full]
        + [pltpu.VMEM(shape, dtype) for shape, dtype in results.values()]
        + [pltpu.VMEM(shape, dtype) for shape, dtype in vmem.values()]
        + [
            pltpu.SemaphoreType.DMA((len(names) + 1,)),
            pltpu.SemaphoreType.DMA((len(route),)),
            pltpu.SemaphoreType.DMA((len(outs),)),
            near_sems,
            near_sems,
            tree_sems,
            tree_sems,
            tree_sems,
            tree_sems,
            pltpu.SemaphoreType.DMA((10,)),
        ],
        compiler_params=pltpu.CompilerParams(
            collective_id=cid, has_side_effects=True, vmem_limit_bytes=61 << 20
        ),
    )(*arrays)
    whole_arrays = [x.reshape(-1, x.shape[2]) for x in got[: len(tree)]]
    return whole_arrays, types.SimpleNamespace(**dict(zip(results, got[len(tree) :]))), got[-2]


def pick_grads(first, second, grads, scale, table):
    tokens, picks = first.shape
    width = grads.shape[1]
    per_block = 16
    rows = per_block * NKEYS
    blocks = table.shape[0] // rows

    def body(first_ref, second_ref, grads_ref, scale_ref, table_ref, out_ref, kept):
        step = pl.program_id(0)

        @pl.when(step == 0)
        def _():
            kept[...] = jnp.zeros_like(kept)

        own = first_ref[...]
        low = second_ref[...] & 127
        factor = jnp.broadcast_to(scale_ref[...], (tokens, 128))
        total = kept[...]
        for b in range(per_block):
            every = mt(grads_ref[...], table_ref[b * NKEYS : (b + 1) * NKEYS, :])
            packed = (every[:, 128:] * factor).astype(I32) * 65536 + (
                every[:, :128] * factor
            ).astype(I32)
            found = jnp.take_along_axis(packed, low, axis=1, mode="promise_in_bounds")
            total = jnp.where(own == step * per_block + b, found, total)
        kept[...] = total

        @pl.when(step == blocks - 1)
        def _():
            p = kept[...]
            right = lax.shift_right_arithmetic(lax.shift_left(p, 16), 16)
            left = lax.shift_right_arithmetic(p - right, 16)
            both = jnp.where(second_ref[...] >= 128, left, right).astype(F32) / factor
            out_ref[...] = both.T.astype(BF16)

    return pl.pallas_call(
        body,
        grid=(blocks,),
        out_shape=jax.ShapeDtypeStruct((picks, tokens), BF16),
        in_specs=[whole(x.shape) for x in (first, second, grads, scale)]
        + [pl.BlockSpec((rows, width), lambda s: (s, 0))],
        out_specs=whole((picks, tokens)),
        scratch_shapes=[pltpu.VMEM((tokens, picks), I32)],
        compiler_params=pltpu.CompilerParams(vmem_limit_bytes=48 << 20),
    )(first, second, grads, scale, table)


def by_part(down, parts):
    shaped = down.reshape(down.shape[0], NAD, parts, RANK).transpose(0, 2, 1, 3)
    return shaped.reshape(down.shape)


def add_up(inputs, plans):
    shapes = []
    for x, (axis, sizes) in zip(inputs, plans):
        for size in sizes:
            if isinstance(size, tuple):
                shapes.append((size[0], x.shape[1], size[1]))
            else:
                shapes.append((x.shape[1], size) if axis else (size, x.shape[2]))

    def body(*refs):
        outs = iter(refs[len(inputs) :])
        for ref, (axis, sizes) in zip(refs, plans):

            def total(start, size):
                cut = slice(start, start + size)
                return sum(
                    (ref[p, :, cut] if axis else ref[p, cut, :]).astype(F32)
                    for p in range(ref.shape[0])
                )

            at = 0
            for size in sizes:
                out = next(outs)
                if isinstance(size, tuple):
                    for q in range(size[0]):
                        out[q] = total(at, size[1])
                        at += size[1]
                else:
                    out[...] = total(at, size)
                    at += size

    return stage(body, [(shape, F32) for shape in shapes], inputs)


def make_ready(segments, adapters, project_in, down_input, down_memory, turned, joined, local):
    count = segments.shape[1]
    parts, lines, width = project_in.shape

    def body(segments_ref, adapters_ref, project_ref, input_ref, memory_ref, *refs):
        ins, outs = refs[: len(turned) + len(joined)], refs[len(turned) + len(joined) :]

        def ordered(ref, parts):
            size = NAD * parts * RANK
            row = lax.broadcasted_iota(I32, (size, size), 0)
            column = lax.broadcasted_iota(I32, (size, size), 1)
            part, rest = lax.div(column, NAD * RANK), lax.rem(column, NAD * RANK)
            adapter, rank = lax.div(rest, RANK), lax.rem(rest, RANK)
            came = adapter * (parts * RANK) + part * RANK + rank
            return mm(ref[...], jnp.where(row == came, 1.0, 0.0).astype(BF16)).astype(BF16)

        for p in range(parts):
            outs[0][:, p * width : (p + 1) * width] = project_ref[p]
        outs[1][...] = ordered(input_ref, 3)
        outs[2][...] = ordered(memory_ref, 2)
        for p in range(parts):
            outs[3][:, p * width : (p + 1) * width] = ins[len(turned)][p]
        at = parts * width
        for ref in ins[len(turned) + 1 :]:
            outs[3][:, at : at + ref.shape[1]] = ref[...]
            at += ref.shape[1]
        for ref, out in zip(ins[: len(turned)], outs[4:]):
            out[...] = ref[...].astype(F32).T.astype(BF16)
        owner_ref, below_ref, owner_own_ref = outs[-3:]
        across = jnp.broadcast_to(segments_ref[...], (8, count))
        owner = jnp.zeros_like(across)
        for s in range(adapters.shape[1]):
            owner = jnp.where(across == s, adapters_ref[0:1, s : s + 1], owner)
        owner_ref[...] = owner.T[:, 0:1]
        below_ref[...] = across.T[:, 0:1]
        own = pl.ds(pl.multiple_of(lax.axis_index(TP) * local, local), local)
        owner_own_ref[...] = owner_ref[own, :]

    small = parts * width + sum(x.shape[1] for x in joined[1:])
    return stage(
        body,
        [
            ((lines, parts * width), BF16),
            (down_input.shape, BF16),
            (down_memory.shape, BF16),
            ((joined[1].shape[0], small), BF16),
        ]
        + [(x.shape[::-1], BF16) for x in turned]
        + [((count, 1), I32), ((count, 1), I32), ((local, 1), I32)],
        (segments, adapters, project_in, down_input, down_memory, *turned, *joined),
    )


def on_device(
    inputs,
    cotangent,
    norm_attend,
    norm_memory,
    project_in,
    project_out,
    query_weight,
    gate_weight,
    memory_out,
    half_keys,
    value_table,
    key_picks,
    segment_ids,
    adapter_ids,
    down_input,
    up_input,
    down_attend,
    up_attend,
    down_memory,
    up_query,
    up_gate,
    down_mixed,
    up_mixed,
):
    groups = lax.axis_size(DP)
    ranks = lax.axis_size(TP)
    rank = lax.axis_index(TP)
    local = inputs.shape[0]
    count = segment_ids.shape[0]
    width = project_in.shape[2]
    model = inputs.shape[1]

    across = segment_ids[None, :]
    attend_turned = down_attend.T
    joined = (up_input.transpose(1, 0, 2), up_query, up_gate, up_attend, up_mixed, down_mixed.T)
    turned = (project_out, memory_out)
    if project_out.shape[1] % 128 == 0:
        ready = make_ready(
            across,
            adapter_ids,
            project_in.transpose(1, 0, 2),
            down_input,
            down_memory,
            turned,
            joined,
            local,
        )
        flat_in, parted_input, parted_memory, small, out_turned, mixed_turned = ready[:6]
        owner, below, owner_own = ready[6:]
    else:
        flat_in = project_in.reshape(project_in.shape[0], 3 * width)
        parted_input, parted_memory = by_part(down_input, 3), by_part(down_memory, 2)
        out_turned, mixed_turned = [x.T for x in turned]
        small = jnp.concatenate((up_input.reshape(-1, 3 * width),) + joined[1:], axis=1)
        below = segment_ids[:, None]
        owner = jnp.zeros_like(below)
        for s in range(adapter_ids.shape[1]):
            owner = jnp.where(below == s, adapter_ids[0, s], owner)
        owner_own = lax.dynamic_slice_in_dim(owner, rank * local, local, 0)
    spots, at = [], 0
    for size in (3 * width, up_query.shape[1], width, model, model, width):
        spots.append(slice(at, at + size))
        at += size
    gain_one, gain_two, keys = norm_attend[None, :], norm_memory[None, :], half_keys[0]
    (
        (
            full_in,
            full_down_input,
            ups,
            out_t,
            attend_t,
            full_query,
            full_gate,
            full_down_memory,
            mixed_t,
        ),
        kept,
        table,
    ) = forward(
        dict(
            flat_in=flat_in,
            down_input=parted_input,
            ups=small,
            out_t=out_turned,
            attend_t=attend_turned,
            query=query_weight,
            gate=gate_weight,
            down_memory=parted_memory,
            mixed_t=mixed_turned,
            inputs=inputs,
            cotangent=cotangent,
            gain_one=gain_one,
            gain_two=gain_two,
            owner=owner,
            owner_own=owner_own,
            across=across,
            below=below,
            keys=keys,
        ),
        value_table,
        key_picks,
        spots,
        1,
    )
    mixed = kept.mixed
    partial_mixed = mt(mixed, mixed_t).astype(BF16).reshape(ranks, local, model)

    def block_of(blocks, d):
        return lax.dynamic_index_in_dim(blocks, lax.rem(rank + d, ranks), 0, keepdims=False)

    def turn(d):
        return [(p, (p + d) % ranks) for p in range(ranks)]

    mixed_parts = [block_of(partial_mixed, 0)] + [
        lax.ppermute(block_of(partial_mixed, d), TP, turn(d)) for d in range(1, ranks)
    ]
    picked = pick_grads(
        kept.first, kept.second, kept.grad_recalled, kept.scale, table.reshape(-1, width)
    )
    picked, mixed_parts = lax.optimization_barrier((picked, mixed_parts))
    given = dict(
        picked=picked.reshape(ranks, -1, count),
        weights=kept.weights,
        keys=keys,
        picks=lax.dynamic_index_in_dim(key_picks, rank, 0, keepdims=False),
        query=full_query,
        gate=full_gate,
        ups=ups,
        grad_gate=kept.grad_gate,
        mixed=mixed,
        owner=owner,
        owner_own=owner_own,
        middle=kept.middle,
        cotangent=cotangent,
        gain_two=gain_two,
        down_memory=full_down_memory,
        out_t=out_t,
        attend_t=attend_t,
        low_three=kept.low_three,
        own_cotangent=kept.own_cotangent,
        low_four_back=kept.low_four_back,
        normed_rows=kept.normed_rows,
        projected=kept.projected,
        across=across,
        below=below,
        full_in=full_in,
        low_one=kept.low_one,
        attended=kept.attended,
        two_short=kept.two_short,
        down_input=full_down_input,
        inputs=inputs,
        gain_one=gain_one,
        normed_one=kept.normed_one,
    )
    wides, (outputs, input_grad, up_parts, memory_parts, down_parts) = backward(
        given, mixed_parts, spots, 5
    )
    (
        grad_up_input,
        grad_up_query,
        grad_up_gate,
        grad_up_mixed,
        grad_down_attend,
        grad_down_mixed,
        grad_up_attend,
        grad_down_memory,
        grad_down_input,
    ) = add_up(
        (up_parts, memory_parts, down_parts),
        (
            (1, ((3, width), *wides[3:])),
            (0, (memory_parts.shape[1],)),
            (0, (down_parts.shape[1],)),
        ),
    )
    return (
        outputs,
        input_grad,
        grad_down_input.T,
        grad_up_input.transpose(1, 0, 2),
        grad_down_attend.T,
        grad_up_attend,
        grad_down_memory.T,
        grad_up_query,
        grad_up_gate,
        grad_down_mixed.T,
        grad_up_mixed,
    )


def solution(mesh):
    rows = P((DP, TP), None)
    both = P(DP, TP)
    wide = P(DP, None)
    turned = P(TP, DP)
    split = P(DP, None, TP)
    return jax.shard_map(
        on_device,
        mesh=mesh,
        in_specs=(
            rows,
            rows,
            P(),
            P(),
            split,
            turned,
            both,
            both,
            turned,
            P(TP, None, None, None),
            both,
            P(None, None, None, DP),
            P(DP),
            wide,
            wide,
            split,
            turned,
            wide,
            wide,
            both,
            both,
            turned,
            wide,
        ),
        out_specs=(rows, rows, both, split, turned, both, both, both, both, turned, both),
        check_vma=False,
    )
```

time: 591 us -> 382 us (0.65); the launches traced: 583 us -> 380 us
  Pallas kernels: 456 us -> 363 us
  matrix products: 55.9 us -> 1.59 us
  other arithmetic: 32.1 us -> 0 us
  between operations: 15.7 us -> 0.76 us
  local copies, waits for them, and re-layouts: 22.1 us -> 13.8 us
    pallas_call x15 -> x4, Pallas kernels: 403 us -> 311 us  [the longest x1 211 us: forward(): pl.pallas_call(body, out_shape=[jax.ShapeDtypeStruct(shape, dtype) for sh...]
    dot_general x32 -> x0, matrix products: 32.2 us -> none  [the longest x21 22.7 us: mm(): lax.dot_general(a, b, (((1,), (0,)), ((), ())), preferred_element_type=F32)]
    dot_general x16 -> x1, matrix products: 23.7 us -> 1.59 us  [mt(): lax.dot_general(a, b, (((1,), (1,)), ((), ())), preferred_element_type=F32)]
    reduce_sum x12 -> x0, other arithmetic: 14.3 us -> none  [the longest x1 3.39 us: on_device(): largest = jnp.max(jnp.sum(jnp.square(value_table.astype(F32)), axis=1))]
    convert_element_type x8 -> x0, other arithmetic: 7.84 us -> none  [the longest x2 4.15 us: on_device(): normed_one = rms_forward(input_rows.astype(F32), gain_one).astype(BF16)]
  transfers between devices with their start and end apart: 1 -> 3, of which waited for: 0 -> 0; matrix products, arithmetic and copies ran while one was open for 8% -> 0% of each run, Pallas kernels for 36% -> 14%
where the time goes in v2:
time: 382 us; the launch traced here: 380 us
  Pallas kernels  363 us (95%)
  local copies, waits for them, and re-layouts  13.8 us (4%)
    pallas_call x1, Pallas kernels, forward(): pl.pallas_call(body, out_shape=[jax.ShapeDtypeStruct(shape, dtype) for sh...  211 us
    pallas_call x1, Pallas kernels, backward(): pl.pallas_call(body, out_shape=[jax.ShapeDtypeStruct(shape, dtype) for sh...  95.7 us
    pallas_call x1, Pallas kernels, pick_grads(): pl.pallas_call(body, grid=(blocks,), out_shape=jax.ShapeDtypeStruct((pick...  51.6 us
    unnamed x18, local copies, waits for them, and re-layouts  8.89 us
  transfers between devices with their start and end apart: 3, of which 0 were waited for; matrix products, arithmetic and copies ran while one was open for 0% of the time, Pallas kernels for 14%

profile of v2, /device:TPU:9, one launch (start us, length us, event | category | flops | bytes accessed | tf_op | source)
XLA Modules:
  0.0 380.4 jit_solution(11392802710225300989)
XLA Ops:
  0.7 1.3 broadcast_in_dim.10.refs_11_.refs_30_
  1.9 1.3 broadcast_in_dim.11.refs_12_.refs_13_
  3.2 2.4 shard_map.302
  5.6 211.1 %shard_map.303 = (bf16[8,128,768]{2,1,0:T(8,128)(2,1)}, bf16[8,128,384]{2,1,0:T(8,128)(2,1)}, bf16[8,16,3840]{2,1,0:T(8,128)(2,1)}, bf16[8,128,1024]{2,1,0:T(8,1...) custom-call(bf16[128,768]{1,0:T(8,128)(2,1)} %get-tuple-element.66.r, ...), custom_call_target="tpu_custom_call" | custom-call | tf_op jit(solution)/shard_map/pallas_call | solution.py:1167
  216.7 1.6 convolution_convert_fusion
  218.3 0.8 dynamic-slice_bitcast_fusion
  219.1 0.0 collective-permute-start
  219.1 0.0 collective-permute-start.1
  219.1 1.5 collective-permute-start.2
  220.6 0.0 copy-start.1
  220.6 0.9 copy-done.1
  221.5 0.0 copy-start.2
  221.5 0.9 copy-done.2
  222.5 0.0 copy-start.3
  222.5 0.9 copy-done.3
  223.4 0.0 copy-start.4
  223.4 0.9 copy-done.4
  224.4 51.6 %shard_map.304 = bf16[128,512]{1,0:T(8,128)(2,1)S(1)} custom-call(s32[512,128]{1,0:T(8,128)S(1)} %copy-done.3, s32[512,128]{1,0:T(8,128)S(1)} %copy-done.4, bf16[512,256]{1,0:T(8,128)(2,1)S(1)} %copy-done.1, f32[512,1]{1,0:T(8,128)S(1)} %copy-done.2, bf16[65536,256]{1,0:T(8,128)(2,1)} %bitcast.36), custom_call_target="tpu_custom_call" | custom-call | tf_op jit(solution)/shard_map/pallas_call | solution.py:1231
  276.0 0.0 copy-start
  276.0 0.6 copy-done
  276.7 1.5 dynamic-slice_bitcast_fusion.4.refs_3_
  278.2 0.0 collective-permute-done.refs_33_
  278.2 0.0 copy-start.5
  278.2 0.0 collective-permute-done.1.refs_34_
  278.2 0.0 copy-start.6
  278.2 0.0 collective-permute-done.2.refs_35_
  278.2 0.0 copy-start.7
  278.2 0.7 copy-done.5
  278.9 0.1 copy-done.6
  279.0 0.1 copy-done.7
  279.1 95.7 %shard_map.305 = (bf16[128,1024]{1,0:T(8,128)(2,1)}, f32[128,1024]{1,0:T(8,128)}, bf16[8,16,2560]{2,1,0:T(8,128)(2,1)}, bf16[8,64,128]{2,1,0:T(8,128)(2,1)}, bf16[8,96,128]{2,1,0:T(8,128)(2,1)}) custom-call(bf16[4,32,512]{2,1,0:T(8,128)(2,1)} %bitcast.35, f32[32,512]{1,0:T(8,128)} %get-tuple-element.83.refs_1_, bf16[2,256,256]{2,1,0:T(8,128)(2,1)} %bitcast.41, ...), custom_call_target="tpu_custom_call" | custom-call | tf_op jit(solution)/shard_map/pallas_call | solution.py:496
  374.9 1.9 shard_map.306
  376.8 1.7 copy.36
  378.5 1.9 copy.37
Async XLA Ops:
  219.1 59.1 %collective-permute-start = (bf16[128,1024]{1,0:T(8,128)(2,1)S(1)}, bf16[128,1024]{1,0:T(8,128)(2,1)S(1)}, u32[]{:S(2)}, u32[]{:S(2)}) collective-permute-start(bf16[128,1024]{1,0:T(8,128)(2,1)S(1)} %get-tuple-element.123), channel_id=1, source_target_pairs={{0,1},{1,2},{2,3},{3,0},{4,5},{5,6},{6,7},{7,4},{8,9},{9,10},{10,1... | collective-permute-start | bytes 786440 | tf_op jit(solution)/shard_map/ppermute | solution.py:1450
  219.1 59.1 %collective-permute-start.1 = (bf16[128,1024]{1,0:T(8,128)(2,1)S(1)}, bf16[128,1024]{1,0:T(8,128)(2,1)S(1)}, u32[]{:S(2)}, u32[]{:S(2)}) collective-permute-start(bf16[128,1024]{1,0:T(8,128)(2,1)S(1)} %get-tuple-element.122), channel_id=1, source_target_pairs={{0,2},{1,3},{2,0},{3,1},{4,6},{5,7},{6,4},{7,5},{8,10},{9,11},{10,... | collective-permute-start | bytes 786440 | tf_op jit(solution)/shard_map/ppermute | solution.py:1450
  219.1 59.1 %collective-permute-start.2 = (bf16[128,1024]{1,0:T(8,128)(2,1)S(1)}, bf16[128,1024]{1,0:T(8,128)(2,1)S(1)}, u32[]{:S(2)}, u32[]{:S(2)}) collective-permute-start(bf16[128,1024]{1,0:T(8,128)(2,1)S(1)} %get-tuple-element.121), channel_id=1, source_target_pairs={{0,3},{1,0},{2,1},{3,2},{4,7},{5,4},{6,5},{7,6},{8,11},{9,8},{10,9... | collective-permute-start | bytes 786440 | tf_op jit(solution)/shard_map/ppermute | solution.py:1450
  220.6 0.9 copy-start.1
  221.5 0.9 copy-start.2
  222.5 0.9 copy-start.3
  223.4 0.9 copy-start.4
  276.0 0.7 copy-start
  278.2 0.7 copy-start.5
  278.2 0.8 copy-start.6
  278.2 0.9 copy-start.7

commit v3 on v2

--- a/solution.py
+++ b/solution.py
@@ -40,7 +40,7 @@
     return pl.BlockSpec(shape, lambda *_: (0,) * len(shape))
 
 
-def stage(body, outs, ins, scratch=(), limit=56):
+def stage(body, outs, ins, scratch=(), limit=61):
     return pl.pallas_call(
         body,
         grid=(1,),
@@ -211,7 +211,10 @@
             )
 
         loads = [
-            pltpu.make_async_copy(refs[i + 1], rest[i], loaded.at[i]) for i in range(len(inputs))
+            pltpu.make_async_copy(
+                refs[i + 1].at[rank] if x is shown.picks else refs[i + 1], rest[i], loaded.at[i]
+            )
+            for i, x in enumerate(inputs)
         ]
         for load in loads:
             load.start()
@@ -341,7 +344,7 @@
         grad_three = lengthen(v.three_sum[:, own_tokens], owner_own)
         upstream = total(v.normed_in) + mt(grad_three, down_ref[...])
         grad = cotangent_ref[...].astype(F32) + rms_backward(
-            middle_ref[...], gain_two[...].astype(F32), upstream
+            middle_ref[...], gain_two[...].astype(F32)[None, :], upstream
         )
         v.grad_middle[...] = grad
         branch = grad.astype(BF16)
@@ -478,7 +481,7 @@
         low = lengthen(v.one_sum[:, own_tokens], owner_own)
         upstream = total(v.input_in) + mt(low, down_input_ref[...])
         v.input_grad[...] = v.grad_middle[...] + rms_backward(
-            rows_ref[...].astype(F32), gain_one[...].astype(F32), upstream
+            rows_ref[...].astype(F32), gain_one[...].astype(F32)[None, :], upstream
         )
         stores.append(pltpu.make_async_copy(v.input_grad, outs[1], saved.at[1]))
         stores[1].start()
@@ -498,7 +501,9 @@
         out_shape=[jax.ShapeDtypeStruct(shape, dtype) for shape, dtype in results],
         in_specs=[ANY] * len(arrays),
         out_specs=[ANY] * len(results),
-        scratch_shapes=[pltpu.VMEM(x.shape, x.dtype) for x in inputs]
+        scratch_shapes=[
+            pltpu.VMEM(x.shape[1:] if x is shown.picks else x.shape, x.dtype) for x in inputs
+        ]
         + [pltpu.VMEM(shape, dtype) for shape, dtype in vmem.values()]
         + [
             pltpu.SemaphoreType.DMA((len(inputs),)),
@@ -509,7 +514,7 @@
             far_sems,
         ],
         compiler_params=pltpu.CompilerParams(
-            collective_id=cid, has_side_effects=True, vmem_limit_bytes=58 << 20
+            collective_id=cid, has_side_effects=True, vmem_limit_bytes=61 << 20
         ),
     )(*arrays)
 
@@ -535,22 +540,21 @@
     relayed = chips == 4
     hops = max(chips, 4)
     tree = [
-        (shown.flat_in, 1),
-        (shown.down_input, 2),
-        (shown.ups, 2),
-        (shown.out_t, 1),
-        (shown.attend_t, 2),
-        (shown.query, 2),
-        (shown.gate, 1),
-        (shown.down_memory, 1),
-        (shown.mixed_t, 1),
+        shown.flat_in,
+        shown.down_input,
+        shown.ups,
+        shown.out_t,
+        shown.attend_t,
+        shown.query,
+        shown.gate,
+        shown.down_memory,
+        shown.mixed_t,
     ]
     early, nested, late = (0, 1, 2), (3, 4), (5, 6, 7, 8)
-    cuts = 8
+    cuts = 2
     chunks = tuple(range(len(tree), len(tree) + cuts))
-    route = [way for _, way in tree] + [1] * (cuts // 2) + [2] * (cuts // 2)
     tree_shapes = [
-        (x.shape[0], x.shape[1] * (ranks if a in nested else 1)) for a, (x, _) in enumerate(tree)
+        (x.shape[0], x.shape[1] * (ranks if a in nested else 1)) for a, x in enumerate(tree)
     ]
     full = [((groups, *shape), BF16) for shape in tree_shapes]
     results = dict(
@@ -660,6 +664,9 @@
         def columns(ref, p, wide):
             return ref.at[:, pl.ds(pl.multiple_of(p * wide, wide), wide)]
 
+        def way(a):
+            return 1 if a - len(tree) < cuts // 2 else 2
+
         def cut_of(a):
             return pl.ds((a - len(tree)) * (rows // cuts), rows // cuts)
 
@@ -690,14 +697,14 @@
             return partner(d) if relayed else lax.rem(group - 2 * d + groups, groups)
 
         def to_chip(a, d):
-            relay = relayed and d == 3
-            shard = place(a, holder(route[a])) if relay else source(a)
+            relay = relayed and a in chunks and d == 3
+            shard = place(a, holder(way(a))) if relay else source(a)
             return pltpu.make_async_remote_copy(
                 src_ref=shard,
                 dst_ref=shard if relay else place(a, group),
                 send_sem=tree_send.at[a, d],
                 recv_sem=tree_recv.at[a, d],
-                device_id={DP: partner(3 - route[a] if relay else d)},
+                device_id={DP: partner(3 - way(a) if relay else d)},
                 device_id_type=MESH,
             )
 
@@ -719,8 +726,8 @@
             for a in chosen:
                 own_copy(a).start()
                 if relayed:
-                    to_chip(a, 1).start()
-                    to_chip(a, 2).start()
+                    for d in range(1, 4):
+                        to_chip(a, d).start()
                 else:
 
                     @pl.loop(1, chips)
@@ -734,30 +741,23 @@
                 begin(chosen)
                 return
             for a in chosen:
-                to_chip(a, route[a]).start()
+                to_chip(a, way(a)).start()
+                own_copy(a).start()
+                to_sibling(a, 0).start()
 
         def rest_of_table(chosen):
             if relayed:
                 for a in chosen:
-                    to_chip(a, 3 - route[a]).start()
-                for a in chosen:
-                    own_copy(a).start()
-                    to_sibling(a, 0).start()
+                    to_chip(a, 3 - way(a)).start()
 
         def onward(a, d):
             to_chip(a, d).wait_recv()
             to_sibling(a, d).start()
 
-        def relay(chosen):
-            if relayed:
-                for a in chosen:
-                    onward(a, route[a])
-                    to_chip(a, 3).start()
-
         def other(chosen):
             if relayed:
                 for a in chosen:
-                    onward(a, 3 - route[a])
+                    onward(a, 3 - way(a))
 
         def last(chosen):
             for a in chosen:
@@ -768,6 +768,13 @@
                     @pl.loop(1, chips)
                     def _(d):
                         onward(a, d)
+
+        def collect(chosen):
+            if relayed:
+                for d in range(1, 3):
+                    for a in chosen:
+                        onward(a, d)
+            last(chosen)
 
         def settle(chosen):
             for a in chosen:
@@ -824,30 +831,25 @@
         for c in nest_sent + rows_sent:
             c.start()
         begin(early)
+        begin(late)
         for c in nest_sent:
             c.wait()
         homes[2].wait()
         homes[3].wait()
         begin(nested)
-        begin(late)
+        begin_table(chunks)
         gain_one, owner_ref = need.gain_one, need.owner
         homes[0].wait()
         for c in rows_sent:
             c.wait()
         for c in range(ranks):
             r.normed_one[c * local : (c + 1) * local, :] = rms_forward(
-                v.rows_in[c].astype(F32), gain_one[...].astype(F32)
+                v.rows_in[c].astype(F32), gain_one[...].astype(F32)[None, :]
             ).astype(BF16)
         done(r.normed_one)
         for c in back_sent:
             c.start()
-        relay(early)
-        other(early)
-        relay(nested)
-        relay(late)
-        last(early)
-        begin_table(chunks)
-        rest_of_table(chunks)
+        collect(early)
         settle(early)
         store_trees(early)
         weight_ref, down_ref, ups_ref = gathered[:3]
@@ -894,13 +896,13 @@
         ]
         for c in attended_sent:
             c.start()
+        rest_of_table(chunks)
         own_rows = pl.ds(pl.multiple_of(rank * local, local), local)
         v.attended_in[:, pl.ds(pl.multiple_of(rank * width, width), width)] = r.attended[own_rows, :]
         done(r.low_one)
         done(r.projected)
         done(r.attended)
-        other(nested)
-        last(nested)
+        collect(nested)
         settle(nested)
         store_trees(nested)
         out_ref, attend_ref = gathered[3:5]
@@ -914,7 +916,7 @@
             + mm(low, up(attend_spot))
         )
         r.middle[...] = middle
-        normed = rms_forward(middle, gain_two[...].astype(F32)).astype(BF16)
+        normed = rms_forward(middle, gain_two[...].astype(F32)[None, :]).astype(BF16)
         v.normed_two[...] = normed
         r.normed_rows[own_rows, :] = normed
         r.two_short[rank] = shorten(low)
@@ -933,8 +935,7 @@
         ).T
         done(r.first)
         done(r.second)
-        other(late)
-        last(late)
+        collect(late)
         settle(late)
         store_trees(late)
         query_ref, gate_ref, memory_ref, mixed_ref = gathered[5:]
@@ -955,7 +956,8 @@
             c.wait()
         if relayed:
             for a in chunks:
-                onward(a, route[a])
+                onward(a, way(a))
+                to_chip(a, 3).start()
         done(r.normed_rows)
         done(r.two_short)
 
@@ -1041,12 +1043,9 @@
 
             spread_out(t, s).start()
 
-            @pl.when(t == steps - 9)
+            @pl.when(t == steps - 7)
             def _():
                 other(chunks)
-                if relayed:
-                    for a in chunks:
-                        to_chip(a, 3).start()
 
         spread_out(steps - 2, steps % 2).wait()
         spread_out(steps - 1, (steps - 1) % 2).wait()
@@ -1102,11 +1101,11 @@
             s = lax.rem(b, 2)
             if relayed:
 
-                @pl.when(b == 7)
+                @pl.when(b == 11)
                 def _():
                     last(chunks)
 
-                @pl.when(b == 11)
+                @pl.when(b == 13)
                 def _():
                     arrived(3)
 
@@ -1159,11 +1158,11 @@
             c.wait()
 
     tree_names = [
-        next(i for i, y in enumerate(local_arrays) if y is x) for x, _ in tree
+        next(i for i, y in enumerate(local_arrays) if y is x) for x in tree
     ]
     arrays = [*local_arrays, table, key_picks]
     near_sems = pltpu.SemaphoreType.DMA((8, ranks))
-    tree_sems = pltpu.SemaphoreType.DMA((len(route), hops))
+    tree_sems = pltpu.SemaphoreType.DMA((len(tree) + cuts, hops))
     got = pl.pallas_call(
         body,
         out_shape=[jax.ShapeDtypeStruct(shape, dtype) for shape, dtype in outs],
@@ -1175,7 +1174,7 @@
         + [pltpu.VMEM(shape, dtype) for shape, dtype in vmem.values()]
         + [
             pltpu.SemaphoreType.DMA((len(names) + 1,)),
-            pltpu.SemaphoreType.DMA((len(route),)),
+            pltpu.SemaphoreType.DMA((len(tree) + cuts,)),
             pltpu.SemaphoreType.DMA((len(outs),)),
             near_sems,
             near_sems,
@@ -1200,12 +1199,19 @@
     rows = per_block * NKEYS
     blocks = table.shape[0] // rows
 
-    def body(first_ref, second_ref, grads_ref, scale_ref, table_ref, out_ref, kept):
+    def body(*refs):
+        table_ref, out_ref, kept, sems = refs[4], refs[5], refs[6], refs[11]
+        first_ref, second_ref, grads_ref, scale_ref = refs[7:11]
         step = pl.program_id(0)
 
         @pl.when(step == 0)
         def _():
+            copies = [pltpu.make_async_copy(refs[i], refs[7 + i], sems.at[i]) for i in range(4)]
+            for c in copies:
+                c.start()
             kept[...] = jnp.zeros_like(kept)
+            for c in copies:
+                c.wait()
 
         own = first_ref[...]
         low = second_ref[...] & 127
@@ -1232,11 +1238,12 @@
         body,
         grid=(blocks,),
         out_shape=jax.ShapeDtypeStruct((picks, tokens), BF16),
-        in_specs=[whole(x.shape) for x in (first, second, grads, scale)]
-        + [pl.BlockSpec((rows, width), lambda s: (s, 0))],
+        in_specs=[ANY] * 4 + [pl.BlockSpec((rows, width), lambda s: (s, 0))],
         out_specs=whole((picks, tokens)),
-        scratch_shapes=[pltpu.VMEM((tokens, picks), I32)],
-        compiler_params=pltpu.CompilerParams(vmem_limit_bytes=48 << 20),
+        scratch_shapes=[pltpu.VMEM((tokens, picks), I32)]
+        + [pltpu.VMEM(x.shape, x.dtype) for x in (first, second, grads, scale)]
+        + [pltpu.SemaphoreType.DMA((4,))],
+        compiler_params=pltpu.CompilerParams(vmem_limit_bytes=61 << 20),
     )(first, second, grads, scale, table)
 
 
@@ -1245,7 +1252,7 @@
     return shaped.reshape(down.shape)
 
 
-def add_up(inputs, plans):
+def add_up(inputs, plans, through):
     shapes = []
     for x, (axis, sizes) in zip(inputs, plans):
         for size in sizes:
@@ -1255,7 +1262,9 @@
                 shapes.append((x.shape[1], size) if axis else (size, x.shape[2]))
 
     def body(*refs):
-        outs = iter(refs[len(inputs) :])
+        outs = iter(refs[len(inputs) + len(through) :])
+        for ref in refs[len(inputs) : len(inputs) + len(through)]:
+            next(outs)[...] = ref[...]
         for ref, (axis, sizes) in zip(refs, plans):
 
             def total(start, size):
@@ -1276,7 +1285,8 @@
                     out[...] = total(at, size)
                     at += size
 
-    return stage(body, [(shape, F32) for shape in shapes], inputs)
+    kept = [(x.shape, x.dtype) for x in through]
+    return stage(body, kept + [(shape, F32) for shape in shapes], (*inputs, *through))
 
 
 def make_ready(segments, adapters, project_in, down_input, down_memory, turned, joined, local):
@@ -1396,7 +1406,7 @@
     for size in (3 * width, up_query.shape[1], width, model, model, width):
         spots.append(slice(at, at + size))
         at += size
-    gain_one, gain_two, keys = norm_attend[None, :], norm_memory[None, :], half_keys[0]
+    gain_one, gain_two, keys = norm_attend, norm_memory, half_keys[0]
     (
         (
             full_in,
@@ -1457,7 +1467,7 @@
         picked=picked.reshape(ranks, -1, count),
         weights=kept.weights,
         keys=keys,
-        picks=lax.dynamic_index_in_dim(key_picks, rank, 0, keepdims=False),
+        picks=key_picks,
         query=full_query,
         gate=full_gate,
         ups=ups,
@@ -1491,6 +1501,8 @@
         given, mixed_parts, spots, 5
     )
     (
+        outputs,
+        input_grad,
         grad_up_input,
         grad_up_query,
         grad_up_gate,
@@ -1507,6 +1519,7 @@
             (0, (memory_parts.shape[1],)),
             (0, (down_parts.shape[1],)),
         ),
+        (outputs, input_grad),
     )
     return (
         outputs,

time: 382 us -> 364 us (0.953)
  local copies, waits for them, and re-layouts: 13.8 us -> 1.65 us
  Pallas kernels: 363 us -> 354 us
    pallas_call x1, Pallas kernels: 211 us -> 202 us  [forward(): pl.pallas_call(body, out_shape=[jax.ShapeDtypeStruct(shape, dtype) for sh...]
    unnamed x18 -> x6, local copies, waits for them, and re-layouts: 8.89 us -> 0.88 us
  transfers between devices with their start and end apart: 3 -> 3, of which waited for: 0 -> 0; matrix products, arithmetic and copies ran while one was open for 0% -> 0% of each run, Pallas kernels for 14% -> 15%
where the time goes in v3:
time: 364 us; the launch traced here: 362 us
  Pallas kernels  354 us (97%)
    pallas_call x1, Pallas kernels, forward(): pl.pallas_call(body, out_shape=[jax.ShapeDtypeStruct(shape, dtype) for sh...  202 us
    pallas_call x1, Pallas kernels, backward(): pl.pallas_call(body, out_shape=[jax.ShapeDtypeStruct(shape, dtype) for sh...  93.6 us
    pallas_call x1, Pallas kernels, pick_grads(): pl.pallas_call(body, grid=(blocks,), out_shape=jax.ShapeDtypeStruct((pick...  53.6 us
  transfers between devices with their start and end apart: 3, of which 0 were waited for; matrix products, arithmetic and copies ran while one was open for 0% of the time, Pallas kernels for 15%

profile of v3, /device:TPU:9, one launch (start us, length us, event | category | flops | bytes accessed | tf_op | source)
XLA Modules:
  0.0 361.8 jit_solution(11501053788297060525)
XLA Ops:
  0.7 2.4 shard_map.302
  3.1 202.2 %shard_map.303 = (bf16[8,128,768]{2,1,0:T(8,128)(2,1)}, bf16[8,128,384]{2,1,0:T(8,128)(2,1)}, bf16[8,16,3840]{2,1,0:T(8,128)(2,1)}, bf16[8,128,1024]{2,1,0:T(8,1...) custom-call(bf16[128,768]{1,0:T(8,128)(2,1)} %get-tuple-element.68.r, ...), custom_call_target="tpu_custom_call" | custom-call | tf_op jit(solution)/shard_map/pallas_call | solution.py:1166
  205.3 1.6 convolution_convert_fusion
  207.0 0.8 dynamic-slice_bitcast_fusion
  207.7 0.9 collective-permute-start
  208.6 2.4 collective-permute-start.1
  211.0 0.1 collective-permute-start.2
  211.1 53.6 %shard_map.304 = bf16[128,512]{1,0:T(8,128)(2,1)} custom-call(s32[512,128]{1,0:T(8,128)} %get-tuple-element.77.refs_0_, s32[512,128]{1,0:T(8,128)} %get-tuple-element.78.refs_1_, bf16[512,256]{1,0:T(8,128)(2,1)} %get-tuple-element.79.refs_2_, f32[512,1]{1,0:T(8,128)} %get-tuple-element.80.refs_3_, bf16[65536,256]{1,0:T(8,128)(2,1)} %bitcast.33), custom_call_target="tpu_custom_call" | custom-call | tf_op jit(solution)/shard_map/pallas_call | solution.py:1237
  264.7 0.0 collective-permute-done.refs_33_
  264.7 0.0 copy-start
  264.7 0.0 collective-permute-done.1.refs_34_
  264.8 0.0 copy-start.1
  264.8 0.0 collective-permute-done.2.refs_35_
  264.8 0.0 copy-start.2
  264.8 0.7 copy-done
  265.4 0.1 copy-done.1
  265.6 0.1 copy-done.2
  265.7 93.6 %shard_map.305 = (bf16[128,1024]{1,0:T(8,128)(2,1)}, f32[128,1024]{1,0:T(8,128)}, bf16[8,16,2560]{2,1,0:T(8,128)(2,1)}, bf16[8,64,128]{2,1,0:T(8,128)(2,1)}, bf16[8,96,128]{2,1,0:T(8,128)(2,1)}) custom-call(bf16[4,32,512]{2,1,0:T(8,128)(2,1)} %bitcast.42, f32[32,512]{1,0:T(8,128)} %get-tuple-element.85.refs_1_, bf16[2,256,256]{2,1,0:T(8,128)(2,1)} %bitcast.38, ...), custom_call_target="tpu_custom_call" | custom-call | tf_op jit(solution)/shard_map/pallas_call | solution.py:499
  359.2 2.4 shard_map.306
Async XLA Ops:
  207.7 57.0 %collective-permute-start = (bf16[128,1024]{1,0:T(8,128)(2,1)S(1)}, bf16[128,1024]{1,0:T(8,128)(2,1)S(1)}, u32[]{:S(2)}, u32[]{:S(2)}) collective-permute-start(bf16[128,1024]{1,0:T(8,128)(2,1)S(1)} %get-tuple-element.127), channel_id=1, source_target_pairs={{0,1},{1,2},{2,3},{3,0},{4,5},{5,6},{6,7},{7,4},{8,9},{9,10},{10,1... | collective-permute-start | bytes 786440 | tf_op jit(solution)/shard_map/ppermute | solution.py:1460
  208.6 56.1 %collective-permute-start.1 = (bf16[128,1024]{1,0:T(8,128)(2,1)S(1)}, bf16[128,1024]{1,0:T(8,128)(2,1)S(1)}, u32[]{:S(2)}, u32[]{:S(2)}) collective-permute-start(bf16[128,1024]{1,0:T(8,128)(2,1)S(1)} %get-tuple-element.126), channel_id=1, source_target_pairs={{0,2},{1,3},{2,0},{3,1},{4,6},{5,7},{6,4},{7,5},{8,10},{9,11},{10,... | collective-permute-start | bytes 786440 | tf_op jit(solution)/shard_map/ppermute | solution.py:1460
  211.0 53.8 %collective-permute-start.2 = (bf16[128,1024]{1,0:T(8,128)(2,1)S(1)}, bf16[128,1024]{1,0:T(8,128)(2,1)S(1)}, u32[]{:S(2)}, u32[]{:S(2)}) collective-permute-start(bf16[128,1024]{1,0:T(8,128)(2,1)S(1)} %get-tuple-element.125), channel_id=1, source_target_pairs={{0,3},{1,0},{2,1},{3,2},{4,7},{5,4},{6,5},{7,6},{8,11},{9,8},{10,9... | collective-permute-start | bytes 786440 | tf_op jit(solution)/shard_map/ppermute | solution.py:1460
  264.7 0.7 copy-start
  264.8 0.8 copy-start.1
  264.8 0.9 copy-start.2

commit v4 on v3

--- a/solution.py
+++ b/solution.py
@@ -309,7 +309,7 @@
         query_ref, gate_ref, ups_ref = need.query, need.gate, need.ups
         grad_gate_ref, mixed_ref, owner_ref = need.grad_gate, need.mixed, need.owner
         normed_sent = []
-        for d in list(range(1, ranks)) + [0]:
+        for d in [ranks // 2] + [d for d in range(1, ranks) if d != ranks // 2] + [0]:
             at = pl.ds(pl.multiple_of(lax.rem(rank + d, ranks) * local, local), local)
             asked, gates, own = v.grad_query[at, :], grad_gate_ref[at, :], owner_ref[at, :]
             part = (mt(asked, query_ref[...]) + mt(gates, gate_ref[...])).astype(BF16)
@@ -356,7 +356,7 @@
         v.branch_in[rank] = v.branch_out[:, own_columns_at]
         attended_sent = split(4, v.attended_out, v.attended_in)
         later_sent = shared(5, v.back_in) + split(6, v.branch_out, v.branch_in)
-        for c in attended_sent + later_sent:
+        for c in attended_sent:
             c.start()
 
         low_four = lengthen(v.four_sum[:, own_tokens], owner_own)
@@ -396,6 +396,8 @@
         weight_ref = need.full_in
         for c in attended_sent:
             c.wait()
+        for c in later_sent:
+            c.start()
 
         @pl.loop(0, width // (2 * HD))
         def _(pair):
@@ -430,7 +432,7 @@
             ).astype(BF16)
 
         input_sent = []
-        for d in list(range(1, ranks)) + [0]:
+        for d in [ranks // 2] + [d for d in range(1, ranks) if d != ranks // 2] + [0]:
             at = pl.ds(pl.multiple_of(lax.rem(rank + d, ranks) * local, local), local)
             part = mt(v.grads[at, :], weight_ref[...]).astype(BF16)
             if d:
@@ -575,6 +577,10 @@
         own_cotangent=((count, width), BF16),
         first=((count, picks), I32),
         second=((count, picks), I32),
+        block_0=((local, model), BF16),
+        block_1=((local, model), BF16),
+        block_2=((local, model), BF16),
+        block_3=((local, model), BF16),
     )
     vmem = dict(
         rows_in=((ranks, local, model), BF16),
@@ -590,8 +596,8 @@
         grad_mixed=((count, width), F32),
         picks=(key_picks.shape, I32),
         by_token=((count, picks), F32),
-        low=((NKEYS * stride, 128), F32),
-        high=((NKEYS * stride, 128), F32),
+        low=((NKEYS * stride + sub, 128), F32),
+        high=((NKEYS * stride + sub, 128), F32),
         spread=((2, sub, NKEYS * NKEYS), BF16),
         dense_in=((2, count, piece), BF16),
         table_in=((2, piece, width), BF16),
@@ -1139,6 +1145,10 @@
         r.scale[...] = 32000.0 * lax.rsqrt(jnp.maximum(bound, 1e-30))
         for ref in (r.mixed, r.grad_recalled, r.grad_gate, r.scale):
             done(ref)
+        for d, ref in enumerate((r.block_0, r.block_1, r.block_2, r.block_3)):
+            at = pl.ds(pl.multiple_of(lax.rem(rank + d, ranks) * local, local), local)
+            ref[...] = mt(r.mixed[at, :], flat(mixed_ref)).astype(BF16)
+            done(ref)
         for a in chunks:
             for d in range(4 if relayed else 1):
                 to_sibling(a, d).wait_send()
@@ -1417,7 +1427,7 @@
             full_query,
             full_gate,
             full_down_memory,
-            mixed_t,
+            _,
         ),
         kept,
         table,
@@ -1447,17 +1457,13 @@
         spots,
         1,
     )
-    mixed = kept.mixed
-    partial_mixed = mt(mixed, mixed_t).astype(BF16).reshape(ranks, local, model)
-
-    def block_of(blocks, d):
-        return lax.dynamic_index_in_dim(blocks, lax.rem(rank + d, ranks), 0, keepdims=False)
 
     def turn(d):
         return [(p, (p + d) % ranks) for p in range(ranks)]
 
-    mixed_parts = [block_of(partial_mixed, 0)] + [
-        lax.ppermute(block_of(partial_mixed, d), TP, turn(d)) for d in range(1, ranks)
+    mixed_parts = [kept.block_0] + [
+        lax.ppermute(block, TP, turn(d))
+        for d, block in ((1, kept.block_1), (2, kept.block_2), (3, kept.block_3))
     ]
     picked = pick_grads(
         kept.first, kept.second, kept.grad_recalled, kept.scale, table.reshape(-1, width)
@@ -1472,7 +1478,7 @@
         gate=full_gate,
         ups=ups,
         grad_gate=kept.grad_gate,
-        mixed=mixed,
+        mixed=kept.mixed,
         owner=owner,
         owner_own=owner_own,
         middle=kept.middle,

time: 364 us -> 361 us (level)
  no operation moved by 1% of the time
where the time goes in v4:
time: 361 us; the launch traced here: 360 us
  Pallas kernels  355 us (98%)
  starting transfers between devices  3.62 us (1%)
    pallas_call x1, Pallas kernels, forward(): pl.pallas_call(body, out_shape=[jax.ShapeDtypeStruct(shape, dtype) for sh...  203 us
    pallas_call x1, Pallas kernels, backward(): pl.pallas_call(body, out_shape=[jax.ShapeDtypeStruct(shape, dtype) for sh...  93.3 us
    pallas_call x1, Pallas kernels, pick_grads(): pl.pallas_call(body, grid=(blocks,), out_shape=jax.ShapeDtypeStruct((pick...  53.6 us
  transfers between devices with their start and end apart: 3, of which 0 were waited for; matrix products, arithmetic and copies ran while one was open for 0% of the time, Pallas kernels for 15%

profile of v4, /device:TPU:9, one launch (start us, length us, event | category | flops | bytes accessed | tf_op | source)
XLA Modules:
  0.0 360.1 jit_solution(180932600908695177)
XLA Ops:
  0.6 2.4 shard_map.302
  3.1 203.0 %shard_map.303 = (bf16[8,128,768]{2,1,0:T(8,128)(2,1)}, bf16[8,128,384]{2,1,0:T(8,128)(2,1)}, bf16[8,16,3840]{2,1,0:T(8,128)(2,1)}, bf16[8,128,1024]{2,1,0:T(8,1...) custom-call(bf16[128,768]{1,0:T(8,128)(2,1)} %get-tuple-element.71.r, ...), custom_call_target="tpu_custom_call" | custom-call | tf_op jit(solution)/shard_map/pallas_call | solution.py:1176
  206.1 1.1 collective-permute-start
  207.2 2.3 collective-permute-start.1
  209.6 0.1 collective-permute-start.2
  209.7 53.6 %shard_map.304 = bf16[128,512]{1,0:T(8,128)(2,1)} custom-call(s32[512,128]{1,0:T(8,128)} %get-tuple-element.80.refs_0_, s32[512,128]{1,0:T(8,128)} %get-tuple-element.81.refs_1_, bf16[512,256]{1,0:T(8,128)(2,1)} %get-tuple-element.82.refs_2_, f32[512,1]{1,0:T(8,128)} %get-tuple-element.83.refs_3_, bf16[65536,256]{1,0:T(8,128)(2,1)} %bitcast.21), custom_call_target="tpu_custom_call" | custom-call | tf_op jit(solution)/shard_map/pallas_call | solution.py:1247
  263.3 0.0 collective-permute-done.refs_33_
  263.3 0.0 copy-start
  263.3 0.0 collective-permute-done.1.refs_34_
  263.3 0.0 copy-start.1
  263.3 0.0 collective-permute-done.2.refs_35_
  263.3 0.0 copy-start.2
  263.4 0.7 copy-done
  264.0 0.1 copy-done.1
  264.1 0.1 copy-done.2
  264.2 93.3 %shard_map.305 = (bf16[128,1024]{1,0:T(8,128)(2,1)}, f32[128,1024]{1,0:T(8,128)}, bf16[8,16,2560]{2,1,0:T(8,128)(2,1)}, bf16[8,64,128]{2,1,0:T(8,128)(2,1)}, bf16[8,96,128]{2,1,0:T(8,128)(2,1)}) custom-call(bf16[4,32,512]{2,1,0:T(8,128)(2,1)} %bitcast.29, f32[32,512]{1,0:T(8,128)} %get-tuple-element.90.refs_1_, bf16[2,256,256]{2,1,0:T(8,128)(2,1)} %bitcast.25, ...), custom_call_target="tpu_custom_call" | custom-call | tf_op jit(solution)/shard_map/pallas_call | solution.py:501
  357.5 2.4 shard_map.306
Async XLA Ops:
  206.1 57.2 %collective-permute-start = (bf16[128,1024]{1,0:T(8,128)(2,1)}, bf16[128,1024]{1,0:T(8,128)(2,1)S(1)}, u32[]{:S(2)}, u32[]{:S(2)}) collective-permute-start(bf16[128,1024]{1,0:T(8,128)(2,1)} %get-tuple-element.86), channel_id=1, source_target_pairs={{0,1},{1,2},{2,3},{3,0},{4,5},{5,6},{6,7},{7,4},{8,9},{9,10},{10,1... | collective-permute-start | bytes 786440 | tf_op jit(solution)/shard_map/ppermute | solution.py:1465
  207.2 56.1 %collective-permute-start.1 = (bf16[128,1024]{1,0:T(8,128)(2,1)}, bf16[128,1024]{1,0:T(8,128)(2,1)S(1)}, u32[]{:S(2)}, u32[]{:S(2)}) collective-permute-start(bf16[128,1024]{1,0:T(8,128)(2,1)} %get-tuple-element.87), channel_id=1, source_target_pairs={{0,2},{1,3},{2,0},{3,1},{4,6},{5,7},{6,4},{7,5},{8,10},{9,11},{10,... | collective-permute-start | bytes 786440 | tf_op jit(solution)/shard_map/ppermute | solution.py:1465
  209.6 53.8 %collective-permute-start.2 = (bf16[128,1024]{1,0:T(8,128)(2,1)}, bf16[128,1024]{1,0:T(8,128)(2,1)S(1)}, u32[]{:S(2)}, u32[]{:S(2)}) collective-permute-start(bf16[128,1024]{1,0:T(8,128)(2,1)} %get-tuple-element.88), channel_id=1, source_target_pairs={{0,3},{1,0},{2,1},{3,2},{4,7},{5,4},{6,5},{7,6},{8,11},{9,8},{10,9... | collective-permute-start | bytes 786440 | tf_op jit(solution)/shard_map/ppermute | solution.py:1465
  263.3 0.7 copy-start
  263.3 0.8 copy-start.1
  263.3 0.9 copy-start.2

commit v5 on v4

--- a/solution.py
+++ b/solution.py
@@ -553,7 +553,7 @@
         shown.mixed_t,
     ]
     early, nested, late = (0, 1, 2), (3, 4), (5, 6, 7, 8)
-    cuts = 2
+    cuts = 4
     chunks = tuple(range(len(tree), len(tree) + cuts))
     tree_shapes = [
         (x.shape[0], x.shape[1] * (ranks if a in nested else 1)) for a, x in enumerate(tree)
@@ -1049,7 +1049,7 @@
 
             spread_out(t, s).start()
 
-            @pl.when(t == steps - 7)
+            @pl.when(t == steps - 5)
             def _():
                 other(chunks)
 
@@ -1209,19 +1209,12 @@
     rows = per_block * NKEYS
     blocks = table.shape[0] // rows
 
-    def body(*refs):
-        table_ref, out_ref, kept, sems = refs[4], refs[5], refs[6], refs[11]
-        first_ref, second_ref, grads_ref, scale_ref = refs[7:11]
+    def body(first_ref, second_ref, grads_ref, scale_ref, table_ref, out_ref, kept):
         step = pl.program_id(0)
 
         @pl.when(step == 0)
         def _():
-            copies = [pltpu.make_async_copy(refs[i], refs[7 + i], sems.at[i]) for i in range(4)]
-            for c in copies:
-                c.start()
             kept[...] = jnp.zeros_like(kept)
-            for c in copies:
-                c.wait()
 
         own = first_ref[...]
         low = second_ref[...] & 127
@@ -1248,11 +1241,10 @@
         body,
         grid=(blocks,),
         out_shape=jax.ShapeDtypeStruct((picks, tokens), BF16),
-        in_specs=[ANY] * 4 + [pl.BlockSpec((rows, width), lambda s: (s, 0))],
+        in_specs=[whole(x.shape) for x in (first, second, grads, scale)]
+        + [pl.BlockSpec((rows, width), lambda s: (s, 0))],
         out_specs=whole((picks, tokens)),
-        scratch_shapes=[pltpu.VMEM((tokens, picks), I32)]
-        + [pltpu.VMEM(x.shape, x.dtype) for x in (first, second, grads, scale)]
-        + [pltpu.SemaphoreType.DMA((4,))],
+        scratch_shapes=[pltpu.VMEM((tokens, picks), I32)],
         compiler_params=pltpu.CompilerParams(vmem_limit_bytes=61 << 20),
     )(first, second, grads, scale, table)
 

time: 361 us -> 359 us (level)
  no operation moved by 1% of the time
where the time goes in v5:
time: 359 us; the launch traced here: 357 us
  Pallas kernels  352 us (98%)
  starting transfers between devices  3.62 us (1%)
    pallas_call x1, Pallas kernels, forward(): pl.pallas_call(body, out_shape=[jax.ShapeDtypeStruct(shape, dtype) for sh...  202 us
    pallas_call x1, Pallas kernels, backward(): pl.pallas_call(body, out_shape=[jax.ShapeDtypeStruct(shape, dtype) for sh...  92.7 us
    pallas_call x1, Pallas kernels, pick_grads(): pl.pallas_call(body, grid=(blocks,), out_shape=jax.ShapeDtypeStruct((pick...  52.6 us
  transfers between devices with their start and end apart: 3, of which 0 were waited for; matrix products, arithmetic and copies ran while one was open for 0% of the time, Pallas kernels for 15%

profile of v5, /device:TPU:9, one launch (start us, length us, event | category | flops | bytes accessed | tf_op | source)
XLA Modules:
  0.0 357.3 jit_solution(1945815833725239421)
XLA Ops:
  0.6 2.4 shard_map.302
  3.1 201.8 %shard_map.303 = (bf16[8,128,768]{2,1,0:T(8,128)(2,1)}, bf16[8,128,384]{2,1,0:T(8,128)(2,1)}, bf16[8,16,3840]{2,1,0:T(8,128)(2,1)}, bf16[8,128,1024]{2,1,0:T(8,1...) custom-call(bf16[128,768]{1,0:T(8,128)(2,1)} %get-tuple-element.71.r, ...), custom_call_target="tpu_custom_call" | custom-call | tf_op jit(solution)/shard_map/pallas_call | solution.py:1176
  204.9 1.1 collective-permute-start
  206.0 2.4 collective-permute-start.1
  208.4 0.1 collective-permute-start.2
  208.5 52.6 %shard_map.304 = bf16[128,512]{1,0:T(8,128)(2,1)} custom-call(s32[512,128]{1,0:T(8,128)} %get-tuple-element.80.first_ref, s32[512,128]{1,0:T(8,128)} %get-tuple-element.81.second_ref, bf16[512,256]{1,0:T(8,128)(2,1)} %get-tuple-element.82.grads_ref, f32[512,1]{1,0:T(8,128)} %get-tuple-element.83.scale_ref, bf16[65536,256]{1,0:T(8,128)(2,1)} %bitcast.21), custom_call_target="tpu_custom_call" | custom-call | tf_op jit(solution)/shard_map/pallas_call | solution.py:1240
  261.1 0.0 collective-permute-done.refs_33_
  261.1 0.0 copy-start
  261.1 0.0 collective-permute-done.1.refs_34_
  261.1 0.0 copy-start.1
  261.1 0.0 collective-permute-done.2.refs_35_
  261.1 0.0 copy-start.2
  261.1 0.7 copy-done
  261.8 0.1 copy-done.1
  261.9 0.1 copy-done.2
  262.0 92.7 %shard_map.305 = (bf16[128,1024]{1,0:T(8,128)(2,1)}, f32[128,1024]{1,0:T(8,128)}, bf16[8,16,2560]{2,1,0:T(8,128)(2,1)}, bf16[8,64,128]{2,1,0:T(8,128)(2,1)}, bf16[8,96,128]{2,1,0:T(8,128)(2,1)}) custom-call(bf16[4,32,512]{2,1,0:T(8,128)(2,1)} %bitcast.29, f32[32,512]{1,0:T(8,128)} %get-tuple-element.90.refs_1_, bf16[2,256,256]{2,1,0:T(8,128)(2,1)} %bitcast.25, ...), custom_call_target="tpu_custom_call" | custom-call | tf_op jit(solution)/shard_map/pallas_call | solution.py:501
  354.7 2.4 shard_map.306
Async XLA Ops:
  204.9 56.2 %collective-permute-start = (bf16[128,1024]{1,0:T(8,128)(2,1)}, bf16[128,1024]{1,0:T(8,128)(2,1)S(1)}, u32[]{:S(2)}, u32[]{:S(2)}) collective-permute-start(bf16[128,1024]{1,0:T(8,128)(2,1)} %get-tuple-element.86), channel_id=1, source_target_pairs={{0,1},{1,2},{2,3},{3,0},{4,5},{5,6},{6,7},{7,4},{8,9},{9,10},{10,1... | collective-permute-start | bytes 786440 | tf_op jit(solution)/shard_map/ppermute | solution.py:1457
  206.0 55.1 %collective-permute-start.1 = (bf16[128,1024]{1,0:T(8,128)(2,1)}, bf16[128,1024]{1,0:T(8,128)(2,1)S(1)}, u32[]{:S(2)}, u32[]{:S(2)}) collective-permute-start(bf16[128,1024]{1,0:T(8,128)(2,1)} %get-tuple-element.87), channel_id=1, source_target_pairs={{0,2},{1,3},{2,0},{3,1},{4,6},{5,7},{6,4},{7,5},{8,10},{9,11},{10,... | collective-permute-start | bytes 786440 | tf_op jit(solution)/shard_map/ppermute | solution.py:1457
  208.4 52.7 %collective-permute-start.2 = (bf16[128,1024]{1,0:T(8,128)(2,1)}, bf16[128,1024]{1,0:T(8,128)(2,1)S(1)}, u32[]{:S(2)}, u32[]{:S(2)}) collective-permute-start(bf16[128,1024]{1,0:T(8,128)(2,1)} %get-tuple-element.88), channel_id=1, source_target_pairs={{0,3},{1,0},{2,1},{3,2},{4,7},{5,4},{6,5},{7,6},{8,11},{9,8},{10,9... | collective-permute-start | bytes 786440 | tf_op jit(solution)/shard_map/ppermute | solution.py:1457
  261.1 0.7 copy-start
  261.1 0.8 copy-start.1
  261.1 0.9 copy-start.2
